TPU v7x, 256 devices: a whole 4x4x8 slice. The times are simulated.
256 devices in a mesh: dp: 32 (over y, x, core), mp: 8 (over z).
Axes of the slice: x: 4, y: 4, z: 8, core: 2. Of those that a mesh axis runs over, the one named last changes fastest.
Arguments:
- activations: bfloat16 [4096, 2560], P('dp'), may hold values from -6 to 6
- grad_hidden: bfloat16 [4096, 8192], P('dp', 'mp'), may hold values from -0.059814453 to 0.059814453
- up_weight: bfloat16 [2560, 8192], P('dp', 'mp'), may hold values from -6 to 6
- error_feedback: bfloat16 [32, 2560, 8192], P('dp', None, 'mp'), may hold values from -0.75 to 0.75
- query_previous: float32 [8192, 128], P('mp'), may hold values from -6 to 6
Outputs:
- grad_input: bfloat16 [4096, 2560], P('dp', 'mp')
- error_next: bfloat16 [32, 2560, 8192], P('dp', None, 'mp')
- update: float32 [2560, 8192], P('dp', 'mp')
- query_next: float32 [8192, 128], P('mp')
All inputs are finite; a program needn't handle non-finite values.
Results may differ from a plain program's by a relative error of at most 0.0005.
Values may be sent and summed in bfloat16 or wider, within the bound.
No kernel may reach another device: no remote copies, remote signals or barrier semaphores. Data moves between devices by JAX's collectives and lax.ppermute only.
A program may use at most 128 MiB of HBM per device.

v0:
```python
import jax
import jax.numpy as jnp
from jax import lax
from jax.sharding import PartitionSpec as P

HIGHEST = lax.Precision.HIGHEST


def orthonormal(project, gram_matrix):
    factor = jnp.linalg.cholesky(gram_matrix)
    return lax.linalg.triangular_solve(
        factor, project, left_side=False, lower=True, transpose_a=True
    )


def local(activations, grad_hidden, up_weight, error_feedback, query_previous):
    replicas = lax.axis_size("dp")
    partial_input = lax.dot_general(
        grad_hidden,
        lax.all_gather(up_weight, "dp", axis=0, tiled=True),
        (((1,), (1,)), ((), ())),
        preferred_element_type=jnp.float32,
    )
    grad_input = lax.psum_scatter(partial_input, "mp", scatter_dimension=1, tiled=True).astype(
        jnp.bfloat16
    )
    local_grad = lax.dot_general(
        activations, grad_hidden, (((0,), (0,)), ((), ())), preferred_element_type=jnp.float32
    )
    merged = error_feedback[0].astype(jnp.float32) + local_grad
    project = jnp.dot(merged, query_previous, precision=HIGHEST, preferred_element_type=jnp.float32)
    project = lax.psum(project, ("dp", "mp"))
    gram_matrix = jnp.dot(project.T, project, precision=HIGHEST, preferred_element_type=jnp.float32)
    basis_full = orthonormal(project, gram_matrix)
    query_term = lax.dot_general(
        merged,
        basis_full,
        (((0,), (0,)), ((), ())),
        precision=HIGHEST,
        preferred_element_type=jnp.float32,
    )
    query_next = lax.psum(query_term, "dp") / replicas
    low_rank = lax.dot_general(
        basis_full,
        query_next,
        (((1,), (1,)), ((), ())),
        precision=HIGHEST,
        preferred_element_type=jnp.float32,
    )
    error_next = (merged - low_rank).astype(jnp.bfloat16)[None]
    row_share = merged.shape[0] // replicas
    update = lax.dynamic_slice_in_dim(low_rank, lax.axis_index("dp") * row_share, row_share, 0)
    return (grad_input, error_next, update, query_next)


def solution(mesh):
    in_specs = (P("dp", None), P("dp", "mp"), P("dp", "mp"), P("dp", None, "mp"), P("mp", None))
    out_specs = (P("dp", "mp"), P("dp", None, "mp"), P("dp", "mp"), P("mp", None))
    return jax.shard_map(local, mesh=mesh, in_specs=in_specs, out_specs=out_specs, check_vma=False)
```

profile of v0, /device:TPU:32, one launch (start us, length us, event | category | flops | bytes accessed | tf_op | source)
XLA Modules:
  0.0 500.3 jit_solution(10728935111397148013)
XLA Ops:
  8.0 0.0 copy-start
  8.0 0.0 all-reduce.3.cloned.1.call-start
  8.1 1.0 copy-done
  9.1 4.2 convert_add_fusion
  13.3 4.0 copy-done.1
  17.2 9.4 %fusion.6 = f32[2560,128]{1,0:T(8,128)} fusion(f32[2560,1024]{1,0:T(8,128)S(1)} %convert_add_fusion, f32[1024,128]{1,0:T(8,128)S(1)} %copy-done.5), kind=kOutput, calls=%fused_computation.16 | convolution fusion | flops 4026531840 | bytes 12320768 | tf_op jit(solution)/shard_map/dot_general | solution.py:31
  26.7 0.0 all-reduce.3.cloned.1.call-update
  26.7 0.0 all-gather.2.cloned.1.call-start
  26.7 0.5 all-gather.2.cloned.1.call-update
  27.3 0.2 all-reduce.5.cloned.1.call-start
  27.5 258.9 %all-reduce.3.cloned.1.call-done = f32[2560,128]{1,0:T(8,128)} async-done(((f32[2560,128]{1,0:T(8,128)}), f32[2560,128]{1,0:T(8,128)}) %all-reduce.3.cloned.1.call-update) | async-done | bytes 1310736 | tf_op jit(solution)/shard_map/psum | solution.py:32
  286.4 3.9 fusion.7
  290.3 0.1 copy.9
  290.4 11.7 %cholesky.16 = f32[128,128]{1,0:T(8,128)S(1)} custom-call(f32[128,128]{1,0:T(8,128)S(1)} %fusion.4), custom_call_target="Cholesky" | custom-call | tf_op jit(solution)/shard_map/jit(cholesky)/cholesky | solution.py:10
  302.2 0.6 compare_reduce_fusion
  302.8 0.7 fusion.1
  303.5 9.8 %custom-call.6 = f32[1,128,128]{1,2,0:T(8,128)S(1)} custom-call(f32[1,128,128]{2,1,0:T(8,128)S(1)} %fusion.1), custom_call_target="InvertDiagBlocksLowerTriangular" | custom-call | tf_op jit(solution)/shard_map/triangular_solve | solution.py:11
  313.3 2.5 fusion.2
  315.8 20.0 %fusion.8 = f32[1024,128]{1,0:T(8,128)} fusion(f32[2560,1024]{1,0:T(8,128)} %copy-done.1, f32[2560,128]{1,0:T(8,128)S(1)} %fusion.2), kind=kOutput, calls=%fused_computation.18 | convolution fusion | flops 4026531840 | bytes 12320768 | tf_op jit(solution)/shard_map/dot_general | solution.py:35
  335.8 0.0 all-reduce.5.cloned.1.call-update
  335.8 0.3 reduce-scatter.2.cloned.1.call-start
  336.1 0.0 all-gather.2.cloned.1.call-done
  336.1 5.1 %fusion.5 = f32[128,2560]{0,1:T(8,128)} fusion(bf16[128,1024]{1,0:T(8,128)(2,1)S(1)} %copy-done.4, bf16[2560,1024]{1,0:T(8,128)(2,1)} %all-gather.2.cloned.1.call-done), kind=kOutput, calls=%fused_computation.15 | convolution fusion | flops 671088640 | bytes 6815744 | tf_op jit(solution)/shard_map/dot_general | solution.py:18
  341.2 0.0 reduce-scatter.2.cloned.1.call-update
  341.2 108.8 %all-reduce.5.cloned.1.call-done = f32[1024,128]{1,0:T(8,128)} async-done(((f32[1024,128]{1,0:T(8,128)}), f32[1024,128]{1,0:T(8,128)}) %all-reduce.5.cloned.1.call-update) | async-done | bytes 524304 | tf_op jit(solution)/shard_map/psum | solution.py:42
  450.0 1.1 broadcast_multiply_fusion
  451.1 8.4 %fusion.9 = f32[2560,1024]{1,0:T(8,128)S(1)} fusion(f32[2560,128]{1,0:T(8,128)S(1)} %fusion.2, f32[1024,128]{1,0:T(8,128)S(1)} %broadcast_multiply_fusion), kind=kOutput, calls=%fused_computation.19 | convolution fusion | flops 4026531840 | bytes 12320768 | tf_op jit(solution)/shard_map/dot_general | solution.py:43
  459.5 3.8 copy-done.2
  463.4 0.7 constant_dynamic-slice_fusion
  464.1 11.5 %fusion = bf16[1,2560,1024]{2,1,0:T(8,128)(2,1)} fusion(f32[2560,1024]{1,0:T(8,128)} %copy-done.1, f32[2560,1024]{1,0:T(8,128)} %copy-done.2), kind=kLoop, calls=%fused_computation.2 | loop fusion | flops 5242880 | bytes 26214400 | tf_op jit(solution)/shard_map/broadcast_in_dim | solution.py:50
  475.7 15.1 %reduce-scatter.2.cloned.1.call-done = f32[128,320]{0,1:T(8,128)} async-done(((f32[128,2560]{0,1:T(8,128)}), f32[128,320]{0,1:T(8,128)}) %reduce-scatter.2.cloned.1.call-update) | async-done | bytes 163856 | tf_op jit(solution)/shard_map/reduce_scatter | solution.py:24
  490.8 1.6 convert_element_type.12
  (10 shorter events, 0.1 us)
Async XLA Ops:
  8.0 1.1 copy-start
  8.0 278.3 %all-reduce.3.cloned.1.call-start = ((), (), s32[]{:S(2)}) async-start(), calls=%async_computation.3 | async-start | bytes 2621440 | tf_op jit(solution)/shard_map/psum | solution.py:32
  9.1 8.2 %copy-start.5 = (f32[1024,128]{1,0:T(8,128)S(1)}, f32[1024,128]{1,0:T(8,128)}, u32[]{:S(2)}) copy-start(f32[1024,128]{1,0:T(8,128)} %param.9) | copy-start | bytes 1572868
  13.3 4.0 copy-start.1
  26.7 309.4 %all-gather.2.cloned.1.call-start = ((), (), s32[]{:S(2)}) async-start(), calls=%async_computation.1 | async-start | bytes 5406720 | tf_op jit(solution)/shard_map/all_gather | solution.py:20
  27.3 422.7 %all-reduce.5.cloned.1.call-start = ((), (), s32[]{:S(2)}) async-start(), calls=%async_computation.4 | async-start | bytes 1048576 | tf_op jit(solution)/shard_map/psum | solution.py:42
  315.8 20.3 %copy-start.4 = (bf16[128,1024]{1,0:T(8,128)(2,1)S(1)}, bf16[128,1024]{1,0:T(8,128)(2,1)}, u32[]{:S(2)}) copy-start(bf16[128,1024]{1,0:T(8,128)(2,1)} %param.6) | copy-start | bytes 786436
  335.8 155.0 %reduce-scatter.2.cloned.1.call-start = ((), (), s32[]{:S(2)}) async-start(), calls=%async_computation.2 | async-start | bytes 1474560 | tf_op jit(solution)/shard_map/reduce_scatter | solution.py:24
  451.1 8.5 %copy-start.3 = (f32[1024,128]{1,0:T(8,128)}, f32[1024,128]{1,0:T(8,128)S(1)}, u32[]{:S(2)}) copy-start(f32[1024,128]{1,0:T(8,128)S(1)} %broadcast_multiply_fusion) | copy-start | bytes 1572868
  459.5 3.8 copy-start.2
Sparse Core Ops, SparseCore 0:
  26.8 259.4 all-reduce.2
Sparse Core Ops, SparseCore 1:
  29.7 55.1 all-gather.1
  335.9 114.1 all-reduce.4
  452.4 38.3 reduce-scatter.1
where the time goes:
time: 509 us; the launch traced here: 500 us
  waiting for transfers between devices  383 us (75%)
  matrix products  53.5 us (11%)
  other arithmetic  37 us (7%)
  between operations  16.2 us (3%)
  local copies, waits for them, and re-layouts  9.68 us (2%)
    psum x1, waiting for transfers between devices, local(): project = lax.psum(project, ('dp', 'mp'))  259 us
    psum x1, waiting for transfers between devices, local(): query_next = lax.psum(query_term, 'dp') / replicas  109 us
    dot_general x1, matrix products, local(): lax.dot_general(merged, basis_full, (((0,), (0,)), ((), ())), precision=H...  20 us
    reduce_scatter x1, waiting for transfers between devices, local(): lax.psum_scatter(partial_input, 'mp', scatter_dimension=1, tiled=True)  15.1 us
    another operation x3, other arithmetic, orthonormal(): factor = jnp.linalg.cholesky(gram_matrix)  12.4 us
    broadcast_in_dim x1, other arithmetic, local(): error_next = (merged - low_rank).astype(jnp.bfloat16)[None]  11.5 us
    another operation x2, other arithmetic, orthonormal(): lax.linalg.triangular_solve(factor, project, left_side=False, lower=True,...  10.5 us
  transfers between devices with their start and end apart: 4, of which 3 were waited for; matrix products, arithmetic and copies ran while one was open for 15% of the time, Pallas kernels for 0%

commit v1 on v0

v1 whole, which is shorter than its diff:
```python
import functools

import jax
import jax.numpy as jnp
from jax import lax
from jax.experimental import pallas as pl
from jax.experimental.pallas import tpu as pltpu
from jax.sharding import PartitionSpec as P

HIGHEST = lax.Precision.HIGHEST
F32 = jnp.float32
BF16 = jnp.bfloat16
BLOCK = 512
VMEM_LIMIT = 48 << 20


def dot(a, b, dims):
    return lax.dot_general(a, b, (dims, ((), ())), preferred_element_type=F32)


def pair(x):
    high = x.astype(BF16)
    rest = (x - high.astype(F32)).astype(BF16)
    return jnp.concatenate([high, rest], axis=1)


def folded(x):
    half = x.shape[1] // 2
    return x[:, :half] + x[:, half:]


def project_kernel(acts, hidden, error, query, out, query_pair, token_pair):
    @pl.when(pl.program_id(0) == 0)
    def _():
        split = pair(query[...])
        query_pair[...] = split
        token_pair[...] = pair(folded(dot(hidden[...], split, ((1,), (0,)))))

    total = dot(error[...], query_pair[...], ((1,), (0,)))
    total += dot(acts[...], token_pair[...], ((0,), (0,)))
    out[...] = folded(total)


def project_part(acts, hidden, error, query):
    tokens, rows = acts.shape
    columns, rank = query.shape
    return pl.pallas_call(
        project_kernel,
        grid=(rows // BLOCK,),
        in_specs=[
            pl.BlockSpec((tokens, BLOCK), lambda i: (0, i)),
            pl.BlockSpec((tokens, columns), lambda i: (0, 0)),
            pl.BlockSpec((BLOCK, columns), lambda i: (i, 0)),
            pl.BlockSpec((columns, rank), lambda i: (0, 0)),
        ],
        out_specs=pl.BlockSpec((BLOCK, rank), lambda i: (i, 0)),
        out_shape=jax.ShapeDtypeStruct((rows, rank), F32),
        scratch_shapes=[pltpu.VMEM((columns, 2 * rank), BF16), pltpu.VMEM((tokens, 2 * rank), BF16)],
        compiler_params=pltpu.CompilerParams(vmem_limit_bytes=VMEM_LIMIT),
        cost_estimate=pl.CostEstimate(
            flops=4 * rows * columns * rank, bytes_accessed=2 * rows * columns, transcendentals=0
        ),
        name="project_part",
    )(acts, hidden, error, query)


def query_kernel(acts, hidden, error, project, out, gram, total, tokens_sum, gram_sum):
    step = pl.program_id(0)

    @pl.when(step == 0)
    def _():
        total[...] = jnp.zeros_like(total)
        tokens_sum[...] = jnp.zeros_like(tokens_sum)
        gram_sum[...] = jnp.zeros_like(gram_sum)

    split = pair(project[...])
    total[...] += dot(error[...], split, ((0,), (0,)))
    tokens_sum[...] += dot(acts[...], split, ((1,), (0,)))
    gram_sum[...] += dot(split, split, ((0,), (0,)))

    @pl.when(step == pl.num_programs(0) - 1)
    def _():
        spread = pair(folded(tokens_sum[...]))
        out[...] = folded(total[...] + dot(hidden[...], spread, ((0,), (0,))))
        half = gram.shape[0]
        gram[...] = folded(gram_sum[:half, :] + gram_sum[half:, :])


def query_part(acts, hidden, error, project):
    tokens, rows = acts.shape
    columns = hidden.shape[1]
    rank = project.shape[1]
    return pl.pallas_call(
        query_kernel,
        grid=(rows // BLOCK,),
        in_specs=[
            pl.BlockSpec((tokens, BLOCK), lambda i: (0, i)),
            pl.BlockSpec((tokens, columns), lambda i: (0, 0)),
            pl.BlockSpec((BLOCK, columns), lambda i: (i, 0)),
            pl.BlockSpec((BLOCK, rank), lambda i: (i, 0)),
        ],
        out_specs=(
            pl.BlockSpec((columns, rank), lambda i: (0, 0)),
            pl.BlockSpec((rank, rank), lambda i: (0, 0)),
        ),
        out_shape=(
            jax.ShapeDtypeStruct((columns, rank), F32),
            jax.ShapeDtypeStruct((rank, rank), F32),
        ),
        scratch_shapes=[
            pltpu.VMEM((columns, 2 * rank), F32),
            pltpu.VMEM((tokens, 2 * rank), F32),
            pltpu.VMEM((2 * rank, 2 * rank), F32),
        ],
        compiler_params=pltpu.CompilerParams(vmem_limit_bytes=VMEM_LIMIT),
        cost_estimate=pl.CostEstimate(
            flops=4 * rows * columns * rank, bytes_accessed=2 * rows * columns, transcendentals=0
        ),
        name="query_part",
    )(acts, hidden, error, project)


def residual_kernel(acts, hidden, error, basis, basis_share, query, out, update, first, second):
    rank = query.shape[1]

    @pl.when(pl.program_id(0) == 0)
    def _():
        turned = query[...].T
        high = turned.astype(BF16)
        rest = (turned - high.astype(F32)).astype(BF16)
        first[:rank, :] = high
        first[rank:, :] = high
        second[:rank, :] = rest
        second[rank:, :] = -hidden[...]
        share = pair(basis_share[...])
        update[...] = dot(share, first[...], ((1,), (0,))) + dot(share[:, :rank], rest, ((1,), (0,)))

    split = pair(basis[...])
    mixed = jnp.concatenate([split[:, :rank], acts[...].T], axis=1)
    change = dot(split, first[...], ((1,), (0,))) + dot(mixed, second[...], ((1,), (0,)))
    out[...] = (error[...].astype(F32) - change).astype(BF16)


def residual(acts, hidden, error, basis, basis_share, query):
    tokens, rows = acts.shape
    columns, rank = query.shape
    share = basis_share.shape[0]
    return pl.pallas_call(
        residual_kernel,
        grid=(rows // BLOCK,),
        in_specs=[
            pl.BlockSpec((tokens, BLOCK), lambda i: (0, i)),
            pl.BlockSpec((tokens, columns), lambda i: (0, 0)),
            pl.BlockSpec((BLOCK, columns), lambda i: (i, 0)),
            pl.BlockSpec((BLOCK, rank), lambda i: (i, 0)),
            pl.BlockSpec((share, rank), lambda i: (0, 0)),
            pl.BlockSpec((columns, rank), lambda i: (0, 0)),
        ],
        out_specs=(
            pl.BlockSpec((BLOCK, columns), lambda i: (i, 0)),
            pl.BlockSpec((share, columns), lambda i: (0, 0)),
        ),
        out_shape=(
            jax.ShapeDtypeStruct((rows, columns), BF16),
            jax.ShapeDtypeStruct((share, columns), F32),
        ),
        scratch_shapes=[
            pltpu.VMEM((2 * rank, columns), BF16),
            pltpu.VMEM((rank + tokens, columns), BF16),
        ],
        compiler_params=pltpu.CompilerParams(vmem_limit_bytes=VMEM_LIMIT),
        cost_estimate=pl.CostEstimate(
            flops=8 * rows * columns * rank, bytes_accessed=4 * rows * columns, transcendentals=0
        ),
        name="residual",
    )(acts, hidden, error, basis, basis_share, query)


CORES = 2


def chips_of(replicas):
    return [list(range(core, replicas, CORES)) for core in range(CORES)]


def swapped(x, replicas):
    return lax.ppermute(x, "dp", [(i, i ^ 1) for i in range(replicas)])


def scatter_sum(x, replicas):
    core = lax.axis_index("dp") % CORES
    half = x.shape[0] // CORES
    theirs = swapped(lax.dynamic_slice_in_dim(x, (1 - core) * half, half, 0), replicas)
    x = lax.dynamic_slice_in_dim(x, core * half, half, 0) + theirs
    chips = replicas // CORES
    pieces = lax.all_to_all(
        x.reshape(chips, half // chips, -1), "dp", 0, 0, axis_index_groups=chips_of(replicas)
    )
    return jnp.sum(pieces, axis=0)


def gather_rows(x, replicas):
    chips = replicas // CORES
    spread = jnp.broadcast_to(x[None], (chips, *x.shape))
    mine = lax.all_to_all(spread, "dp", 0, 0, axis_index_groups=chips_of(replicas))
    mine = mine.reshape(chips * x.shape[0], -1)
    theirs = swapped(mine, replicas)
    core = lax.axis_index("dp") % CORES
    return jnp.where(
        core == 0, jnp.concatenate([mine, theirs], 0), jnp.concatenate([theirs, mine], 0)
    )


def sum_over_mp(x):
    ranks = lax.axis_size("mp")
    spread = jnp.broadcast_to(x[None], (ranks, *x.shape))
    return jnp.sum(lax.all_to_all(spread, "mp", 0, 0), axis=0)


def inverse_factor(gram_matrix):
    factor = jnp.linalg.cholesky(gram_matrix)
    identity = jnp.eye(gram_matrix.shape[0], dtype=F32)
    return lax.linalg.triangular_solve(factor, identity, left_side=False, lower=True, transpose_a=True)


def local(activations, grad_hidden, up_weight, error_feedback, query_previous):
    replicas = lax.axis_size("dp")
    error = error_feedback[0]
    partial_input = lax.dot_general(
        grad_hidden,
        lax.all_gather(up_weight, "dp", axis=0, tiled=True),
        (((1,), (1,)), ((), ())),
        preferred_element_type=F32,
    )
    grad_input = lax.psum_scatter(partial_input, "mp", scatter_dimension=1, tiled=True).astype(BF16)

    part = project_part(activations, grad_hidden, error, query_previous)
    project = gather_rows(sum_over_mp(scatter_sum(part, replicas)), replicas)
    part, gram_matrix = query_part(activations, grad_hidden, error, project)
    inverse = inverse_factor(gram_matrix)
    total = gather_rows(scatter_sum(part, replicas), replicas)
    basis = jnp.dot(project, inverse, precision=HIGHEST, preferred_element_type=F32)
    query_next = jnp.dot(total, inverse, precision=HIGHEST, preferred_element_type=F32) / replicas
    share = basis.shape[0] // replicas
    basis_share = lax.dynamic_slice_in_dim(basis, lax.axis_index("dp") * share, share, 0)
    error_next, update = residual(
        activations, grad_hidden, error, basis, basis_share, query_next
    )
    return (grad_input, error_next[None], update, query_next)


def solution(mesh):
    in_specs = (P("dp", None), P("dp", "mp"), P("dp", "mp"), P("dp", None, "mp"), P("mp", None))
    out_specs = (P("dp", "mp"), P("dp", None, "mp"), P("dp", "mp"), P("mp", None))
    return jax.shard_map(local, mesh=mesh, in_specs=in_specs, out_specs=out_specs, check_vma=False)
```

time: 509 us -> 147 us (0.29); the launches traced: 500 us -> 144 us
  waiting for transfers between devices: 383 us -> 4.17 us
  blocking collectives: 0 us -> 56.6 us
  matrix products: 53.5 us -> 7.04 us
  Pallas kernels: 0 us -> 19.8 us
  other arithmetic: 37 us -> 25.4 us
  starting transfers between devices: 0.59 us -> 11.6 us
    psum x2 -> x0, waiting for transfers between devices: 368 us -> none  [the longest x1 259 us: local(): project = lax.psum(project, ('dp', 'mp'))]
    all_to_all x0 -> x3, blocking collectives: none -> 56.6 us  [the longest x1 22.1 us: scatter_sum(): lax.all_to_all(x.reshape(chips, half // chips, -1), 'dp', 0, 0, axis_inde...]
    dot_general x5 -> x2, matrix products: 45.9 us -> 1.74 us  [the longest x1 1.17 us: local(): jnp.dot(project, inverse, precision=HIGHEST, preferred_element_type=F32)]
    pallas_call x0 -> x3, Pallas kernels: none -> 19.8 us  [the longest x1 8.31 us: residual(): pl.pallas_call(residual_kernel, grid=(rows // BLOCK,), in_specs=[pl.Block...]
    reduce_scatter x1, waiting for transfers between devices: 15.1 us -> 0.01 us  [local(): lax.psum_scatter(partial_input, 'mp', scatter_dimension=1, tiled=True)]
    broadcast_in_dim x1 -> x0, other arithmetic: 11.5 us -> none  [local(): error_next = (merged - low_rank).astype(jnp.bfloat16)[None]]
    all_to_all x0 -> x2, starting transfers between devices: none -> 10.7 us  [the longest x1 7.17 us: gather_rows(): lax.all_to_all(spread, 'dp', 0, 0, axis_index_groups=chips_of(replicas))]
  transfers between devices with their start and end apart: 4 -> 8, of which waited for: 3 -> 3; matrix products, arithmetic and copies ran while one was open for 15% -> 22% of each run, Pallas kernels for 0% -> 14%
where the time goes in v1:
time: 147 us; the launch traced here: 144 us
  blocking collectives  56.6 us (39%)
  other arithmetic  25.4 us (17%)
  Pallas kernels  19.8 us (13%)
  between operations  14.3 us (10%)
  starting transfers between devices  11.6 us (8%)
  matrix products  7.04 us (5%)
  local copies, waits for them, and re-layouts  4.98 us (3%)
  waiting for transfers between devices  4.17 us (3%)
    all_to_all x1, blocking collectives, scatter_sum(): lax.all_to_all(x.reshape(chips, half // chips, -1), 'dp', 0, 0, axis_inde...  22.1 us
    all_to_all x1, blocking collectives, sum_over_mp(): return jnp.sum(lax.all_to_all(spread, 'mp', 0, 0), axis=0)  18.9 us
    all_to_all x1, blocking collectives, gather_rows(): lax.all_to_all(spread, 'dp', 0, 0, axis_index_groups=chips_of(replicas))  15.6 us
    another operation x3, other arithmetic, inverse_factor(): factor = jnp.linalg.cholesky(gram_matrix)  12.4 us
    another operation x2, other arithmetic, inverse_factor(): lax.linalg.triangular_solve(factor, identity, left_side=False, lower=True...  10.5 us
    pallas_call x1, Pallas kernels, residual(): pl.pallas_call(residual_kernel, grid=(rows // BLOCK,), in_specs=[pl.Block...  8.31 us
    all_to_all x1, starting transfers between devices, gather_rows(): lax.all_to_all(spread, 'dp', 0, 0, axis_index_groups=chips_of(replicas))  7.17 us
    pallas_call x1, Pallas kernels, query_part(): pl.pallas_call(query_kernel, grid=(rows // BLOCK,), in_specs=[pl.BlockSpe...  5.93 us
  transfers between devices with their start and end apart: 8, of which 3 were waited for; matrix products, arithmetic and copies ran while one was open for 22% of the time, Pallas kernels for 14%

profile of v1, /device:TPU:32, one launch (start us, length us, event | category | flops | bytes accessed | tf_op | source)
XLA Modules:
  0.0 143.9 jit_solution(1802495419997515973)
XLA Ops:
  7.2 0.7 all-gather.2.cloned.1.call-update
  8.0 0.9 copy-done
  8.9 1.1 copy-done.2
  10.0 1.0 copy-done.4
  11.0 5.6 %project_part.1 = f32[2560,128]{1,0:T(8,128)S(1)} custom-call(bf16[128,2560]{1,0:T(8,128)(2,1)S(1)} %copy-done.2, bf16[128,1024]{1,0:T(8,128)(2,1)S(1)} %copy-done, bf16[2560,1024]{1,0:T(8,128)(2,1)} %bitcast.20, f32[1024,128]{1,0:T(8,128)S(1)} %copy-done.4), custom_call_target="tpu_custom_call" | custom-call | flops 1342177280 | bytes 5242880 | tf_op jit(solution)/shard_map/project_part/pallas_call | solution.py:47
  16.7 0.1 collective-permute-start
  16.8 2.1 %collective-permute-done = f32[1280,128]{1,0:T(8,128)S(1)} collective-permute-done((f32[1280,128]{1,0:T(8,128)S(1)}, f32[1280,128]{1,0:T(8,128)S(1)}, u32[]{:S(2)}, u32[]{:S(2)}) %collective-permute-start) | collective-permute-done | bytes 655392 | tf_op jit(solution)/shard_map/ppermute | solution.py:187
  19.0 22.1 %all_to_all.25 = f32[16,80,128]{2,1,0:T(8,128)S(1)} all-to-all(f32[16,80,128]{2,1,0:T(8,128)S(1)} %bitcast.23), channel_id=1, replica_groups={{0,16,32,48,64,80,96,112,128,144,160,176,192,208,224,240},{8,24,40,56,7..., dimensions={0} | all-to-all | bytes 1310720 | tf_op jit(solution)/shard_map/all_to_all | solution.py:196
  41.1 18.9 %all_to_all.26 = f32[8,80,128]{2,1,0:T(8,128)S(1)} all-to-all(f32[8,80,128]{2,1,0:T(8,128)S(1)} %broadcast_in_dim.10), channel_id=1, replica_groups=mesh['dp'=32,'mp'=8] {'mp'}, dimensions={0} | all-to-all | bytes 655360 | tf_op jit(solution)/shard_map/all_to_all | solution.py:217
  60.1 15.6 %all_to_all.27 = f32[16,80,128]{2,1,0:T(8,128)S(1)} all-to-all(f32[16,80,128]{2,1,0:T(8,128)S(1)} %broadcast_in_dim.11), channel_id=1, replica_groups={{0,16,32,48,64,80,96,112,128,144,160,176,192,208,224,240},{8,24,40,56,7..., dimensions={0} | all-to-all | bytes 1310720 | tf_op jit(solution)/shard_map/all_to_all | solution.py:205
  75.8 5.1 %fusion.11 = f32[128,2560]{0,1:T(8,128)} fusion(bf16[128,1024]{1,0:T(8,128)(2,1)S(1)} %copy-done.1, bf16[2560,1024]{1,0:T(8,128)(2,1)} %all-gather.2.cloned.1.call-done), kind=kOutput, calls=%fused_computation.25 | convolution fusion | flops 671088640 | bytes 6815744 | tf_op jit(solution)/shard_map/dot_general | solution.py:229
  80.9 0.1 maximum_select_fusion.project
  81.1 0.9 copy-done.3
  82.0 5.9 %query_part.1 = (f32[1024,128]{1,0:T(8,128)S(1)}, f32[128,128]{1,0:T(8,128)S(1)}) custom-call(bf16[128,2560]{1,0:T(8,128)(2,1)S(1)} %copy-done.3, bf16[128,1024]{1,0:T(8,128)(2,1)S(1)} %copy-done.1, bf16[2560,1024]{1,0:T(8,128)(2,1)} %bitcast.21, f32[2560,128]{1,0:T(8,128)S(1)} %maximum_select_fusion.project), custom_call_target="tpu_custom_call" | custom-call | flops 1342177280 | bytes 5242880 | tf_op jit(solution)/shard_map/query_part/pallas_call | solution.py:93
  88.0 0.6 collective-permute-start.2
  88.6 0.1 copy.10
  88.6 1.1 collective-permute-done.2
  89.7 0.7 dynamic-slice_add_fusion.1
  90.4 3.5 %all-to-all-start.3 = ((f32[16,32,128]{2,1,0:T(8,128)}), f32[16,32,128]{2,1,0:T(8,128)S(1)}, u32[]{:S(2)}, u32[]{:S(2)}) async-start(f32[16,32,128]{2,1,0:T(8,128)} %bitcast.6), calls=%async_computation.4 | async-start | bytes 524288 | tf_op jit(solution)/shard_map/all_to_all | solution.py:196
  94.0 11.7 %cholesky.14 = f32[128,128]{1,0:T(8,128)S(1)} custom-call(f32[128,128]{1,0:T(8,128)S(1)} %fusion.9), custom_call_target="Cholesky" | custom-call | tf_op jit(solution)/shard_map/jit(cholesky)/cholesky | solution.py:221
  105.8 0.6 compare_reduce_fusion
  106.4 0.7 broadcast_in_dim.12
  107.2 7.2 %all-to-all-start.4 = ((f32[16,32,128]{2,1,0:T(8,128)}), f32[16,32,128]{2,1,0:T(8,128)S(1)}, u32[]{:S(2)}, u32[]{:S(2)}) async-start(f32[16,32,128]{2,1,0:T(8,128)} %broadcast_in_dim.12), calls=%async_computation.5 | async-start | bytes 524288 | tf_op jit(solution)/shard_map/all_to_all | solution.py:205
  114.3 0.7 fusion.6
  115.0 9.8 %custom-call.6 = f32[1,128,128]{1,2,0:T(8,128)S(1)} custom-call(f32[1,128,128]{2,1,0:T(8,128)S(1)} %fusion.6), custom_call_target="InvertDiagBlocksLowerTriangular" | custom-call | tf_op jit(solution)/shard_map/triangular_solve | solution.py:223
  124.8 0.2 fusion.7
  125.0 0.1 collective-permute-start.3
  125.1 1.2 fusion.12.basis
  126.3 0.3 collective-permute-done.3
  126.6 0.6 convolution_multiply_fusion.query
  127.2 8.3 %residual.1 = (bf16[2560,1024]{1,0:T(8,128)(2,1)}, f32[80,1024]{1,0:T(8,128)}) custom-call(bf16[128,2560]{1,0:T(8,128)(2,1)S(1)} %copy-done.3, bf16[128,1024]{1,0:T(8,128)(2,1)S(1)} %copy-done.1, bf16[2560,1024]{1,0:T(8,128)(2,1)} %bitcast.22, f32[2560,128]{1,0:T(8,128)S(1)} %fusion.12.basis, f32[80,128]{1,0:T(8,128)S(1)} %constant_dynamic-slice_fusion.1.basis_share, ...), custom_call_target="tpu_custom_call" | custom-call | flops 2684354560 | bytes 10485760 | tf_op jit(solution)/shard_map/residual/pallas_call | solution.py:148
  135.5 1.6 %convert_element_type.4 = bf16[128,320]{0,1:T(8,128)(2,1)} convert(f32[128,320]{0,1:T(8,128)} %reduce-scatter.2.cloned.1.call-done) | non-fusion elementwise | flops 40960 | bytes 245760 | tf_op jit(solution)/shard_map/convert_element_type | solution.py:235
  (28 shorter events, 0.5 us)
Async XLA Ops:
  7.2 68.6 %all-gather.2.cloned.1.call-start = ((), (), s32[]{:S(2)}) async-start(), calls=%async_computation.6 | async-start | bytes 5406720 | tf_op jit(solution)/shard_map/all_gather | solution.py:231
  7.9 127.6 %reduce-scatter.2.cloned.1.call-start = ((), (), s32[]{:S(2)}) async-start(), calls=%async_computation.7 | async-start | bytes 1474560 | tf_op jit(solution)/shard_map/reduce_scatter | solution.py:235
  8.0 1.0 copy-start
  8.9 1.1 copy-start.2
  10.0 1.0 copy-start.4
  16.7 2.2 %collective-permute-start = (f32[1280,128]{1,0:T(8,128)S(1)}, f32[1280,128]{1,0:T(8,128)S(1)}, u32[]{:S(2)}, u32[]{:S(2)}) collective-permute-start(f32[1280,128]{1,0:T(8,128)S(1)} %constant_dynamic-slice_fusion.2), channel_id=1, source_target_pairs={{0,8},{8,0},{16,24},{24,16},{32,40},{40,32},{48,56},{56,48},{64,72... | collective-permute-start | bytes 1966088 | tf_op jit(solution)/shard_map/ppermute | solution.py:187
  60.1 15.7 %copy-start.1 = (bf16[128,1024]{1,0:T(8,128)(2,1)S(1)}, bf16[128,1024]{1,0:T(8,128)(2,1)}, u32[]{:S(2)}) copy-start(bf16[128,1024]{1,0:T(8,128)(2,1)} %hidden.5) | copy-start | bytes 786436
  75.7 5.2 %collective-permute-start.1 = (f32[1280,128]{1,0:T(8,128)S(1)}, f32[1280,128]{1,0:T(8,128)S(1)}, u32[]{:S(2)}, u32[]{:S(2)}) collective-permute-start(f32[1280,128]{1,0:T(8,128)S(1)} %bitcast.24), channel_id=1, source_target_pairs={{0,8},{8,0},{16,24},{24,16},{32,40},{40,32},{48,56},{56,48},{64,72... | collective-permute-start | bytes 1966088 | tf_op jit(solution)/shard_map/ppermute | solution.py:187
  80.9 1.1 copy-start.3
  88.0 1.8 %collective-permute-start.2 = (f32[512,128]{1,0:T(8,128)S(1)}, f32[512,128]{1,0:T(8,128)S(1)}, u32[]{:S(2)}, u32[]{:S(2)}) collective-permute-start(f32[512,128]{1,0:T(8,128)S(1)} %constant_dynamic-slice_fusion), channel_id=1, source_target_pairs={{0,8},{8,0},{16,24},{24,16},{32,40},{40,32},{48,56},{56,48},{64,72... | collective-permute-start | bytes 786440 | tf_op jit(solution)/shard_map/ppermute | solution.py:187
  90.4 16.0 %all-to-all-start.3 = ((f32[16,32,128]{2,1,0:T(8,128)}), f32[16,32,128]{2,1,0:T(8,128)S(1)}, u32[]{:S(2)}, u32[]{:S(2)}) async-start(f32[16,32,128]{2,1,0:T(8,128)} %bitcast.6), calls=%async_computation.4 | async-start | bytes 524288 | tf_op jit(solution)/shard_map/all_to_all | solution.py:196
  107.2 17.9 %all-to-all-start.4 = ((f32[16,32,128]{2,1,0:T(8,128)}), f32[16,32,128]{2,1,0:T(8,128)S(1)}, u32[]{:S(2)}, u32[]{:S(2)}) async-start(f32[16,32,128]{2,1,0:T(8,128)} %broadcast_in_dim.12), calls=%async_computation.5 | async-start | bytes 524288 | tf_op jit(solution)/shard_map/all_to_all | solution.py:205
  125.0 1.6 %collective-permute-start.3 = (f32[512,128]{1,0:T(8,128)S(1)}, f32[512,128]{1,0:T(8,128)S(1)}, u32[]{:S(2)}, u32[]{:S(2)}) collective-permute-start(f32[512,128]{1,0:T(8,128)S(1)} %bitcast.26), channel_id=1, source_target_pairs={{0,8},{8,0},{16,24},{24,16},{32,40},{40,32},{48,56},{56,48},{64,72... | collective-permute-start | bytes 786440 | tf_op jit(solution)/shard_map/ppermute | solution.py:187
  127.2 8.3 %copy-start.5 = (f32[1024,128]{1,0:T(8,128)}, f32[1024,128]{1,0:T(8,128)S(1)}, u32[]{:S(2)}) copy-start(f32[1024,128]{1,0:T(8,128)S(1)} %convolution_multiply_fusion.query) | copy-start | bytes 1572868
Sparse Core Ops, SparseCore 0:
  10.5 63.5 all-gather.1
  81.0 37.5 reduce-scatter.1

commit v2 on v1

--- a/solution.py
+++ b/solution.py
@@ -120,7 +120,7 @@
     )(acts, hidden, error, project)
 
 
-def residual_kernel(acts, hidden, error, basis, basis_share, query, out, update, first, second):
+def residual_kernel(acts, hidden, error, basis, basis_share, query, out, update, factors):
     rank = query.shape[1]
 
     @pl.when(pl.program_id(0) == 0)
@@ -128,16 +128,17 @@
         turned = query[...].T
         high = turned.astype(BF16)
         rest = (turned - high.astype(F32)).astype(BF16)
-        first[:rank, :] = high
-        first[rank:, :] = high
-        second[:rank, :] = rest
-        second[rank:, :] = -hidden[...]
+        factors[:rank, :] = high
+        factors[rank : 2 * rank, :] = high
+        factors[2 * rank : 3 * rank, :] = rest
+        factors[3 * rank :, :] = -hidden[...]
         share = pair(basis_share[...])
-        update[...] = dot(share, first[...], ((1,), (0,))) + dot(share[:, :rank], rest, ((1,), (0,)))
+        share = jnp.concatenate([share, share[:, :rank]], axis=1)
+        update[...] = dot(share, factors[: 3 * rank, :], ((1,), (0,)))
 
     split = pair(basis[...])
-    mixed = jnp.concatenate([split[:, :rank], acts[...].T], axis=1)
-    change = dot(split, first[...], ((1,), (0,))) + dot(mixed, second[...], ((1,), (0,)))
+    mixed = jnp.concatenate([split, split[:, :rank], acts[...].T], axis=1)
+    change = dot(mixed, factors[...], ((1,), (0,)))
     out[...] = (error[...].astype(F32) - change).astype(BF16)
 
 
@@ -165,8 +166,7 @@
             jax.ShapeDtypeStruct((share, columns), F32),
         ),
         scratch_shapes=[
-            pltpu.VMEM((2 * rank, columns), BF16),
-            pltpu.VMEM((rank + tokens, columns), BF16),
+            pltpu.VMEM((3 * rank + tokens, columns), BF16),
         ],
         compiler_params=pltpu.CompilerParams(vmem_limit_bytes=VMEM_LIMIT),
         cost_estimate=pl.CostEstimate(
@@ -217,22 +217,79 @@
     return jnp.sum(lax.all_to_all(spread, "mp", 0, 0), axis=0)
 
 
+SUB = 8
+
+
+def inverse_factor_kernel(gram, out, table):
+    rank = gram.shape[0]
+    table[:, :rank] = gram[...]
+    row = lax.broadcasted_iota(jnp.int32, (rank, rank), 0)
+    column = lax.broadcasted_iota(jnp.int32, (rank, rank), 1)
+    table[:, rank:] = jnp.where(row == column, 1.0, 0.0)
+    place = lax.broadcasted_iota(jnp.int32, (SUB, 2 * rank), 0)
+    for first in range(0, rank, SUB):
+        panel = table[first : first + SUB, :]
+        for j in range(SUB):
+            across = panel[:, first + j : first + j + 1]
+            pivot = across[j : j + 1, :]
+            scale = lax.rsqrt(pivot)
+            scale = scale * (1.5 - 0.5 * pivot * scale * scale)
+            solved = panel[j : j + 1, :] * scale
+            reduced = panel - (across * scale) * solved
+            panel = jnp.where(place > j, reduced, jnp.where(place == j, solved, panel))
+        table[first : first + SUB, :] = panel
+        if first + SUB < rank:
+            change = lax.dot_general(
+                panel[:, :rank],
+                panel,
+                (((0,), (0,)), ((), ())),
+                precision=HIGHEST,
+                preferred_element_type=F32,
+            )
+            table[first + SUB :, :] -= change[first + SUB :, :]
+    out[...] = table[:, rank:].T
+
+
 def inverse_factor(gram_matrix):
-    factor = jnp.linalg.cholesky(gram_matrix)
-    identity = jnp.eye(gram_matrix.shape[0], dtype=F32)
-    return lax.linalg.triangular_solve(factor, identity, left_side=False, lower=True, transpose_a=True)
+    rank = gram_matrix.shape[0]
+    return pl.pallas_call(
+        inverse_factor_kernel,
+        out_shape=jax.ShapeDtypeStruct((rank, rank), F32),
+        grid=(1,),
+        in_specs=[pl.BlockSpec((rank, rank), lambda i: (0, 0))],
+        out_specs=pl.BlockSpec((rank, rank), lambda i: (0, 0)),
+        scratch_shapes=[pltpu.VMEM((rank, 2 * rank), F32)],
+        compiler_params=pltpu.CompilerParams(vmem_limit_bytes=VMEM_LIMIT),
+        cost_estimate=pl.CostEstimate(flops=2 * 10**9, bytes_accessed=10**7, transcendentals=128),
+        name="inverse_factor",
+    )(gram_matrix)
+
+
+def input_gradient(grad_hidden, up_weight, replicas):
+    core = lax.axis_index("dp") % CORES
+    theirs = swapped(grad_hidden, replicas)
+    both = jnp.concatenate(
+        [jnp.where(core == 0, grad_hidden, theirs), jnp.where(core == 0, theirs, grad_hidden)], 0
+    )
+    weight = lax.all_gather(
+        up_weight, "dp", axis=0, tiled=True, axis_index_groups=chips_of(replicas)
+    )
+    partial_input = dot(both, weight, ((1,), (1,)))
+    turned = lax.psum_scatter(partial_input, "mp", scatter_dimension=1, tiled=True).astype(BF16).T
+    tokens, share = grad_hidden.shape[0], up_weight.shape[0]
+    mine = jnp.where(core == 0, turned[:, :tokens], turned[:, tokens:])
+    other = swapped(jnp.where(core == 0, turned[:, tokens:], turned[:, :tokens]), replicas)
+    mine, other = (x.reshape(-1, 1, share, tokens) for x in (mine, other))
+    ordered = jnp.where(
+        core == 0, jnp.concatenate([mine, other], 1), jnp.concatenate([other, mine], 1)
+    )
+    return ordered.reshape(-1, tokens).T
 
 
 def local(activations, grad_hidden, up_weight, error_feedback, query_previous):
     replicas = lax.axis_size("dp")
     error = error_feedback[0]
-    partial_input = lax.dot_general(
-        grad_hidden,
-        lax.all_gather(up_weight, "dp", axis=0, tiled=True),
-        (((1,), (1,)), ((), ())),
-        preferred_element_type=F32,
-    )
-    grad_input = lax.psum_scatter(partial_input, "mp", scatter_dimension=1, tiled=True).astype(BF16)
+    grad_input = input_gradient(grad_hidden, up_weight, replicas)
 
     part = project_part(activations, grad_hidden, error, query_previous)
     project = gather_rows(sum_over_mp(scatter_sum(part, replicas)), replicas)

time: 147 us -> 146 us (level)
  the two profiles are of different devices: /device:TPU:32 before, /device:TPU:1 now
where the time goes in v2:
time: 146 us; the launch traced here: 145 us
  blocking collectives  48.9 us (33%)
  Pallas kernels  35.6 us (24%)
  starting transfers between devices  20.3 us (14%)
  between operations  14.3 us (10%)
  waiting for transfers between devices  10.5 us (7%)
  matrix products  7.28 us (5%)
  local copies, waits for them, and re-layouts  7.01 us (5%)
  other arithmetic  1.48 us (1%)
    all_to_all x2, blocking collectives, scatter_sum(): lax.all_to_all(x.reshape(chips, half // chips, -1), 'dp', 0, 0, axis_inde...  31 us
    all_to_all x1, blocking collectives, sum_over_mp(): return jnp.sum(lax.all_to_all(spread, 'mp', 0, 0), axis=0)  17.9 us
    pallas_call x1, Pallas kernels, inverse_factor(): pl.pallas_call(inverse_factor_kernel, out_shape=jax.ShapeDtypeStruct((ran...  16.1 us
    ppermute x6, starting transfers between devices, swapped(): return lax.ppermute(x, 'dp', [(i, i ^ 1) for i in range(replicas)])  12.5 us
    pallas_call x1, Pallas kernels, residual(): pl.pallas_call(residual_kernel, grid=(rows // BLOCK,), in_specs=[pl.Block...  8 us
    all_to_all x2, starting transfers between devices, gather_rows(): lax.all_to_all(spread, 'dp', 0, 0, axis_index_groups=chips_of(replicas))  7.79 us
    pallas_call x1, Pallas kernels, query_part(): pl.pallas_call(query_kernel, grid=(rows // BLOCK,), in_specs=[pl.BlockSpe...  5.93 us
    pallas_call x1, Pallas kernels, project_part(): pl.pallas_call(project_kernel, grid=(rows // BLOCK,), in_specs=[pl.BlockS...  5.61 us
  transfers between devices with their start and end apart: 10, of which 4 were waited for; matrix products, arithmetic and copies ran while one was open for 6% of the time, Pallas kernels for 24%

profile of v2, /device:TPU:1, one launch (start us, length us, event | category | flops | bytes accessed | tf_op | source)
XLA Modules:
  0.0 145.4 jit_solution(6597257045615689658)
XLA Ops:
  7.2 0.7 all-gather.2.cloned.1.call-update
  7.9 1.1 copy-done
  9.0 0.9 copy-done.2
  10.0 1.0 copy-done.4
  11.0 5.6 %project_part.1 = f32[2560,128]{1,0:T(8,128)S(1)} custom-call(bf16[128,2560]{1,0:T(8,128)(2,1)S(1)} %copy-done, bf16[128,1024]{1,0:T(8,128)(2,1)S(1)} %copy-done.2, bf16[2560,1024]{1,0:T(8,128)(2,1)} %bitcast.17, f32[1024,128]{1,0:T(8,128)S(1)} %copy-done.4), custom_call_target="tpu_custom_call" | custom-call | flops 1342177280 | bytes 5242880 | tf_op jit(solution)/shard_map/project_part/pallas_call | solution.py:47
  16.7 3.3 %collective-permute-start.2 = (f32[1280,128]{1,0:T(8,128)S(1)}, f32[1280,128]{1,0:T(8,128)S(1)}, u32[]{:S(2)}, u32[]{:S(2)}) collective-permute-start(f32[1280,128]{1,0:T(8,128)S(1)} %constant_dynamic-slice_fusion.2), channel_id=1, source_target_pairs={{0,8},{8,0},{16,24},{24,16},{32,40},{40,32},{48,56},{56,48},{64,72... | collective-permute-start | bytes 1966088 | tf_op jit(solution)/shard_map/ppermute | solution.py:187
  20.0 1.7 %collective-permute-done.2 = f32[1280,128]{1,0:T(8,128)S(1)} collective-permute-done((f32[1280,128]{1,0:T(8,128)S(1)}, f32[1280,128]{1,0:T(8,128)S(1)}, u32[]{:S(2)}, u32[]{:S(2)}) %collective-permute-start.2) | collective-permute-done | bytes 655392 | tf_op jit(solution)/shard_map/ppermute | solution.py:187
  21.8 19.6 %all_to_all.25 = f32[16,80,128]{2,1,0:T(8,128)S(1)} all-to-all(f32[16,80,128]{2,1,0:T(8,128)S(1)} %bitcast.20), channel_id=1, replica_groups={{0,16,32,48,64,80,96,112,128,144,160,176,192,208,224,240},{8,24,40,56,7..., dimensions={0} | all-to-all | bytes 1310720 | tf_op jit(solution)/shard_map/all_to_all | solution.py:196
  41.5 17.9 %all_to_all.26 = f32[8,80,128]{2,1,0:T(8,128)S(1)} all-to-all(f32[8,80,128]{2,1,0:T(8,128)S(1)} %broadcast_in_dim.8), channel_id=1, replica_groups=mesh['dp'=32,'mp'=8] {'mp'}, dimensions={0} | all-to-all | bytes 655360 | tf_op jit(solution)/shard_map/all_to_all | solution.py:217
  59.4 0.9 broadcast_in_dim.9
  60.3 3.6 %all-to-all-start.2 = ((f32[16,80,128]{2,1,0:T(8,128)}), f32[16,80,128]{2,1,0:T(8,128)S(1)}, u32[]{:S(2)}, u32[]{:S(2)}) async-start(f32[16,80,128]{2,1,0:T(8,128)} %broadcast_in_dim.9), calls=%async_computation.3 | async-start | bytes 1310720 | tf_op jit(solution)/shard_map/all_to_all | solution.py:205
  63.9 3.6 %collective-permute-start = (bf16[128,1024]{1,0:T(8,128)(2,1)S(1)}, bf16[128,1024]{1,0:T(8,128)(2,1)S(1)}, u32[]{:S(2)}, u32[]{:S(2)}) collective-permute-start(bf16[128,1024]{1,0:T(8,128)(2,1)S(1)} %copy-done.3), channel_id=1, source_target_pairs={{0,8},{8,0},{16,24},{24,16},{32,40},{40,32},{48,56},{56,48},{64,72... | collective-permute-start | bytes 786440 | tf_op jit(solution)/shard_map/ppermute | solution.py:187
  67.5 1.2 collective-permute-done
  68.7 5.4 %all-to-all-done.2 = f32[16,80,128]{2,1,0:T(8,128)S(1)} async-done(((f32[16,80,128]{2,1,0:T(8,128)}), f32[16,80,128]{2,1,0:T(8,128)S(1)}, u32[]{:S(2)}, u32[]{:S(2)}) %all-to-all-start.2) | async-done | bytes 655392 | tf_op jit(solution)/shard_map/all_to_all | solution.py:205
  74.1 4.0 %collective-permute-start.3 = (f32[1280,128]{1,0:T(8,128)S(1)}, f32[1280,128]{1,0:T(8,128)S(1)}, u32[]{:S(2)}, u32[]{:S(2)}) collective-permute-start(f32[1280,128]{1,0:T(8,128)S(1)} %bitcast.21), channel_id=1, source_target_pairs={{0,8},{8,0},{16,24},{24,16},{32,40},{40,32},{48,56},{56,48},{64,72... | collective-permute-start | bytes 1966088 | tf_op jit(solution)/shard_map/ppermute | solution.py:187
  78.1 3.7 %fusion = f32[256,1280]{0,1:T(8,128)} fusion(bf16[1280,1024]{1,0:T(8,128)(2,1)} %all-gather.2.cloned.1.call-done, bf16[128,1024]{1,0:T(8,128)(2,1)S(1)} %get-tuple-element.13, bf16[128,1024]{1,0:T(8,128)(2,1)S(1)} %get-tuple-element.12), kind=kOutput, calls=%fused_computation.3 | convolution fusion | flops 672137216 | bytes 4456448 | tf_op jit(solution)/shard_map/dot_general | solution.py:18
  81.9 0.1 maximum_select_fusion.project
  82.0 0.9 copy-done.1
  82.9 5.9 %query_part.1 = (f32[1024,128]{1,0:T(8,128)S(1)}, f32[128,128]{1,0:T(8,128)S(1)}) custom-call(bf16[128,2560]{1,0:T(8,128)(2,1)S(1)} %copy-done.1, bf16[128,1024]{1,0:T(8,128)(2,1)S(1)} %copy-done.3, bf16[2560,1024]{1,0:T(8,128)(2,1)} %bitcast.18, f32[2560,128]{1,0:T(8,128)S(1)} %maximum_select_fusion.project), custom_call_target="tpu_custom_call" | custom-call | flops 1342177280 | bytes 5242880 | tf_op jit(solution)/shard_map/query_part/pallas_call | solution.py:93
  89.0 1.5 %collective-permute-done.4 = f32[512,128]{1,0:T(8,128)S(1)} collective-permute-done((f32[512,128]{1,0:T(8,128)S(1)}, f32[512,128]{1,0:T(8,128)S(1)}, u32[]{:S(2)}, u32[]{:S(2)}) %collective-permute-start.4) | collective-permute-done | bytes 262176 | tf_op jit(solution)/shard_map/ppermute | solution.py:187
  90.6 11.4 %all_to_all.27 = f32[16,32,128]{2,1,0:T(8,128)S(1)} all-to-all(f32[16,32,128]{2,1,0:T(8,128)S(1)} %bitcast.23), channel_id=1, replica_groups={{0,16,32,48,64,80,96,112,128,144,160,176,192,208,224,240},{8,24,40,56,7..., dimensions={0} | all-to-all | bytes 524288 | tf_op jit(solution)/shard_map/all_to_all | solution.py:196
  102.0 0.7 broadcast_in_dim.10
  102.7 4.2 %all-to-all-start.4 = ((f32[16,32,128]{2,1,0:T(8,128)}), f32[16,32,128]{2,1,0:T(8,128)}, u32[]{:S(2)}, u32[]{:S(2)}) async-start(f32[16,32,128]{2,1,0:T(8,128)} %broadcast_in_dim.10), calls=%async_computation.5 | async-start | bytes 524288 | tf_op jit(solution)/shard_map/all_to_all | solution.py:205
  106.9 16.1 %inverse_factor.1 = f32[128,128]{1,0:T(8,128)S(1)} custom-call(f32[128,128]{1,0:T(8,128)S(1)} %get-tuple-element.8.gram), custom_call_target="tpu_custom_call" | custom-call | flops 2000000000 | bytes 10000000 | tf_op jit(solution)/shard_map/inverse_factor/pallas_call | solution.py:255
  123.0 0.6 copy-done.5
  123.7 1.3 collective-permute-start.5
  124.9 2.0 %fusion.12.basis = f32[2560,128]{1,0:T(8,128)S(1)} fusion(f32[2560,128]{1,0:T(8,128)S(1)} %maximum_select_fusion.project, f32[128,128]{1,0:T(8,128)} %copy-done.5), kind=kOutput, calls=%fused_computation.26 | convolution fusion | flops 503316480 | bytes 2686976 | tf_op jit(solution)/shard_map/dot_general | solution.py:299
  127.0 1.6 %convolution_multiply_fusion.query = f32[1024,128]{1,0:T(8,128)S(1)} fusion(f32[128,128]{1,0:T(8,128)S(1)} %copy-done.6, f32[512,128]{1,0:T(8,128)S(1)} %collective-permute-done.5, f32[512,128]{1,0:T(8,128)} %bitcast.9, pred[]{:T(512)S(6)} %eq.8), kind=kOutput, calls=%fused_computation.1 | convolution fusion | flops 201850880 | bytes 1114113 | tf_op jit(solution)/shard_map/dot_general | solution.py:300
  128.6 1.1 convert_bitcast_fusion
  129.8 0.2 collective-permute-start.1
  129.9 8.0 %residual.1 = (bf16[2560,1024]{1,0:T(8,128)(2,1)}, f32[80,1024]{1,0:T(8,128)}) custom-call(bf16[128,2560]{1,0:T(8,128)(2,1)S(1)} %copy-done.1, bf16[128,1024]{1,0:T(8,128)(2,1)S(1)} %copy-done.3, bf16[2560,1024]{1,0:T(8,128)(2,1)} %bitcast.19, f32[2560,128]{1,0:T(8,128)S(1)} %fusion.12.basis, f32[80,128]{1,0:T(8,128)S(1)} %constant_dynamic-slice_fusion.1.basis_share, ...), custom_call_target="tpu_custom_call" | custom-call | flops 2684354560 | bytes 10485760 | tf_op jit(solution)/shard_map/residual/pallas_call | solution.py:149
  137.9 0.6 copy.10
  (33 shorter events, 0.6 us)
Async XLA Ops:
  7.2 71.0 %all-gather.2.cloned.1.call-start = ((), (), s32[]{:S(2)}) async-start(), calls=%async_computation.6 | async-start | bytes 2785280 | tf_op jit(solution)/shard_map/all_gather | solution.py:274
  7.9 1.1 copy-start
  9.0 0.9 copy-start.2
  10.0 1.0 copy-start.4
  16.7 5.1 %collective-permute-start.2 = (f32[1280,128]{1,0:T(8,128)S(1)}, f32[1280,128]{1,0:T(8,128)S(1)}, u32[]{:S(2)}, u32[]{:S(2)}) collective-permute-start(f32[1280,128]{1,0:T(8,128)S(1)} %constant_dynamic-slice_fusion.2), channel_id=1, source_target_pairs={{0,8},{8,0},{16,24},{24,16},{32,40},{40,32},{48,56},{56,48},{64,72... | collective-permute-start | bytes 1966088 | tf_op jit(solution)/shard_map/ppermute | solution.py:187
  59.4 4.6 %copy-start.3 = (bf16[128,1024]{1,0:T(8,128)(2,1)S(1)}, bf16[128,1024]{1,0:T(8,128)(2,1)}, u32[]{:S(2)}) copy-start(bf16[128,1024]{1,0:T(8,128)(2,1)} %hidden.5) | copy-start | bytes 786436
  60.3 13.8 %all-to-all-start.2 = ((f32[16,80,128]{2,1,0:T(8,128)}), f32[16,80,128]{2,1,0:T(8,128)S(1)}, u32[]{:S(2)}, u32[]{:S(2)}) async-start(f32[16,80,128]{2,1,0:T(8,128)} %broadcast_in_dim.9), calls=%async_computation.3 | async-start | bytes 1310720 | tf_op jit(solution)/shard_map/all_to_all | solution.py:205
  63.9 64.7 %reduce-scatter.2.cloned.1.call-start = ((), (), s32[]{:S(2)}) async-start(), calls=%async_computation.7 | async-start | bytes 1474560 | tf_op jit(solution)/shard_map/reduce_scatter | solution.py:278
  63.9 4.7 %collective-permute-start = (bf16[128,1024]{1,0:T(8,128)(2,1)S(1)}, bf16[128,1024]{1,0:T(8,128)(2,1)S(1)}, u32[]{:S(2)}, u32[]{:S(2)}) collective-permute-start(bf16[128,1024]{1,0:T(8,128)(2,1)S(1)} %copy-done.3), channel_id=1, source_target_pairs={{0,8},{8,0},{16,24},{24,16},{32,40},{40,32},{48,56},{56,48},{64,72... | collective-permute-start | bytes 786440 | tf_op jit(solution)/shard_map/ppermute | solution.py:187
  74.1 7.8 %collective-permute-start.3 = (f32[1280,128]{1,0:T(8,128)S(1)}, f32[1280,128]{1,0:T(8,128)S(1)}, u32[]{:S(2)}, u32[]{:S(2)}) collective-permute-start(f32[1280,128]{1,0:T(8,128)S(1)} %bitcast.21), channel_id=1, source_target_pairs={{0,8},{8,0},{16,24},{24,16},{32,40},{40,32},{48,56},{56,48},{64,72... | collective-permute-start | bytes 1966088 | tf_op jit(solution)/shard_map/ppermute | solution.py:187
  81.9 1.1 copy-start.1
  88.9 1.6 %collective-permute-start.4 = (f32[512,128]{1,0:T(8,128)S(1)}, f32[512,128]{1,0:T(8,128)S(1)}, u32[]{:S(2)}, u32[]{:S(2)}) collective-permute-start(f32[512,128]{1,0:T(8,128)S(1)} %constant_dynamic-slice_fusion), channel_id=1, source_target_pairs={{0,8},{8,0},{16,24},{24,16},{32,40},{40,32},{48,56},{56,48},{64,72... | collective-permute-start | bytes 786440 | tf_op jit(solution)/shard_map/ppermute | solution.py:187
  102.7 20.9 %all-to-all-start.4 = ((f32[16,32,128]{2,1,0:T(8,128)}), f32[16,32,128]{2,1,0:T(8,128)}, u32[]{:S(2)}, u32[]{:S(2)}) async-start(f32[16,32,128]{2,1,0:T(8,128)} %broadcast_in_dim.10), calls=%async_computation.5 | async-start | bytes 524288 | tf_op jit(solution)/shard_map/all_to_all | solution.py:205
  123.0 0.6 copy-start.5
  123.7 3.3 %copy-start.6 = (f32[128,128]{1,0:T(8,128)S(1)}, f32[128,128]{1,0:T(8,128)}, u32[]{:S(2)}) copy-start(f32[128,128]{1,0:T(8,128)} %copy-done.5) | copy-start | bytes 196612
  123.7 3.3 %collective-permute-start.5 = (f32[512,128]{1,0:T(8,128)}, f32[512,128]{1,0:T(8,128)S(1)}, u32[]{:S(2)}, u32[]{:S(2)}) collective-permute-start(f32[512,128]{1,0:T(8,128)} %bitcast.9), channel_id=1, source_target_pairs={{0,8},{8,0},{16,24},{24,16},{32,40},{40,32},{48,56},{56,48},{64,72... | collective-permute-start | bytes 786440 | tf_op jit(solution)/shard_map/ppermute | solution.py:187
  128.6 9.3 %copy-start.7 = (f32[1024,128]{1,0:T(8,128)}, f32[1024,128]{1,0:T(8,128)S(1)}, u32[]{:S(2)}) copy-start(f32[1024,128]{1,0:T(8,128)S(1)} %convolution_multiply_fusion.query) | copy-start | bytes 1572868
  129.8 8.2 %collective-permute-start.1 = (bf16[160,128]{1,0:T(8,128)(2,1)S(1)}, bf16[160,128]{1,0:T(8,128)(2,1)S(1)}, u32[]{:S(2)}, u32[]{:S(2)}) collective-permute-start(bf16[160,128]{1,0:T(8,128)(2,1)S(1)} %get-tuple-element.15), channel_id=1, source_target_pairs={{0,8},{8,0},{16,24},{24,16},{32,40},{40,32},{48,56},{56,48},{64,72... | collective-permute-start | bytes 122888 | tf_op jit(solution)/shard_map/ppermute | solution.py:187
Sparse Core Ops, SparseCore 0:
  10.4 58.7 all-gather.1
  82.0 32.1 reduce-scatter.1

commit v3 on v2

v3 whole, which is shorter than its diff:
```python
import functools

import jax
import jax.numpy as jnp
from jax import lax
from jax.experimental import pallas as pl
from jax.experimental.pallas import tpu as pltpu
from jax.sharding import PartitionSpec as P

HIGHEST = lax.Precision.HIGHEST
F32 = jnp.float32
BF16 = jnp.bfloat16
BLOCK = 640
CORES = 2
VMEM_LIMIT = 48 << 20

def dot(a, b, dims):
    return lax.dot_general(a, b, (dims, ((), ())), preferred_element_type=F32)

def pair(x):
    high = x.astype(BF16)
    rest = (x - high.astype(F32)).astype(BF16)
    return jnp.concatenate([high, rest], axis=1)

def folded(x):
    half = x.shape[1] // 2
    return x[:, :half] + x[:, half:]

def load(source, target, sem):
    copy = pltpu.make_async_copy(source, target, sem)
    copy.start()
    return copy

def row_of(step, core, rows):
    half = rows // CORES
    steps = half // BLOCK
    own = jnp.where(step < steps, core, 1 - core)
    return pl.multiple_of(own * half + lax.rem(step, steps) * BLOCK, BLOCK)

def start_rows(core, error, error_rows, sems):
    rows = error.shape[0]

    def start(step, carry):
        load(error.at[pl.ds(row_of(step, core, rows), BLOCK)], error_rows.at[step], sems.at[step])
        return carry

    lax.fori_loop(0, rows // BLOCK, start, 0)

def wait_rows(step, error, error_rows, sems):
    pltpu.make_async_copy(error.at[pl.ds(0, BLOCK)], error_rows.at[step], sems.at[step]).wait()

def halves(core, rows, body, first, second):
    steps = rows // CORES // BLOCK
    for base, ref in ((0, first), (steps, second)):

        def step_of(i, carry, base=base, ref=ref):
            body(base + i, row_of(base + i, core, rows), pl.multiple_of(i * BLOCK, BLOCK), ref)
            return carry

        lax.fori_loop(0, steps, step_of, 0)

def project_kernel(place, acts, hidden, error, query, mine, theirs,
                   acts_in, hidden_in, query_in, error_rows, query_pair, token_pair, small, sems):
    core = place[0]
    copies = [
        load(query, query_in, small.at[0]),
        load(hidden, hidden_in, small.at[1]),
        load(acts, acts_in, small.at[2]),
    ]
    start_rows(core, error, error_rows, sems)
    copies[0].wait()
    split = pair(query_in[...])
    query_pair[...] = split
    copies[1].wait()
    token_pair[...] = pair(folded(dot(hidden_in[...], split, ((1,), (0,)))))
    copies[2].wait()

    def body(step, row, at, ref):
        wait_rows(step, error, error_rows, sems)
        total = dot(error_rows[step], query_pair[...], ((1,), (0,)))
        total += dot(acts_in[:, pl.ds(row, BLOCK)], token_pair[...], ((0,), (0,)))
        ref[pl.ds(at, BLOCK), :] = folded(total)

    halves(core, error.shape[0], body, mine, theirs)

HBM = pl.BlockSpec(memory_space=pltpu.HBM)
SCALARS = pl.BlockSpec(memory_space=pltpu.SMEM)

def whole(shape):
    return pl.BlockSpec(shape, lambda i: (0,) * len(shape))

def project_part(place, acts, hidden, error, query):
    tokens, rows = acts.shape
    columns, rank = query.shape
    half = (rows // CORES, rank)
    return pl.pallas_call(
        project_kernel,
        grid=(1,),
        in_specs=[SCALARS, HBM, HBM, HBM, HBM],
        out_specs=(whole(half), whole(half)),
        out_shape=(jax.ShapeDtypeStruct(half, F32),) * 2,
        scratch_shapes=[
            pltpu.VMEM((tokens, rows), BF16),
            pltpu.VMEM((tokens, columns), BF16),
            pltpu.VMEM((columns, rank), F32),
            pltpu.VMEM((rows // BLOCK, BLOCK, columns), BF16),
            pltpu.VMEM((columns, 2 * rank), BF16),
            pltpu.VMEM((tokens, 2 * rank), BF16),
            pltpu.SemaphoreType.DMA((3,)),
            pltpu.SemaphoreType.DMA((rows // BLOCK,)),
        ],
        compiler_params=pltpu.CompilerParams(vmem_limit_bytes=60 << 20),
        cost_estimate=pl.CostEstimate(
            flops=4 * rows * columns * rank, bytes_accessed=2 * rows * columns, transcendentals=0
        ),
        name="project_part",
    )(place, acts, hidden, error, query)

def query_kernel(place, acts, hidden, error, own, other, mine, theirs, gram,
                 acts_in, hidden_in, error_rows, total, tokens_sum, gram_sum, small, sems):
    core = place[0]
    rank = gram.shape[0]
    acts_copy = load(acts, acts_in, small.at[0])
    start_rows(core, error, error_rows, sems)
    hidden_copy = load(hidden, hidden_in, small.at[1])
    total[...] = jnp.zeros_like(total)
    tokens_sum[...] = jnp.zeros_like(tokens_sum)
    gram_sum[...] = jnp.zeros_like(gram_sum)
    acts_copy.wait()

    def body(step, row, at, ref):
        split = pair(ref[pl.ds(at, BLOCK), :])
        gram_sum[...] += dot(split, split, ((0,), (0,)))
        tokens_sum[...] += dot(acts_in[:, pl.ds(row, BLOCK)], split, ((1,), (0,)))
        wait_rows(step, error, error_rows, sems)
        total[...] += dot(split, error_rows[step], ((0,), (0,)))

    halves(core, error.shape[0], body, own, other)
    hidden_copy.wait()
    spread = pair(folded(tokens_sum[...]))
    turned = total[...] + dot(spread, hidden_in[...], ((0,), (0,)))
    total[:rank, :] = turned[:rank, :] + turned[rank:, :]
    half = mine.shape[0]
    mine[...] = total[:rank, pl.ds(pl.multiple_of(core * half, half), half)].T
    theirs[...] = total[:rank, pl.ds(pl.multiple_of((1 - core) * half, half), half)].T
    gram[...] = folded(gram_sum[:rank, :] + gram_sum[rank:, :])

def query_part(place, acts, hidden, error, own, other):
    tokens, rows = acts.shape
    columns = hidden.shape[1]
    rank = own.shape[1]
    half = (columns // CORES, rank)
    return pl.pallas_call(
        query_kernel,
        grid=(1,),
        in_specs=[SCALARS, HBM, HBM, HBM, whole(own.shape), whole(own.shape)],
        out_specs=(whole(half), whole(half), whole((rank, rank))),
        out_shape=(
            jax.ShapeDtypeStruct(half, F32),
            jax.ShapeDtypeStruct(half, F32),
            jax.ShapeDtypeStruct((rank, rank), F32),
        ),
        scratch_shapes=[
            pltpu.VMEM((tokens, rows), BF16),
            pltpu.VMEM((tokens, columns), BF16),
            pltpu.VMEM((rows // BLOCK, BLOCK, columns), BF16),
            pltpu.VMEM((2 * rank, columns), F32),
            pltpu.VMEM((tokens, 2 * rank), F32),
            pltpu.VMEM((2 * rank, 2 * rank), F32),
            pltpu.SemaphoreType.DMA((2,)),
            pltpu.SemaphoreType.DMA((rows // BLOCK,)),
        ],
        compiler_params=pltpu.CompilerParams(vmem_limit_bytes=VMEM_LIMIT),
        cost_estimate=pl.CostEstimate(
            flops=4 * rows * columns * rank, bytes_accessed=2 * rows * columns, transcendentals=0
        ),
        name="query_part",
    )(place, acts, hidden, error, own, other)

def triple(x):
    split = pair(x)
    return jnp.concatenate([split, split[:, : x.shape[1]]], axis=1)

def stacked(x):
    high = x.astype(BF16)
    rest = (x - high.astype(F32)).astype(BF16)
    return jnp.concatenate([high, high, rest], axis=0)

def residual_kernel(place, acts, hidden, error, own, other, inverse, query_own, query_other,
                    out, update, query,
                    acts_in, hidden_in, error_rows, turn, factors, small, sems, sent):
    core, replica, replicas = place[0], place[1], place[2]
    rank = inverse.shape[0]
    rows = error.shape[0]
    acts_copy = load(acts, acts_in, small.at[0])
    hidden_copy = load(hidden, hidden_in, small.at[1])
    start_rows(core, error, error_rows, sems)
    turn[...] = stacked(inverse[...])
    scale = 1.0 / replicas.astype(F32)
    half = query_own.shape[0]
    for ref, first in ((query_own, core * half), (query_other, (1 - core) * half)):
        query[pl.ds(pl.multiple_of(first, half), half), :] = (
            dot(triple(ref[...]), turn[...], ((1,), (0,))) * scale
        )
    factors[: 3 * rank, :] = stacked(query[...].T)
    hidden_copy.wait()
    factors[3 * rank :, :] = -hidden_in[...]
    share = update.shape[0]
    first = replica * share
    within = lax.rem(first, rows // CORES)
    at = pl.ds(pl.multiple_of(within, 8), share)
    own_half = jnp.where(first < rows // CORES, 0, 1) == core
    picked = jnp.where(own_half, own[at, :], other[at, :])
    basis = dot(triple(picked), turn[...], ((1,), (0,)))
    update[...] = dot(triple(basis), factors[: 3 * rank, :], ((1,), (0,)))
    acts_copy.wait()

    def body(step, row, at, ref):
        basis = dot(triple(ref[pl.ds(at, BLOCK), :]), turn[...], ((1,), (0,)))
        mixed = jnp.concatenate([triple(basis), acts_in[:, pl.ds(row, BLOCK)].T], axis=1)
        change = dot(mixed, factors[...], ((1,), (0,)))
        wait_rows(step, error, error_rows, sems)
        error_rows[step] = (error_rows[step].astype(F32) - change).astype(BF16)
        load(error_rows.at[step], out.at[pl.ds(row, BLOCK)], sent.at[step])

    halves(core, rows, body, own, other)

    def drain(step, carry):
        pltpu.make_async_copy(error_rows.at[step], out.at[pl.ds(0, BLOCK)], sent.at[step]).wait()
        return carry

    lax.fori_loop(0, rows // BLOCK, drain, 0)

def residual(place, acts, hidden, error, own, other, inverse, query_own, query_other, share):
    tokens, rows = acts.shape
    columns = hidden.shape[1]
    rank = inverse.shape[0]
    return pl.pallas_call(
        residual_kernel,
        grid=(1,),
        in_specs=[
            SCALARS, HBM, HBM, HBM, whole(own.shape), whole(own.shape), whole(inverse.shape),
            whole(query_own.shape), whole(query_own.shape),
        ],
        out_specs=(HBM, whole((share, columns)), whole((columns, rank))),
        out_shape=(
            jax.ShapeDtypeStruct((rows, columns), BF16),
            jax.ShapeDtypeStruct((share, columns), F32),
            jax.ShapeDtypeStruct((columns, rank), F32),
        ),
        scratch_shapes=[
            pltpu.VMEM((tokens, rows), BF16),
            pltpu.VMEM((tokens, columns), BF16),
            pltpu.VMEM((rows // BLOCK, BLOCK, columns), BF16),
            pltpu.VMEM((3 * rank, rank), BF16),
            pltpu.VMEM((3 * rank + tokens, columns), BF16),
            pltpu.SemaphoreType.DMA((2,)),
            pltpu.SemaphoreType.DMA((rows // BLOCK,)),
            pltpu.SemaphoreType.DMA((rows // BLOCK,)),
        ],
        compiler_params=pltpu.CompilerParams(vmem_limit_bytes=VMEM_LIMIT),
        cost_estimate=pl.CostEstimate(
            flops=8 * rows * columns * rank, bytes_accessed=4 * rows * columns, transcendentals=0
        ),
        name="residual",
    )(place, acts, hidden, error, own, other, inverse, query_own, query_other)


def chips_of(replicas):
    return [list(range(core, replicas, CORES)) for core in range(CORES)]

def swapped(x, replicas):
    return lax.ppermute(x, "dp", [(i, i ^ 1) for i in range(replicas)])

def scatter_sum(mine, theirs, replicas):
    x = mine + swapped(theirs, replicas)
    chips = replicas // CORES
    pieces = lax.all_to_all(
        x.reshape(chips, x.shape[0] // chips, -1), "dp", 0, 0, axis_index_groups=chips_of(replicas)
    )
    return jnp.sum(pieces, axis=0)

def gather_rows(x, replicas):
    chips = replicas // CORES
    spread = jnp.broadcast_to(x[None], (chips, *x.shape))
    mine = lax.all_to_all(spread, "dp", 0, 0, axis_index_groups=chips_of(replicas))
    return mine.reshape(chips * x.shape[0], -1)

def sum_over_mp(x):
    ranks = lax.axis_size("mp")
    spread = jnp.broadcast_to(x[None], (ranks, *x.shape))
    return jnp.sum(lax.all_to_all(spread, "mp", 0, 0), axis=0)

SUB = 32
GROUP = 8

def inverse_factor_kernel(gram, out, table):
    rank = gram.shape[0]
    table[:, :rank] = gram[...]
    row = lax.broadcasted_iota(jnp.int32, (rank, rank), 0)
    column = lax.broadcasted_iota(jnp.int32, (rank, rank), 1)
    table[:, rank:] = jnp.where(row == column, 1.0, 0.0)
    shape = (SUB, rank)
    place = lax.broadcasted_iota(jnp.int32, shape, 0)
    for first in range(0, rank, SUB):
        parts = [table[first : first + SUB, :rank], table[first : first + SUB, rank:]]
        for j in range(SUB):
            if j % GROUP == 0:
                columns = [
                    jnp.broadcast_to(parts[0][:, first + k : first + k + 1], shape)
                    for k in range(j, j + GROUP)
                ]
            across = columns.pop(0)
            pivot = across[j : j + 1, :]
            scale = lax.rsqrt(pivot)
            factor = jnp.where(place > j, across * (scale * scale), 0.0)
            columns = [x - factor * x[j : j + 1, :] for x in columns]
            keep = jnp.where(place == j, scale, 1.0)
            parts = [x * keep - factor * x[j : j + 1, :] for x in parts]
        panel = jnp.concatenate(parts, axis=1)
        table[first : first + SUB, :] = panel
        if first + SUB < rank:
            change = lax.dot_general(
                parts[0],
                panel,
                (((0,), (0,)), ((), ())),
                precision=HIGHEST,
                preferred_element_type=F32,
            )
            table[first + SUB :, :] -= change[first + SUB :, :]
    out[...] = table[:, rank:].T

def inverse_factor(gram_matrix):
    rank = gram_matrix.shape[0]
    return pl.pallas_call(
        inverse_factor_kernel,
        out_shape=jax.ShapeDtypeStruct((rank, rank), F32),
        grid=(1,),
        in_specs=[pl.BlockSpec((rank, rank), lambda i: (0, 0))],
        out_specs=pl.BlockSpec((rank, rank), lambda i: (0, 0)),
        scratch_shapes=[pltpu.VMEM((rank, 2 * rank), F32)],
        compiler_params=pltpu.CompilerParams(vmem_limit_bytes=VMEM_LIMIT),
        cost_estimate=pl.CostEstimate(flops=2 * 10**9, bytes_accessed=10**7, transcendentals=128),
        name="inverse_factor",
    )(gram_matrix)

def input_gradient(grad_hidden, up_weight):
    partial_input = dot(grad_hidden, lax.all_gather(up_weight, "dp", axis=0, tiled=True), ((1,), (1,)))
    return lax.psum_scatter(partial_input, "mp", scatter_dimension=1, tiled=True)

def local(activations, grad_hidden, up_weight, error_feedback, query_previous):
    replicas = lax.axis_size("dp")
    error = error_feedback[0]
    replica = lax.axis_index("dp")
    place = jnp.stack([replica % CORES, replica, jnp.int32(replicas)])
    mine, theirs = project_part(place, activations, grad_hidden, error, query_previous)
    own = gather_rows(sum_over_mp(scatter_sum(mine, theirs, replicas)), replicas)
    other = swapped(own, replicas)
    grad_input = input_gradient(grad_hidden, up_weight)
    mine, theirs, gram_matrix = query_part(place, activations, grad_hidden, error, own, other)
    inverse = inverse_factor(gram_matrix)
    query_own = gather_rows(scatter_sum(mine, theirs, replicas), replicas)
    query_own, inverse = lax.optimization_barrier((query_own, inverse))
    query_other = swapped(query_own, replicas)
    error_next, update, query_next = residual(
        place, activations, grad_hidden, error, own, other, inverse, query_own, query_other,
        error.shape[0] // replicas,
    )
    grad_input, error_next = lax.optimization_barrier((grad_input, error_next))
    return (grad_input.astype(BF16), error_next[None], update, query_next)

def solution(mesh):
    in_specs = (P("dp", None), P("dp", "mp"), P("dp", "mp"), P("dp", None, "mp"), P("mp", None))
    out_specs = (P("dp", "mp"), P("dp", None, "mp"), P("dp", "mp"), P("mp", None))
    return jax.shard_map(local, mesh=mesh, in_specs=in_specs, out_specs=out_specs, check_vma=False)
```

time: 146 us -> 136 us (0.932)
  the two profiles are of different devices: /device:TPU:1 before, /device:TPU:32 now
where the time goes in v3:
time: 136 us; the launch traced here: 135 us
  blocking collectives  56.3 us (41%)
  Pallas kernels  24.9 us (18%)
  waiting for transfers between devices  21.5 us (16%)
  between operations  14.2 us (10%)
  starting transfers between devices  7.97 us (6%)
  matrix products  5.12 us (4%)
  other arithmetic  3.41 us (3%)
  local copies, waits for them, and re-layouts  1.65 us (1%)
    all_to_all x2, blocking collectives, scatter_sum(): lax.all_to_all(x.reshape(chips, x.shape[0] // chips, -1), 'dp', 0, 0, axi...  35.9 us
    all_to_all x1, blocking collectives, sum_over_mp(): return jnp.sum(lax.all_to_all(spread, 'mp', 0, 0), axis=0)  20.4 us
    all_gather x1, waiting for transfers between devices, input_gradient(): lax.all_gather(up_weight, 'dp', axis=0, tiled=True)  9.42 us
    pallas_call x1, Pallas kernels, residual(): pl.pallas_call(residual_kernel, grid=(1,), in_specs=[SCALARS, HBM, HBM, H...  8.75 us
    all_to_all x2, starting transfers between devices, gather_rows(): lax.all_to_all(spread, 'dp', 0, 0, axis_index_groups=chips_of(replicas))  7.13 us
    ppermute x4, waiting for transfers between devices, swapped(): return lax.ppermute(x, 'dp', [(i, i ^ 1) for i in range(replicas)])  6.96 us
    pallas_call x1, Pallas kernels, query_part(): pl.pallas_call(query_kernel, grid=(1,), in_specs=[SCALARS, HBM, HBM, HBM,...  6.09 us
    pallas_call x1, Pallas kernels, project_part(): pl.pallas_call(project_kernel, grid=(1,), in_specs=[SCALARS, HBM, HBM, HB...  5.86 us
  transfers between devices with their start and end apart: 8, of which 6 were waited for; matrix products, arithmetic and copies ran while one was open for 6% of the time, Pallas kernels for 18%

profile of v3, /device:TPU:32, one launch (start us, length us, event | category | flops | bytes accessed | tf_op | source)
XLA Modules:
  0.0 135.1 jit_solution(4668844224963425778)
XLA Ops:
  7.2 0.0 all-gather.2.cloned.1.call-start
  7.2 0.7 all-gather.2.cloned.1.call-update
  7.9 0.6 pad_add_fusion.place
  8.5 5.9 %project_part.1 = (f32[1280,128]{1,0:T(8,128)}, f32[1280,128]{1,0:T(8,128)}) custom-call(s32[3]{0:T(128)} %pad_add_fusion.place, bf16[128,2560]{1,0:T(8,128)(2,1)} %acts.5, bf16[128,1024]{1,0:T(8,128)(2,1)} %hidden.5, bf16[2560,1024]{1,0:T(8,128)(2,1)} %bitcast.15, f32[1024,128]{1,0:T(8,128)} %query.1), custom_call_target="tpu_custom_call" | custom-call | flops 1342177280 | bytes 5242880 | tf_op jit(solution)/shard_map/project_part/pallas_call | solution.py:96
  14.4 0.0 copy-start
  14.4 0.1 collective-permute-start
  14.5 2.3 %collective-permute-done = f32[1280,128]{1,0:T(8,128)S(1)} collective-permute-done((f32[1280,128]{1,0:T(8,128)}, f32[1280,128]{1,0:T(8,128)S(1)}, u32[]{:S(2)}, u32[]{:S(2)}) %collective-permute-start) | collective-permute-done | bytes 655392 | tf_op jit(solution)/shard_map/ppermute | solution.py:273
  16.8 1.2 add.13
  17.9 21.8 %all_to_all.25 = f32[16,80,128]{2,1,0:T(8,128)S(1)} all-to-all(f32[16,80,128]{2,1,0:T(8,128)S(1)} %bitcast.18), channel_id=1, replica_groups={{0,16,32,48,64,80,96,112,128,144,160,176,192,208,224,240},{8,24,40,56,7..., dimensions={0} | all-to-all | bytes 1310720 | tf_op jit(solution)/shard_map/all_to_all | solution.py:278
  39.9 20.4 %all_to_all.26 = f32[8,80,128]{2,1,0:T(8,128)S(1)} all-to-all(f32[8,80,128]{2,1,0:T(8,128)S(1)} %broadcast_in_dim.8), channel_id=1, replica_groups=mesh['dp'=32,'mp'=8] {'mp'}, dimensions={0} | all-to-all | bytes 655360 | tf_op jit(solution)/shard_map/all_to_all | solution.py:292
  60.3 0.9 broadcast_in_dim.9
  61.1 3.6 %all-to-all-start.2 = ((f32[16,80,128]{2,1,0:T(8,128)}), f32[16,80,128]{2,1,0:T(8,128)S(1)}, u32[]{:S(2)}, u32[]{:S(2)}) async-start(f32[16,80,128]{2,1,0:T(8,128)} %broadcast_in_dim.9), calls=%async_computation.3 | async-start | bytes 1310720 | tf_op jit(solution)/shard_map/all_to_all | solution.py:286
  64.7 0.0 copy-start.1
  64.8 0.0 copy-start.2
  64.8 0.0 reduce-scatter.2.cloned.1.call-start
  64.8 9.4 %all-gather.2.cloned.1.call-done = bf16[2560,1024]{1,0:T(8,128)(2,1)} async-done(((bf16[80,1024]{1,0:T(8,128)(2,1)}), bf16[2560,1024]{1,0:T(8,128)(2,1)}) %all-gather.2.cloned.1.call-update) | async-done | bytes 5242896 | tf_op jit(solution)/shard_map/all_gather | solution.py:348
  74.2 5.1 %fusion = f32[128,2560]{0,1:T(8,128)} fusion(bf16[128,1024]{1,0:T(8,128)(2,1)S(1)} %copy-done, bf16[2560,1024]{1,0:T(8,128)(2,1)} %all-gather.2.cloned.1.call-done), kind=kOutput, calls=%fused_computation.1 | convolution fusion | flops 671088640 | bytes 6815744 | tf_op jit(solution)/shard_map/dot_general | solution.py:18
  79.4 0.0 reduce-scatter.2.cloned.1.call-update
  79.4 0.3 collective-permute-start.1
  79.7 1.8 %collective-permute-done.1.other = f32[1280,128]{1,0:T(8,128)S(1)} collective-permute-done((f32[1280,128]{1,0:T(8,128)S(1)}, f32[1280,128]{1,0:T(8,128)S(1)}, u32[]{:S(2)}, u32[]{:S(2)}) %collective-permute-start.1) | collective-permute-done | bytes 655392 | tf_op jit(solution)/shard_map/ppermute | solution.py:273
  81.6 6.1 %query_part.1 = (f32[512,128]{1,0:T(8,128)S(1)}, f32[512,128]{1,0:T(8,128)S(1)}, f32[128,128]{1,0:T(8,128)S(1)}) custom-call(s32[3]{0:T(128)S(1)} %copy-done.2, bf16[128,2560]{1,0:T(8,128)(2,1)S(1)} %copy-done.1, bf16[128,1024]{1,0:T(8,128)(2,1)S(1)} %copy-done, bf16[2560,1024]{1,0:T(8,128)(2,1)} %bitcast.16, f32[1280,128]{1,0:T(8,128)S(1)} %bitcast.11, ...), custom_call_target="tpu_custom_call" | custom-call | flops 1342177280 | bytes 5242880 | tf_op jit(solution)/shard_map/query_part/pallas_call | solution.py:153
  87.7 0.3 collective-permute-start.2
  88.0 1.3 collective-permute-done.2
  89.3 14.0 %all_to_all.27 = f32[16,32,128]{2,1,0:T(8,128)S(1)} all-to-all(f32[16,32,128]{2,1,0:T(8,128)S(1)} %bitcast.19), channel_id=1, replica_groups={{0,16,32,48,64,80,96,112,128,144,160,176,192,208,224,240},{8,24,40,56,7..., dimensions={0} | all-to-all | bytes 524288 | tf_op jit(solution)/shard_map/all_to_all | solution.py:278
  103.4 0.7 broadcast_in_dim.10
  104.1 3.5 %all-to-all-start.4 = ((f32[16,32,128]{2,1,0:T(8,128)}), f32[16,32,128]{2,1,0:T(8,128)S(1)}, u32[]{:S(2)}, u32[]{:S(2)}) async-start(f32[16,32,128]{2,1,0:T(8,128)} %broadcast_in_dim.10), calls=%async_computation.5 | async-start | bytes 524288 | tf_op jit(solution)/shard_map/all_to_all | solution.py:286
  107.7 4.2 %inverse_factor.1.inverse = f32[128,128]{1,0:T(8,128)S(1)} custom-call(f32[128,128]{1,0:T(8,128)S(1)} %get-tuple-element.20.gram), custom_call_target="tpu_custom_call" | custom-call | flops 2000000000 | bytes 10000000 | tf_op jit(solution)/shard_map/inverse_factor/pallas_call | solution.py:335
  111.9 4.4 %all-to-all-done.4 = f32[16,32,128]{2,1,0:T(8,128)S(1)} async-done(((f32[16,32,128]{2,1,0:T(8,128)}), f32[16,32,128]{2,1,0:T(8,128)S(1)}, u32[]{:S(2)}, u32[]{:S(2)}) %all-to-all-start.4) | async-done | bytes 262176 | tf_op jit(solution)/shard_map/all_to_all | solution.py:286
  116.3 1.5 %collective-permute-done.3.query_other = f32[512,128]{1,0:T(8,128)S(1)} collective-permute-done((f32[512,128]{1,0:T(8,128)S(1)}, f32[512,128]{1,0:T(8,128)S(1)}, u32[]{:S(2)}, u32[]{:S(2)}) %collective-permute-start.3) | collective-permute-done | bytes 262176 | tf_op jit(solution)/shard_map/ppermute | solution.py:273
  117.9 8.8 %residual.1 = (bf16[2560,1024]{1,0:T(8,128)(2,1)}, f32[80,1024]{1,0:T(8,128)}, f32[1024,128]{1,0:T(8,128)}) custom-call(s32[3]{0:T(128)S(1)} %copy-done.2, bf16[128,2560]{1,0:T(8,128)(2,1)S(1)} %copy-done.1, bf16[128,1024]{1,0:T(8,128)(2,1)S(1)} %copy-done, bf16[2560,1024]{1,0:T(8,128)(2,1)} %bitcast.17, f32[1280,128]{1,0:T(8,128)S(1)} %bitcast.12, ...), custom_call_target="tpu_custom_call" | custom-call | flops 2684354560 | bytes 10485760 | tf_op jit(solution)/shard_map/residual/pallas_call | solution.py:238
  126.6 0.0 reduce-scatter.2.cloned.1.call-done
  126.7 1.6 %convert_element_type.3 = bf16[128,320]{0,1:T(8,128)(2,1)} convert(f32[128,320]{0,1:T(8,128)} %reduce-scatter.2.cloned.1.call-done) | non-fusion elementwise | flops 40960 | bytes 245760 | tf_op jit(solution)/shard_map/convert_element_type | solution.py:370
  (10 shorter events, 0.1 us)
Async XLA Ops:
  7.2 67.1 %all-gather.2.cloned.1.call-start = ((), (), s32[]{:S(2)}) async-start(), calls=%async_computation.6 | async-start | bytes 5406720 | tf_op jit(solution)/shard_map/all_gather | solution.py:348
  14.4 59.9 %copy-start = (bf16[128,1024]{1,0:T(8,128)(2,1)S(1)}, bf16[128,1024]{1,0:T(8,128)(2,1)}, u32[]{:S(2)}) copy-start(bf16[128,1024]{1,0:T(8,128)(2,1)} %hidden.5) | copy-start | bytes 786436
  14.4 2.4 %collective-permute-start = (f32[1280,128]{1,0:T(8,128)}, f32[1280,128]{1,0:T(8,128)S(1)}, u32[]{:S(2)}, u32[]{:S(2)}) collective-permute-start(f32[1280,128]{1,0:T(8,128)} %get-tuple-element.17), channel_id=1, source_target_pairs={{0,8},{8,0},{16,24},{24,16},{32,40},{40,32},{48,56},{56,48},{64,72... | collective-permute-start | bytes 1966088 | tf_op jit(solution)/shard_map/ppermute | solution.py:273
  61.1 18.2 %all-to-all-start.2 = ((f32[16,80,128]{2,1,0:T(8,128)}), f32[16,80,128]{2,1,0:T(8,128)S(1)}, u32[]{:S(2)}, u32[]{:S(2)}) async-start(f32[16,80,128]{2,1,0:T(8,128)} %broadcast_in_dim.9), calls=%async_computation.3 | async-start | bytes 1310720 | tf_op jit(solution)/shard_map/all_to_all | solution.py:286
  64.7 16.8 %copy-start.1 = (bf16[128,2560]{1,0:T(8,128)(2,1)S(1)}, bf16[128,2560]{1,0:T(8,128)(2,1)}, u32[]{:S(2)}) copy-start(bf16[128,2560]{1,0:T(8,128)(2,1)} %acts.5) | copy-start | bytes 1966084
  64.8 16.8 %copy-start.2 = (s32[3]{0:T(128)S(1)}, s32[3]{0:T(128)}, u32[]{:S(2)}) copy-start(s32[3]{0:T(128)} %pad_add_fusion.place) | copy-start | bytes 40
  64.8 61.9 %reduce-scatter.2.cloned.1.call-start = ((), (), s32[]{:S(2)}) async-start(), calls=%async_computation.7 | async-start | bytes 1474560 | tf_op jit(solution)/shard_map/reduce_scatter | solution.py:349
  79.4 2.2 %collective-permute-start.1 = (f32[1280,128]{1,0:T(8,128)S(1)}, f32[1280,128]{1,0:T(8,128)S(1)}, u32[]{:S(2)}, u32[]{:S(2)}) collective-permute-start(f32[1280,128]{1,0:T(8,128)S(1)} %bitcast.10), channel_id=1, source_target_pairs={{0,8},{8,0},{16,24},{24,16},{32,40},{40,32},{48,56},{56,48},{64,72... | collective-permute-start | bytes 1966088 | tf_op jit(solution)/shard_map/ppermute | solution.py:273
  87.7 1.6 %collective-permute-start.2 = (f32[512,128]{1,0:T(8,128)S(1)}, f32[512,128]{1,0:T(8,128)S(1)}, u32[]{:S(2)}, u32[]{:S(2)}) collective-permute-start(f32[512,128]{1,0:T(8,128)S(1)} %get-tuple-element.19), channel_id=1, source_target_pairs={{0,8},{8,0},{16,24},{24,16},{32,40},{40,32},{48,56},{56,48},{64,72... | collective-permute-start | bytes 786440 | tf_op jit(solution)/shard_map/ppermute | solution.py:273
  104.1 12.2 %all-to-all-start.4 = ((f32[16,32,128]{2,1,0:T(8,128)}), f32[16,32,128]{2,1,0:T(8,128)S(1)}, u32[]{:S(2)}, u32[]{:S(2)}) async-start(f32[16,32,128]{2,1,0:T(8,128)} %broadcast_in_dim.10), calls=%async_computation.5 | async-start | bytes 524288 | tf_op jit(solution)/shard_map/all_to_all | solution.py:286
  116.3 1.5 %collective-permute-start.3 = (f32[512,128]{1,0:T(8,128)S(1)}, f32[512,128]{1,0:T(8,128)S(1)}, u32[]{:S(2)}, u32[]{:S(2)}) collective-permute-start(f32[512,128]{1,0:T(8,128)S(1)} %bitcast.13), channel_id=1, source_target_pairs={{0,8},{8,0},{16,24},{24,16},{32,40},{40,32},{48,56},{56,48},{64,72... | collective-permute-start | bytes 786440 | tf_op jit(solution)/shard_map/ppermute | solution.py:273
Sparse Core Ops, SparseCore 0:
  10.5 63.6 all-gather.1
  79.5 39.6 reduce-scatter.1

commit v4 on v3

--- a/solution.py
+++ b/solution.py
@@ -272,13 +272,13 @@
 def swapped(x, replicas):
     return lax.ppermute(x, "dp", [(i, i ^ 1) for i in range(replicas)])
 
-def scatter_sum(mine, theirs, replicas):
-    x = mine + swapped(theirs, replicas)
+def scatter_sum(x, replicas):
     chips = replicas // CORES
     pieces = lax.all_to_all(
         x.reshape(chips, x.shape[0] // chips, -1), "dp", 0, 0, axis_index_groups=chips_of(replicas)
     )
     return jnp.sum(pieces, axis=0)
+
 
 def gather_rows(x, replicas):
     chips = replicas // CORES
@@ -344,30 +344,137 @@
         name="inverse_factor",
     )(gram_matrix)
 
-def input_gradient(grad_hidden, up_weight):
-    partial_input = dot(grad_hidden, lax.all_gather(up_weight, "dp", axis=0, tiled=True), ((1,), (1,)))
-    return lax.psum_scatter(partial_input, "mp", scatter_dimension=1, tiled=True)
+def gradient_kernel(place, *refs):
+    core, across, down = place[0], place[3], place[4]
+    tokens, weights, out, table = refs[:WIDE], refs[WIDE : WIDE + HIGH], refs[-2], refs[-1]
+    share = weights[0].shape[0] // CORES
+    count = tokens[0].shape[0]
+    for d, ref in enumerate(tokens):
+        table[d * count : (d + 1) * count, :] = ref[...]
+    for e, ref in enumerate(weights):
+        block = dot(ref[...], table[...], ((1,), (1,)))
+        y = lax.rem(down - e + HIGH, HIGH)
+        for d in range(WIDE):
+            x = lax.rem(across - d + WIDE, WIDE)
+            for side, of_core in ((0, core), (1, 1 - core)):
+                at = pl.ds(pl.multiple_of(of_core * share, 8), share)
+                out[y, x, at, :] = block[
+                    side * share : (side + 1) * share, d * count : (d + 1) * count
+                ]
+
+
+def gradient_part(place, tokens, weights):
+    count, columns = tokens[0].shape
+    rows = weights[0].shape[0]
+    return pl.pallas_call(
+        gradient_kernel,
+        grid=(1,),
+        in_specs=[SCALARS, *(whole(x.shape) for x in (*tokens, *weights))],
+        out_specs=whole((HIGH, WIDE, rows, count)),
+        out_shape=jax.ShapeDtypeStruct((HIGH, WIDE, rows, count), F32),
+        scratch_shapes=[pltpu.VMEM((WIDE * count, columns), BF16)],
+        compiler_params=pltpu.CompilerParams(vmem_limit_bytes=60 << 20),
+        cost_estimate=pl.CostEstimate(
+            flops=2 * WIDE * HIGH * rows * count * columns, bytes_accessed=10**7, transcendentals=0
+        ),
+        name="gradient_part",
+    )(place, *tokens, *weights)
+
+
+WIDE = 4
+HIGH = 4
+
+
+def index_of(y, x, core):
+    return (y % HIGH * WIDE + x % WIDE) * CORES + core
+
+
+def shifted(x, replicas, rows, columns):
+    pairs = []
+    for i in range(replicas):
+        at, core = divmod(i, CORES)
+        y, across = divmod(at, WIDE)
+        pairs.append((i, index_of(y + rows, across + columns, core)))
+    return lax.ppermute(x, "dp", pairs)
+
+
+def after(x, earlier):
+    return lax.optimization_barrier((x, earlier))[0]
+
+
+def split_step(x, bit, distance, axis):
+    ranks = lax.axis_size("mp")
+    keep = lax.dynamic_index_in_dim(x, bit, axis, keepdims=False)
+    send = lax.dynamic_index_in_dim(x, 1 - bit, axis, keepdims=False)
+    return keep, lax.ppermute(send, "mp", [(i, i ^ distance) for i in range(ranks)])
+
+
+def settle(x, replicas):
+    ranks = lax.axis_size("mp")
+    across = lax.axis_index("dp") // CORES % WIDE
+    low = across % 2
+    got = []
+    for flip in range(2):
+        pairs = []
+        for i in range(replicas):
+            at, core = divmod(i, CORES)
+            y, column = divmod(at, WIDE)
+            for z in range(ranks):
+                to = index_of(y, 2 * (z % 2) + (column % 2 ^ flip), core)
+                pairs.append((i * ranks + z, to * ranks + (z // 2 * 2 + column // 2)))
+        piece = lax.dynamic_index_in_dim(x, low ^ flip, 0, keepdims=False)
+        got.append(lax.ppermute(piece, ("dp", "mp"), pairs))
+    return got, low
+
 
 def local(activations, grad_hidden, up_weight, error_feedback, query_previous):
     replicas = lax.axis_size("dp")
     error = error_feedback[0]
     replica = lax.axis_index("dp")
-    place = jnp.stack([replica % CORES, replica, jnp.int32(replicas)])
+    plane = lax.axis_index("mp")
+    chip = replica // CORES
+    place = jnp.stack(
+        [replica % CORES, replica, jnp.int32(replicas), chip % WIDE, chip // WIDE]
+    )
+    rows = jnp.concatenate([up_weight, swapped(up_weight, replicas)], axis=0)
     mine, theirs = project_part(place, activations, grad_hidden, error, query_previous)
-    own = gather_rows(sum_over_mp(scatter_sum(mine, theirs, replicas)), replicas)
+    mine = mine + swapped(theirs, replicas)
+
+    rows, hidden, mine = lax.optimization_barrier((rows, grad_hidden, mine))
+    tokens = [hidden] + [shifted(hidden, replicas, 0, d) for d in range(1, WIDE)]
+    weights = [rows] + [shifted(rows, replicas, e, 0) for e in range(1, HIGH)]
+    share = sum_over_mp(scatter_sum(mine, replicas))
+    tokens, weights, share = lax.optimization_barrier((tokens, weights, share))
+
+    own = gather_rows(share, replicas)
+    part = gradient_part(place, tokens, weights)
+    own, part = lax.optimization_barrier((own, part))
+    part = part.reshape(HIGH, 2, -1, part.shape[-1])
+    keep, sent = split_step(part, plane % 2, 1, 1)
     other = swapped(own, replicas)
-    grad_input = input_gradient(grad_hidden, up_weight)
     mine, theirs, gram_matrix = query_part(place, activations, grad_hidden, error, own, other)
     inverse = inverse_factor(gram_matrix)
-    query_own = gather_rows(scatter_sum(mine, theirs, replicas), replicas)
+
+    part = (after(keep, gram_matrix) + sent).reshape(HIGH // 2, 2, *keep.shape[1:])
+    keep, sent = split_step(part, plane // 2 % 2, 2, 1)
+    query_share = scatter_sum(mine + swapped(theirs, replicas), replicas)
+    part = after(keep, query_share) + sent
+    keep, sent = split_step(part, plane // 4, 4, 0)
+    query_own = gather_rows(query_share, replicas)
     query_own, inverse = lax.optimization_barrier((query_own, inverse))
+    part = (after(keep, query_own) + sent).astype(BF16)
+    got, low = settle(part.reshape(2, -1, part.shape[-1]), replicas)
     query_other = swapped(query_own, replicas)
     error_next, update, query_next = residual(
         place, activations, grad_hidden, error, own, other, inverse, query_own, query_other,
         error.shape[0] // replicas,
     )
-    grad_input, error_next = lax.optimization_barrier((grad_input, error_next))
-    return (grad_input.astype(BF16), error_next[None], update, query_next)
+    got = after(got, error_next)
+    grad_input = jnp.where(
+        low == 0, jnp.concatenate(got, axis=0), jnp.concatenate(got[::-1], axis=0)
+    ).T
+    return (grad_input, error_next[None], update, query_next)
+
 
 def solution(mesh):
     in_specs = (P("dp", None), P("dp", "mp"), P("dp", "mp"), P("dp", None, "mp"), P("mp", None))

time: 136 us -> 147 us (1.081)
  blocking collectives: 56.3 us -> 20.1 us
  starting transfers between devices: 7.97 us -> 38.4 us
  waiting for transfers between devices: 21.5 us -> 46.2 us
  between operations: 14.2 us -> 1 us
  matrix products: 5.12 us -> 0 us
  Pallas kernels: 24.9 us -> 29.5 us
  local copies, waits for them, and re-layouts: 1.65 us -> 5.43 us
  other arithmetic: 3.41 us -> 6.03 us
    ppermute x0 -> x11, waiting for transfers between devices: none -> 25.5 us  [the longest x3 14.5 us: split_step(): lax.ppermute(send, 'mp', [(i, i ^ distance) for i in range(ranks)])]
    all_to_all x1 -> x0, blocking collectives: 20.4 us -> none  [sum_over_mp(): return jnp.sum(lax.all_to_all(spread, 'mp', 0, 0), axis=0)]
    ppermute x0 -> x11, starting transfers between devices: none -> 17.3 us  [the longest x2 6.47 us: settle(): got.append(lax.ppermute(piece, ('dp', 'mp'), pairs))]
    all_to_all x2 -> x1, blocking collectives: 35.9 us -> 20.1 us  [scatter_sum(): lax.all_to_all(x.reshape(chips, x.shape[0] // chips, -1), 'dp', 0, 0, axi...]
    all_to_all x0 -> x2, starting transfers between devices: none -> 12.1 us  [the longest x1 8.57 us: sum_over_mp(): return jnp.sum(lax.all_to_all(spread, 'mp', 0, 0), axis=0)]
    all_to_all x0 -> x2, waiting for transfers between devices: none -> 10.4 us  [the longest x1 8.6 us: scatter_sum(): lax.all_to_all(x.reshape(chips, x.shape[0] // chips, -1), 'dp', 0, 0, axi...]
    all_gather x1 -> x0, waiting for transfers between devices: 9.42 us -> none  [input_gradient(): lax.all_gather(up_weight, 'dp', axis=0, tiled=True)]
    ppermute x4 -> x5, waiting for transfers between devices: 6.96 us -> 1.83 us  [swapped(): return lax.ppermute(x, 'dp', [(i, i ^ 1) for i in range(replicas)])]
  transfers between devices with their start and end apart: 8 -> 20, of which waited for: 6 -> 11; matrix products, arithmetic and copies ran while one was open for 6% -> 5% of each run, Pallas kernels for 18% -> 16%
where the time goes in v4:
time: 147 us
  waiting for transfers between devices  46.2 us (31%)
  starting transfers between devices  38.4 us (26%)
  Pallas kernels  29.5 us (20%)
  blocking collectives  20.1 us (14%)
  other arithmetic  6.03 us (4%)
  local copies, waits for them, and re-layouts  5.43 us (4%)
    all_to_all x1, blocking collectives, scatter_sum(): lax.all_to_all(x.reshape(chips, x.shape[0] // chips, -1), 'dp', 0, 0, axi...  20.1 us
    ppermute x3, waiting for transfers between devices, split_step(): lax.ppermute(send, 'mp', [(i, i ^ distance) for i in range(ranks)])  14.5 us
    ppermute x6, waiting for transfers between devices, shifted(): return lax.ppermute(x, 'dp', pairs)  11 us
    pallas_call x1, Pallas kernels, residual(): pl.pallas_call(residual_kernel, grid=(1,), in_specs=[SCALARS, HBM, HBM, H...  8.98 us
    all_to_all x1, waiting for transfers between devices, scatter_sum(): lax.all_to_all(x.reshape(chips, x.shape[0] // chips, -1), 'dp', 0, 0, axi...  8.6 us
    all_to_all x1, starting transfers between devices, sum_over_mp(): return jnp.sum(lax.all_to_all(spread, 'mp', 0, 0), axis=0)  8.57 us
    all_to_all x2, waiting for transfers between devices, gather_rows(): lax.all_to_all(spread, 'dp', 0, 0, axis_index_groups=chips_of(replicas))  8.45 us
    all_to_all x2, starting transfers between devices, gather_rows(): lax.all_to_all(spread, 'dp', 0, 0, axis_index_groups=chips_of(replicas))  7.98 us
  transfers between devices with their start and end apart: 20, of which 11 were waited for; matrix products, arithmetic and copies ran while one was open for 5% of the time, Pallas kernels for 16%

profile of v4, /device:TPU:32, one launch (start us, length us, event | category | flops | bytes accessed | tf_op | source)
XLA Modules:
  0.0 146.6 jit_solution(18307985229875458765)
XLA Ops:
  1.4 6.0 %project_part.1 = (f32[1280,128]{1,0:T(8,128)}, f32[1280,128]{1,0:T(8,128)}) custom-call(s32[5]{0:T(128)} %stack.19.place, bf16[128,2560]{1,0:T(8,128)(2,1)} %acts.5, bf16[128,1024]{1,0:T(8,128)(2,1)} %hidden.5, bf16[2560,1024]{1,0:T(8,128)(2,1)} %bitcast.36, f32[1024,128]{1,0:T(8,128)} %query.1), custom_call_target="tpu_custom_call" | custom-call | flops 1342177280 | bytes 5242880 | tf_op jit(solution)/shard_map/project_part/pallas_call | solution.py:96
  7.9 1.8 %collective-permute-done = bf16[80,1024]{1,0:T(8,128)(2,1)S(1)} collective-permute-done((bf16[80,1024]{1,0:T(8,128)(2,1)S(1)}, bf16[80,1024]{1,0:T(8,128)(2,1)S(1)}, u32[]{:S(2)}, u32[]{:S(2)}) %collective-permute-start) | collective-permute-done | bytes 163872 | tf_op jit(solution)/shard_map/ppermute | solution.py:273
  9.8 1.3 add.70
  11.1 20.1 %all_to_all.25 = f32[16,80,128]{2,1,0:T(8,128)S(1)} all-to-all(f32[16,80,128]{2,1,0:T(8,128)S(1)} %bitcast.40), channel_id=1, replica_groups={{0,16,32,48,64,80,96,112,128,144,160,176,192,208,224,240},{8,24,40,56,7..., dimensions={0} | all-to-all | bytes 1310720 | tf_op jit(solution)/shard_map/all_to_all | solution.py:277
  32.0 8.6 %all-to-all-start.1 = ((f32[8,80,128]{2,1,0:T(8,128)}), f32[8,80,128]{2,1,0:T(8,128)S(1)}, u32[]{:S(2)}, u32[]{:S(2)}) async-start(f32[8,80,128]{2,1,0:T(8,128)} %broadcast_in_dim.8), calls=%async_computation.1 | async-start | bytes 655360 | tf_op jit(solution)/shard_map/all_to_all | solution.py:292
  41.5 1.2 collective-permute-start.7
  42.7 1.5 %collective-permute-start.6 = (bf16[160,1024]{1,0:T(8,128)(2,1)S(1)}, bf16[160,1024]{1,0:T(8,128)(2,1)S(1)}, u32[]{:S(2)}, u32[]{:S(2)}) collective-permute-start(bf16[160,1024]{1,0:T(8,128)(2,1)S(1)} %pad_maximum_fusion.refs_4_), channel_id=1, source_target_pairs={{0,128},{8,136},{16,144},{24,152},{32,160},{40,168},{48,176},{56,1... | collective-permute-start | bytes 983048 | tf_op jit(solution)/shard_map/ppermute | solution.py:398
  44.2 1.4 collective-permute-start.3
  45.6 4.3 %collective-permute-done.4.refs_3_ = bf16[128,1024]{1,0:T(8,128)(2,1)S(1)} collective-permute-done((bf16[128,1024]{1,0:T(8,128)(2,1)S(1)}, bf16[128,1024]{1,0:T(8,128)(2,1)S(1)}, u32[]{:S(2)}, u32[]{:S(2)}) %collective-permute-start.4) | collective-permute-done | bytes 262176 | tf_op jit(solution)/shard_map/ppermute | solution.py:398
  49.8 1.8 %all-to-all-done.1 = f32[8,80,128]{2,1,0:T(8,128)S(1)} async-done(((f32[8,80,128]{2,1,0:T(8,128)}), f32[8,80,128]{2,1,0:T(8,128)S(1)}, u32[]{:S(2)}, u32[]{:S(2)}) %all-to-all-start.1) | async-done | bytes 327712 | tf_op jit(solution)/shard_map/all_to_all | solution.py:292
  51.6 2.7 %collective-permute-done.3.refs_2_ = bf16[128,1024]{1,0:T(8,128)(2,1)S(1)} collective-permute-done((bf16[128,1024]{1,0:T(8,128)(2,1)S(1)}, bf16[128,1024]{1,0:T(8,128)(2,1)S(1)}, u32[]{:S(2)}, u32[]{:S(2)}) %collective-permute-start.3) | collective-permute-done | bytes 262176 | tf_op jit(solution)/shard_map/ppermute | solution.py:398
  54.3 3.2 %collective-permute-done.2.refs_1_ = bf16[128,1024]{1,0:T(8,128)(2,1)} collective-permute-done((bf16[128,1024]{1,0:T(8,128)(2,1)S(1)}, bf16[128,1024]{1,0:T(8,128)(2,1)}, u32[]{:S(2)}, u32[]{:S(2)}) %collective-permute-start.2) | collective-permute-done | bytes 262176 | tf_op jit(solution)/shard_map/ppermute | solution.py:398
  58.4 0.9 broadcast_in_dim.9
  59.3 4.4 %all-to-all-start.2 = ((f32[16,80,128]{2,1,0:T(8,128)}), f32[16,80,128]{2,1,0:T(8,128)S(1)}, u32[]{:S(2)}, u32[]{:S(2)}) async-start(f32[16,80,128]{2,1,0:T(8,128)} %broadcast_in_dim.9), calls=%async_computation.2 | async-start | bytes 1310720 | tf_op jit(solution)/shard_map/all_to_all | solution.py:286
  63.8 4.2 %gradient_part.1 = f32[4,4,160,128]{3,2,1,0:T(8,128)} custom-call(s32[5]{0:T(128)} %stack.19.place, bf16[128,1024]{1,0:T(8,128)(2,1)} %hidden.5, bf16[128,1024]{1,0:T(8,128)(2,1)} %collective-permute-done.2.refs_1_, bf16[128,1024]{1,0:T(8,128)(2,1)} %copy-done.9, bf16[128,1024]{1,0:T(8,128)(2,1)} %copy-done.8, bf16[160,1024]{1,0:T(8,128)(2,1)} %copy-done.4, ...), custom_call_target="tpu_custom_call" | custom-call | flops 671088640 | bytes 10000000 | tf_op jit(solution)/shard_map/gradient_part/pallas_call | solution.py:369
  68.0 7.9 %all-to-all-done.2 = f32[16,80,128]{2,1,0:T(8,128)S(1)} async-done(((f32[16,80,128]{2,1,0:T(8,128)}), f32[16,80,128]{2,1,0:T(8,128)S(1)}, u32[]{:S(2)}, u32[]{:S(2)}) %all-to-all-start.2) | async-done | bytes 655392 | tf_op jit(solution)/shard_map/all_to_all | solution.py:286
  75.9 2.2 %dynamic-slice_bitcast_fusion = (f32[4,320,128]{2,1,0:T(8,128)}, f32[4,320,128]{2,1,0:T(8,128)S(1)}) fusion(f32[4,2,320,128]{3,2,1,0:T(8,128)} %bitcast.39, s32[]{:T(128)S(6)} %select_n.83, s32[]{:T(128)S(6)} %select_n.82), kind=kLoop, calls=%fused_computation | loop fusion | bytes 2621448 | tf_op jit(solution)/shard_map/jit(dynamic_index_in_dim)/squeeze | solution.py:408
  78.7 6.1 %query_part.1 = (f32[512,128]{1,0:T(8,128)S(1)}, f32[512,128]{1,0:T(8,128)S(1)}, f32[128,128]{1,0:T(8,128)S(1)}) custom-call(s32[5]{0:T(128)S(1)} %copy-done.3, bf16[128,2560]{1,0:T(8,128)(2,1)S(1)} %copy-done, bf16[128,1024]{1,0:T(8,128)(2,1)S(1)} %copy-done.2, bf16[2560,1024]{1,0:T(8,128)(2,1)} %bitcast.37, f32[1280,128]{1,0:T(8,128)S(1)} %bitcast.32, ...), custom_call_target="tpu_custom_call" | custom-call | flops 1342177280 | bytes 5242880 | tf_op jit(solution)/shard_map/query_part/pallas_call | solution.py:153
  85.4 10.2 %collective-permute-done.9 = f32[4,320,128]{2,1,0:T(8,128)} collective-permute-done((f32[4,320,128]{2,1,0:T(8,128)}, f32[4,320,128]{2,1,0:T(8,128)}, u32[]{:S(2)}, u32[]{:S(2)}) %collective-permute-start.9) | collective-permute-done | bytes 655392 | tf_op jit(solution)/shard_map/ppermute | solution.py:409
  95.6 1.2 add.74
  96.8 2.4 %collective-permute-start.11 = (f32[2,320,128]{2,1,0:T(8,128)S(1)}, f32[2,320,128]{2,1,0:T(8,128)}, u32[]{:S(2)}, u32[]{:S(2)}) collective-permute-start(f32[2,320,128]{2,1,0:T(8,128)S(1)} %get-tuple-element.64), channel_id=1, source_target_pairs={{0,2},{1,3},{2,0},{3,1},{4,6},{5,7},{6,4},{7,5},{8,10},{9,11},{10,... | collective-permute-start | bytes 983048 | tf_op jit(solution)/shard_map/ppermute | solution.py:409
  99.3 1.7 %add.77 = f32[512,128]{1,0:T(8,128)} add(f32[512,128]{1,0:T(8,128)S(1)} %get-tuple-element.51, f32[512,128]{1,0:T(8,128)} %collective-permute-done.10) | non-fusion elementwise | flops 65536 | bytes 786432 | tf_op jit(solution)/shard_map/add | solution.py:460
  101.0 3.5 %all-to-all-start.3 = ((f32[16,32,128]{2,1,0:T(8,128)}), f32[16,32,128]{2,1,0:T(8,128)S(1)}, u32[]{:S(2)}, u32[]{:S(2)}) async-start(f32[16,32,128]{2,1,0:T(8,128)} %bitcast.12), calls=%async_computation.3 | async-start | bytes 524288 | tf_op jit(solution)/shard_map/all_to_all | solution.py:277
  104.6 8.6 %all-to-all-done.3 = f32[16,32,128]{2,1,0:T(8,128)S(1)} async-done(((f32[16,32,128]{2,1,0:T(8,128)}), f32[16,32,128]{2,1,0:T(8,128)S(1)}, u32[]{:S(2)}, u32[]{:S(2)}) %all-to-all-start.3) | async-done | bytes 262176 | tf_op jit(solution)/shard_map/all_to_all | solution.py:277
  113.9 3.5 %all-to-all-start.4 = ((f32[16,32,128]{2,1,0:T(8,128)}), f32[16,32,128]{2,1,0:T(8,128)S(1)}, u32[]{:S(2)}, u32[]{:S(2)}) async-start(f32[16,32,128]{2,1,0:T(8,128)} %broadcast_in_dim.10), calls=%async_computation.4 | async-start | bytes 524288 | tf_op jit(solution)/shard_map/all_to_all | solution.py:286
  117.5 1.0 add.79
  118.5 2.8 %collective-permute-start.12 = (f32[320,128]{1,0:T(8,128)S(1)}, f32[320,128]{1,0:T(8,128)S(1)}, u32[]{:S(2)}, u32[]{:S(2)}) collective-permute-start(f32[320,128]{1,0:T(8,128)S(1)} %get-tuple-element.66), channel_id=1, source_target_pairs={{0,4},{1,5},{2,6},{3,7},{4,0},{5,1},{6,2},{7,3},{8,12},{9,13},{10,... | collective-permute-start | bytes 491528 | tf_op jit(solution)/shard_map/ppermute | solution.py:409
  121.3 4.2 %inverse_factor.1.inverse = f32[128,128]{1,0:T(8,128)S(1)} custom-call(f32[128,128]{1,0:T(8,128)S(1)} %get-tuple-element.49.gram), custom_call_target="tpu_custom_call" | custom-call | flops 2000000000 | bytes 10000000 | tf_op jit(solution)/shard_map/inverse_factor/pallas_call | solution.py:335
  126.1 4.3 %collective-permute-done.12 = f32[320,128]{1,0:T(8,128)S(1)} collective-permute-done((f32[320,128]{1,0:T(8,128)S(1)}, f32[320,128]{1,0:T(8,128)S(1)}, u32[]{:S(2)}, u32[]{:S(2)}) %collective-permute-start.12) | collective-permute-done | bytes 163872 | tf_op jit(solution)/shard_map/ppermute | solution.py:409
  130.5 2.3 %collective-permute-start.14 = (bf16[160,128]{1,0:T(8,128)(2,1)S(1)}, bf16[160,128]{1,0:T(8,128)(2,1)S(1)}, u32[]{:S(2)}, u32[]{:S(2)}) collective-permute-start(bf16[160,128]{1,0:T(8,128)(2,1)S(1)} %get-tuple-element.68), channel_id=1, source_target_pairs={{0,16},{1,48},{2,18},{3,50},{4,20},{5,52},{6,22},{7,54},{8,24},{9,... | collective-permute-start | bytes 122888 | tf_op jit(solution)/shard_map/ppermute | solution.py:426
  132.8 4.1 %collective-permute-start.13 = (bf16[160,128]{1,0:T(8,128)(2,1)S(1)}, bf16[160,128]{1,0:T(8,128)(2,1)S(1)}, u32[]{:S(2)}, u32[]{:S(2)}) collective-permute-start(bf16[160,128]{1,0:T(8,128)(2,1)S(1)} %get-tuple-element.69), channel_id=1, source_target_pairs={{0,0},{1,32},{2,2},{3,34},{4,4},{5,36},{6,6},{7,38},{8,8},{9,40},{... | collective-permute-start | bytes 122888 | tf_op jit(solution)/shard_map/ppermute | solution.py:426
  137.0 9.0 %residual.1 = (bf16[2560,1024]{1,0:T(8,128)(2,1)}, f32[80,1024]{1,0:T(8,128)}, f32[1024,128]{1,0:T(8,128)}) custom-call(s32[5]{0:T(128)S(1)} %copy-done.3, bf16[128,2560]{1,0:T(8,128)(2,1)S(1)} %copy-done, bf16[128,1024]{1,0:T(8,128)(2,1)S(1)} %copy-done.2, bf16[2560,1024]{1,0:T(8,128)(2,1)} %bitcast.38, f32[1280,128]{1,0:T(8,128)S(1)} %bitcast.33, ...), custom_call_target="tpu_custom_call" | custom-call | flops 2684354560 | bytes 10485760 | tf_op jit(solution)/shard_map/residual/pallas_call | solution.py:238
  (54 shorter events, 7.2 us)
Async XLA Ops:
  0.6 6.8 %copy-start.10 = (bf16[80,1024]{1,0:T(8,128)(2,1)S(1)}, bf16[80,1024]{1,0:T(8,128)(2,1)}, u32[]{:S(2)}) copy-start(bf16[80,1024]{1,0:T(8,128)(2,1)} %param.7) | copy-start | bytes 491524
  1.3 39.2 %copy-start.1 = (bf16[128,1024]{1,0:T(8,128)(2,1)S(1)}, bf16[128,1024]{1,0:T(8,128)(2,1)}, u32[]{:S(2)}) copy-start(bf16[128,1024]{1,0:T(8,128)(2,1)} %hidden.5) | copy-start | bytes 786436
  7.3 2.5 %collective-permute-start.1 = (f32[1280,128]{1,0:T(8,128)}, f32[1280,128]{1,0:T(8,128)S(1)}, u32[]{:S(2)}, u32[]{:S(2)}) collective-permute-start(f32[1280,128]{1,0:T(8,128)} %get-tuple-element.34), channel_id=1, source_target_pairs={{0,8},{8,0},{16,24},{24,16},{32,40},{40,32},{48,56},{56,48},{64,72... | collective-permute-start | bytes 1966088 | tf_op jit(solution)/shard_map/ppermute | solution.py:273
  7.4 2.3 %collective-permute-start = (bf16[80,1024]{1,0:T(8,128)(2,1)S(1)}, bf16[80,1024]{1,0:T(8,128)(2,1)S(1)}, u32[]{:S(2)}, u32[]{:S(2)}) collective-permute-start(bf16[80,1024]{1,0:T(8,128)(2,1)S(1)} %copy-done.10), channel_id=1, source_target_pairs={{0,8},{8,0},{16,24},{24,16},{32,40},{40,32},{48,56},{56,48},{64,72... | collective-permute-start | bytes 491528 | tf_op jit(solution)/shard_map/ppermute | solution.py:273
  9.8 54.0 %copy-start.4 = (bf16[160,1024]{1,0:T(8,128)(2,1)}, bf16[160,1024]{1,0:T(8,128)(2,1)S(1)}, u32[]{:S(2)}) copy-start(bf16[160,1024]{1,0:T(8,128)(2,1)S(1)} %pad_maximum_fusion.refs_4_) | copy-start | bytes 983044
  31.2 47.5 %copy-start = (bf16[128,2560]{1,0:T(8,128)(2,1)S(1)}, bf16[128,2560]{1,0:T(8,128)(2,1)}, u32[]{:S(2)}) copy-start(bf16[128,2560]{1,0:T(8,128)(2,1)} %acts.5) | copy-start | bytes 1966084
  31.2 47.5 %copy-start.2 = (bf16[128,1024]{1,0:T(8,128)(2,1)S(1)}, bf16[128,1024]{1,0:T(8,128)(2,1)}, u32[]{:S(2)}) copy-start(bf16[128,1024]{1,0:T(8,128)(2,1)} %hidden.5) | copy-start | bytes 786436
  31.2 47.5 %copy-start.3 = (s32[5]{0:T(128)S(1)}, s32[5]{0:T(128)}, u32[]{:S(2)}) copy-start(s32[5]{0:T(128)} %stack.19.place) | copy-start | bytes 64
  32.0 19.6 %all-to-all-start.1 = ((f32[8,80,128]{2,1,0:T(8,128)}), f32[8,80,128]{2,1,0:T(8,128)S(1)}, u32[]{:S(2)}, u32[]{:S(2)}) async-start(f32[8,80,128]{2,1,0:T(8,128)} %broadcast_in_dim.8), calls=%async_computation.1 | async-start | bytes 655360 | tf_op jit(solution)/shard_map/all_to_all | solution.py:292
  40.6 9.2 %collective-permute-start.4 = (bf16[128,1024]{1,0:T(8,128)(2,1)S(1)}, bf16[128,1024]{1,0:T(8,128)(2,1)S(1)}, u32[]{:S(2)}, u32[]{:S(2)}) collective-permute-start(bf16[128,1024]{1,0:T(8,128)(2,1)S(1)} %copy-done.1), channel_id=1, source_target_pairs={{0,48},{8,56},{16,0},{24,8},{32,16},{40,24},{48,32},{56,40},{64,11... | collective-permute-start | bytes 786440 | tf_op jit(solution)/shard_map/ppermute | solution.py:398
  41.5 16.0 %collective-permute-start.7 = (bf16[160,1024]{1,0:T(8,128)(2,1)S(1)}, bf16[160,1024]{1,0:T(8,128)(2,1)S(1)}, u32[]{:S(2)}, u32[]{:S(2)}) collective-permute-start(bf16[160,1024]{1,0:T(8,128)(2,1)S(1)} %pad_maximum_fusion.refs_4_), channel_id=1, source_target_pairs={{0,192},{8,200},{16,208},{24,216},{32,224},{40,232},{48,240},{56,2... | collective-permute-start | bytes 983048 | tf_op jit(solution)/shard_map/ppermute | solution.py:398
  42.7 14.8 %collective-permute-start.6 = (bf16[160,1024]{1,0:T(8,128)(2,1)S(1)}, bf16[160,1024]{1,0:T(8,128)(2,1)S(1)}, u32[]{:S(2)}, u32[]{:S(2)}) collective-permute-start(bf16[160,1024]{1,0:T(8,128)(2,1)S(1)} %pad_maximum_fusion.refs_4_), channel_id=1, source_target_pairs={{0,128},{8,136},{16,144},{24,152},{32,160},{40,168},{48,176},{56,1... | collective-permute-start | bytes 983048 | tf_op jit(solution)/shard_map/ppermute | solution.py:398
  44.1 14.2 %collective-permute-start.5 = (bf16[160,1024]{1,0:T(8,128)(2,1)S(1)}, bf16[160,1024]{1,0:T(8,128)(2,1)S(1)}, u32[]{:S(2)}, u32[]{:S(2)}) collective-permute-start(bf16[160,1024]{1,0:T(8,128)(2,1)S(1)} %pad_maximum_fusion.refs_4_), channel_id=1, source_target_pairs={{0,64},{8,72},{16,80},{24,88},{32,96},{40,104},{48,112},{56,120},{... | collective-permute-start | bytes 983048 | tf_op jit(solution)/shard_map/ppermute | solution.py:398
  44.2 10.1 %collective-permute-start.3 = (bf16[128,1024]{1,0:T(8,128)(2,1)S(1)}, bf16[128,1024]{1,0:T(8,128)(2,1)S(1)}, u32[]{:S(2)}, u32[]{:S(2)}) collective-permute-start(bf16[128,1024]{1,0:T(8,128)(2,1)S(1)} %copy-done.1), channel_id=1, source_target_pairs={{0,32},{8,40},{16,48},{24,56},{32,0},{40,8},{48,16},{56,24},{64,96... | collective-permute-start | bytes 786440 | tf_op jit(solution)/shard_map/ppermute | solution.py:398
  49.8 14.0 %copy-start.8 = (bf16[128,1024]{1,0:T(8,128)(2,1)}, bf16[128,1024]{1,0:T(8,128)(2,1)S(1)}, u32[]{:S(2)}) copy-start(bf16[128,1024]{1,0:T(8,128)(2,1)S(1)} %collective-permute-done.4.refs_3_) | copy-start | bytes 786436
  49.8 7.7 %collective-permute-start.2 = (bf16[128,1024]{1,0:T(8,128)(2,1)S(1)}, bf16[128,1024]{1,0:T(8,128)(2,1)}, u32[]{:S(2)}, u32[]{:S(2)}) collective-permute-start(bf16[128,1024]{1,0:T(8,128)(2,1)S(1)} %copy-done.1), channel_id=1, source_target_pairs={{0,16},{8,24},{16,32},{24,40},{32,48},{40,56},{48,0},{56,8},{64,80... | collective-permute-start | bytes 786440 | tf_op jit(solution)/shard_map/ppermute | solution.py:398
  54.3 9.5 %copy-start.9 = (bf16[128,1024]{1,0:T(8,128)(2,1)}, bf16[128,1024]{1,0:T(8,128)(2,1)S(1)}, u32[]{:S(2)}) copy-start(bf16[128,1024]{1,0:T(8,128)(2,1)S(1)} %collective-permute-done.3.refs_2_) | copy-start | bytes 786436
  57.5 6.3 %copy-start.5 = (bf16[160,1024]{1,0:T(8,128)(2,1)}, bf16[160,1024]{1,0:T(8,128)(2,1)S(1)}, u32[]{:S(2)}) copy-start(bf16[160,1024]{1,0:T(8,128)(2,1)S(1)} %collective-permute-done.7.refs_7_) | copy-start | bytes 983044
  57.5 6.3 %copy-start.6 = (bf16[160,1024]{1,0:T(8,128)(2,1)}, bf16[160,1024]{1,0:T(8,128)(2,1)S(1)}, u32[]{:S(2)}) copy-start(bf16[160,1024]{1,0:T(8,128)(2,1)S(1)} %collective-permute-done.6.refs_6_) | copy-start | bytes 983044
  58.4 5.5 %copy-start.7 = (bf16[160,1024]{1,0:T(8,128)(2,1)}, bf16[160,1024]{1,0:T(8,128)(2,1)S(1)}, u32[]{:S(2)}) copy-start(bf16[160,1024]{1,0:T(8,128)(2,1)S(1)} %collective-permute-done.5.refs_5_) | copy-start | bytes 983044
  59.3 16.6 %all-to-all-start.2 = ((f32[16,80,128]{2,1,0:T(8,128)}), f32[16,80,128]{2,1,0:T(8,128)S(1)}, u32[]{:S(2)}, u32[]{:S(2)}) async-start(f32[16,80,128]{2,1,0:T(8,128)} %broadcast_in_dim.9), calls=%async_computation.2 | async-start | bytes 1310720 | tf_op jit(solution)/shard_map/all_to_all | solution.py:286
  75.9 2.8 %collective-permute-start.8 = (f32[1280,128]{1,0:T(8,128)S(1)}, f32[1280,128]{1,0:T(8,128)S(1)}, u32[]{:S(2)}, u32[]{:S(2)}) collective-permute-start(f32[1280,128]{1,0:T(8,128)S(1)} %bitcast.31), channel_id=1, source_target_pairs={{0,8},{8,0},{16,24},{24,16},{32,40},{40,32},{48,56},{56,48},{64,72... | collective-permute-start | bytes 1966088 | tf_op jit(solution)/shard_map/ppermute | solution.py:273
  78.1 17.5 %collective-permute-start.9 = (f32[4,320,128]{2,1,0:T(8,128)}, f32[4,320,128]{2,1,0:T(8,128)}, u32[]{:S(2)}, u32[]{:S(2)}) collective-permute-start(f32[4,320,128]{2,1,0:T(8,128)} %get-tuple-element.62), channel_id=1, source_target_pairs={{0,1},{1,0},{2,3},{3,2},{4,5},{5,4},{6,7},{7,6},{8,9},{9,8},{10,11... | collective-permute-start | bytes 1966088 | tf_op jit(solution)/shard_map/ppermute | solution.py:409
  84.9 14.4 %collective-permute-start.10 = (f32[512,128]{1,0:T(8,128)S(1)}, f32[512,128]{1,0:T(8,128)}, u32[]{:S(2)}, u32[]{:S(2)}) collective-permute-start(f32[512,128]{1,0:T(8,128)S(1)} %get-tuple-element.52), channel_id=1, source_target_pairs={{0,8},{8,0},{16,24},{24,16},{32,40},{40,32},{48,56},{56,48},{64,72... | collective-permute-start | bytes 786440 | tf_op jit(solution)/shard_map/ppermute | solution.py:273
  96.8 20.6 %collective-permute-start.11 = (f32[2,320,128]{2,1,0:T(8,128)S(1)}, f32[2,320,128]{2,1,0:T(8,128)}, u32[]{:S(2)}, u32[]{:S(2)}) collective-permute-start(f32[2,320,128]{2,1,0:T(8,128)S(1)} %get-tuple-element.64), channel_id=1, source_target_pairs={{0,2},{1,3},{2,0},{3,1},{4,6},{5,7},{6,4},{7,5},{8,10},{9,11},{10,... | collective-permute-start | bytes 983048 | tf_op jit(solution)/shard_map/ppermute | solution.py:409
  101.0 12.2 %all-to-all-start.3 = ((f32[16,32,128]{2,1,0:T(8,128)}), f32[16,32,128]{2,1,0:T(8,128)S(1)}, u32[]{:S(2)}, u32[]{:S(2)}) async-start(f32[16,32,128]{2,1,0:T(8,128)} %bitcast.12), calls=%async_computation.3 | async-start | bytes 524288 | tf_op jit(solution)/shard_map/all_to_all | solution.py:277
  113.9 12.2 %all-to-all-start.4 = ((f32[16,32,128]{2,1,0:T(8,128)}), f32[16,32,128]{2,1,0:T(8,128)S(1)}, u32[]{:S(2)}, u32[]{:S(2)}) async-start(f32[16,32,128]{2,1,0:T(8,128)} %broadcast_in_dim.10), calls=%async_computation.4 | async-start | bytes 524288 | tf_op jit(solution)/shard_map/all_to_all | solution.py:286
  118.5 11.9 %collective-permute-start.12 = (f32[320,128]{1,0:T(8,128)S(1)}, f32[320,128]{1,0:T(8,128)S(1)}, u32[]{:S(2)}, u32[]{:S(2)}) collective-permute-start(f32[320,128]{1,0:T(8,128)S(1)} %get-tuple-element.66), channel_id=1, source_target_pairs={{0,4},{1,5},{2,6},{3,7},{4,0},{5,1},{6,2},{7,3},{8,12},{9,13},{10,... | collective-permute-start | bytes 491528 | tf_op jit(solution)/shard_map/ppermute | solution.py:409
  126.1 10.9 %collective-permute-start.15 = (f32[512,128]{1,0:T(8,128)S(1)}, f32[512,128]{1,0:T(8,128)S(1)}, u32[]{:S(2)}, u32[]{:S(2)}) collective-permute-start(f32[512,128]{1,0:T(8,128)S(1)} %bitcast.34), channel_id=1, source_target_pairs={{0,8},{8,0},{16,24},{24,16},{32,40},{40,32},{48,56},{56,48},{64,72... | collective-permute-start | bytes 786440 | tf_op jit(solution)/shard_map/ppermute | solution.py:273
  130.5 15.5 %collective-permute-start.14 = (bf16[160,128]{1,0:T(8,128)(2,1)S(1)}, bf16[160,128]{1,0:T(8,128)(2,1)S(1)}, u32[]{:S(2)}, u32[]{:S(2)}) collective-permute-start(bf16[160,128]{1,0:T(8,128)(2,1)S(1)} %get-tuple-element.68), channel_id=1, source_target_pairs={{0,16},{1,48},{2,18},{3,50},{4,20},{5,52},{6,22},{7,54},{8,24},{9,... | collective-permute-start | bytes 122888 | tf_op jit(solution)/shard_map/ppermute | solution.py:426
  132.8 13.2 %collective-permute-start.13 = (bf16[160,128]{1,0:T(8,128)(2,1)S(1)}, bf16[160,128]{1,0:T(8,128)(2,1)S(1)}, u32[]{:S(2)}, u32[]{:S(2)}) collective-permute-start(bf16[160,128]{1,0:T(8,128)(2,1)S(1)} %get-tuple-element.69), channel_id=1, source_target_pairs={{0,0},{1,32},{2,2},{3,34},{4,4},{5,36},{6,6},{7,38},{8,8},{9,40},{... | collective-permute-start | bytes 122888 | tf_op jit(solution)/shard_map/ppermute | solution.py:426

commit v5 on v3

--- a/solution.py
+++ b/solution.py
@@ -272,13 +272,13 @@
 def swapped(x, replicas):
     return lax.ppermute(x, "dp", [(i, i ^ 1) for i in range(replicas)])
 
-def scatter_sum(mine, theirs, replicas):
-    x = mine + swapped(theirs, replicas)
+def scatter_sum(x, replicas):
     chips = replicas // CORES
     pieces = lax.all_to_all(
         x.reshape(chips, x.shape[0] // chips, -1), "dp", 0, 0, axis_index_groups=chips_of(replicas)
     )
     return jnp.sum(pieces, axis=0)
+
 
 def gather_rows(x, replicas):
     chips = replicas // CORES
@@ -344,9 +344,9 @@
         name="inverse_factor",
     )(gram_matrix)
 
-def input_gradient(grad_hidden, up_weight):
-    partial_input = dot(grad_hidden, lax.all_gather(up_weight, "dp", axis=0, tiled=True), ((1,), (1,)))
-    return lax.psum_scatter(partial_input, "mp", scatter_dimension=1, tiled=True)
+def after(x, earlier):
+    return lax.optimization_barrier((x, earlier))[0]
+
 
 def local(activations, grad_hidden, up_weight, error_feedback, query_previous):
     replicas = lax.axis_size("dp")
@@ -354,12 +354,16 @@
     replica = lax.axis_index("dp")
     place = jnp.stack([replica % CORES, replica, jnp.int32(replicas)])
     mine, theirs = project_part(place, activations, grad_hidden, error, query_previous)
-    own = gather_rows(sum_over_mp(scatter_sum(mine, theirs, replicas)), replicas)
+    mine = mine + swapped(theirs, replicas)
+    own = gather_rows(sum_over_mp(scatter_sum(mine, replicas)), replicas)
     other = swapped(own, replicas)
-    grad_input = input_gradient(grad_hidden, up_weight)
     mine, theirs, gram_matrix = query_part(place, activations, grad_hidden, error, own, other)
     inverse = inverse_factor(gram_matrix)
-    query_own = gather_rows(scatter_sum(mine, theirs, replicas), replicas)
+    weight = lax.all_gather(up_weight, "dp", axis=0, tiled=True)
+    partial_input = dot(after(grad_hidden, gram_matrix), weight, ((1,), (1,)))
+    mine = after(mine + swapped(theirs, replicas), partial_input[0, 0])
+    grad_input = lax.psum_scatter(partial_input, "mp", scatter_dimension=1, tiled=True)
+    query_own = gather_rows(scatter_sum(mine, replicas), replicas)
     query_own, inverse = lax.optimization_barrier((query_own, inverse))
     query_other = swapped(query_own, replicas)
     error_next, update, query_next = residual(

time: 136 us -> 137 us (level)
  blocking collectives: 56.3 us -> 70.2 us
  waiting for transfers between devices: 21.5 us -> 12.5 us
  starting transfers between devices: 7.97 us -> 3.93 us
    all_to_all x0 -> x1, blocking collectives: none -> 16 us  [gather_rows(): lax.all_to_all(spread, 'dp', 0, 0, axis_index_groups=chips_of(replicas))]
    all_gather x1, waiting for transfers between devices: 9.42 us -> 0.02 us  [local(): weight = lax.all_gather(up_weight, 'dp', axis=0, tiled=True)]
    all_to_all x2 -> x1, starting transfers between devices: 7.13 us -> 3.53 us  [gather_rows(): lax.all_to_all(spread, 'dp', 0, 0, axis_index_groups=chips_of(replicas))]
    all_to_all x2, blocking collectives: 35.9 us -> 34.1 us  [scatter_sum(): lax.all_to_all(x.reshape(chips, x.shape[0] // chips, -1), 'dp', 0, 0, axi...]
    all_to_all x2 -> x1, waiting for transfers between devices: 4.41 us -> 4.41 us  [gather_rows(): lax.all_to_all(spread, 'dp', 0, 0, axis_index_groups=chips_of(replicas))]
  transfers between devices with their start and end apart: 8 -> 7, of which waited for: 6 -> 5; matrix products, arithmetic and copies ran while one was open for 6% -> 2% of each run, Pallas kernels for 18% -> 18%
where the time goes in v5:
time: 137 us; the launch traced here: 135 us
  blocking collectives  70.2 us (51%)
  Pallas kernels  25 us (18%)
  between operations  14.2 us (10%)
  waiting for transfers between devices  12.5 us (9%)
  matrix products  5.12 us (4%)
  starting transfers between devices  3.93 us (3%)
  other arithmetic  3.41 us (2%)
    all_to_all x2, blocking collectives, scatter_sum(): lax.all_to_all(x.reshape(chips, x.shape[0] // chips, -1), 'dp', 0, 0, axi...  34.1 us
    all_to_all x1, blocking collectives, sum_over_mp(): return jnp.sum(lax.all_to_all(spread, 'mp', 0, 0), axis=0)  20.1 us
    all_to_all x1, blocking collectives, gather_rows(): lax.all_to_all(spread, 'dp', 0, 0, axis_index_groups=chips_of(replicas))  16 us
    pallas_call x1, Pallas kernels, residual(): pl.pallas_call(residual_kernel, grid=(1,), in_specs=[SCALARS, HBM, HBM, H...  8.76 us
    ppermute x4, waiting for transfers between devices, swapped(): return lax.ppermute(x, 'dp', [(i, i ^ 1) for i in range(replicas)])  7.33 us
    pallas_call x1, Pallas kernels, query_part(): pl.pallas_call(query_kernel, grid=(1,), in_specs=[SCALARS, HBM, HBM, HBM,...  6.09 us
    pallas_call x1, Pallas kernels, project_part(): pl.pallas_call(project_kernel, grid=(1,), in_specs=[SCALARS, HBM, HBM, HB...  5.87 us
    dot_general x1, matrix products, dot(): return lax.dot_general(a, b, (dims, ((), ())), preferred_element_type=F32)  5.12 us
  transfers between devices with their start and end apart: 7, of which 5 were waited for; matrix products, arithmetic and copies ran while one was open for 2% of the time, Pallas kernels for 18%

profile of v5, /device:TPU:32, one launch (start us, length us, event | category | flops | bytes accessed | tf_op | source)
XLA Modules:
  0.0 135.1 jit_solution(13394431986883416036)
XLA Ops:
  7.2 0.0 all-gather.2.cloned.1.call-start
  7.2 0.7 all-gather.2.cloned.1.call-update
  7.9 0.0 reduce-scatter.2.cloned.1.call-start
  8.0 0.6 pad_add_fusion.place
  8.5 5.9 %project_part.1 = (f32[1280,128]{1,0:T(8,128)}, f32[1280,128]{1,0:T(8,128)}) custom-call(s32[3]{0:T(128)} %pad_add_fusion.place, bf16[128,2560]{1,0:T(8,128)(2,1)} %acts.5, bf16[128,1024]{1,0:T(8,128)(2,1)} %hidden.5, bf16[2560,1024]{1,0:T(8,128)(2,1)} %bitcast.15, f32[1024,128]{1,0:T(8,128)} %query.1), custom_call_target="tpu_custom_call" | custom-call | flops 1342177280 | bytes 5242880 | tf_op jit(solution)/shard_map/project_part/pallas_call | solution.py:96
  14.4 0.0 copy-start
  14.4 0.0 copy-start.1
  14.4 0.0 copy-start.2
  14.5 0.1 collective-permute-start
  14.6 2.3 %collective-permute-done = f32[1280,128]{1,0:T(8,128)S(1)} collective-permute-done((f32[1280,128]{1,0:T(8,128)}, f32[1280,128]{1,0:T(8,128)S(1)}, u32[]{:S(2)}, u32[]{:S(2)}) %collective-permute-start) | collective-permute-done | bytes 655392 | tf_op jit(solution)/shard_map/ppermute | solution.py:273
  16.9 1.2 add.13
  18.0 21.9 %all_to_all.25 = f32[16,80,128]{2,1,0:T(8,128)S(1)} all-to-all(f32[16,80,128]{2,1,0:T(8,128)S(1)} %bitcast.18), channel_id=1, replica_groups={{0,16,32,48,64,80,96,112,128,144,160,176,192,208,224,240},{8,24,40,56,7..., dimensions={0} | all-to-all | bytes 1310720 | tf_op jit(solution)/shard_map/all_to_all | solution.py:277
  39.9 20.1 %all_to_all.26 = f32[8,80,128]{2,1,0:T(8,128)S(1)} all-to-all(f32[8,80,128]{2,1,0:T(8,128)S(1)} %broadcast_in_dim.8), channel_id=1, replica_groups=mesh['dp'=32,'mp'=8] {'mp'}, dimensions={0} | all-to-all | bytes 655360 | tf_op jit(solution)/shard_map/all_to_all | solution.py:292
  60.1 16.0 %all_to_all.27 = f32[16,80,128]{2,1,0:T(8,128)S(1)} all-to-all(f32[16,80,128]{2,1,0:T(8,128)S(1)} %broadcast_in_dim.9), channel_id=1, replica_groups={{0,16,32,48,64,80,96,112,128,144,160,176,192,208,224,240},{8,24,40,56,7..., dimensions={0} | all-to-all | bytes 1310720 | tf_op jit(solution)/shard_map/all_to_all | solution.py:286
  76.1 0.0 collective-permute-start.1
  76.1 2.1 %collective-permute-done.1.other = f32[1280,128]{1,0:T(8,128)S(1)} collective-permute-done((f32[1280,128]{1,0:T(8,128)S(1)}, f32[1280,128]{1,0:T(8,128)S(1)}, u32[]{:S(2)}, u32[]{:S(2)}) %collective-permute-start.1) | collective-permute-done | bytes 655392 | tf_op jit(solution)/shard_map/ppermute | solution.py:273
  78.2 6.1 %query_part.1 = (f32[512,128]{1,0:T(8,128)S(1)}, f32[512,128]{1,0:T(8,128)S(1)}, f32[128,128]{1,0:T(8,128)S(1)}) custom-call(s32[3]{0:T(128)S(1)} %copy-done.2, bf16[128,2560]{1,0:T(8,128)(2,1)S(1)} %copy-done.1, bf16[128,1024]{1,0:T(8,128)(2,1)S(1)} %copy-done, bf16[2560,1024]{1,0:T(8,128)(2,1)} %bitcast.16, f32[1280,128]{1,0:T(8,128)S(1)} %bitcast.11, ...), custom_call_target="tpu_custom_call" | custom-call | flops 1342177280 | bytes 5242880 | tf_op jit(solution)/shard_map/query_part/pallas_call | solution.py:153
  84.3 0.0 all-gather.2.cloned.1.call-done
  84.3 5.1 %fusion = f32[128,2560]{0,1:T(8,128)} fusion(bf16[128,1024]{1,0:T(8,128)(2,1)S(1)} %copy-done, bf16[2560,1024]{1,0:T(8,128)(2,1)} %all-gather.2.cloned.1.call-done), kind=kOutput, calls=%fused_computation.1 | convolution fusion | flops 671088640 | bytes 6815744 | tf_op jit(solution)/shard_map/dot_general | solution.py:18
  89.5 0.0 reduce-scatter.2.cloned.1.call-update
  89.5 0.2 collective-permute-start.2
  89.7 1.4 %collective-permute-done.2 = f32[512,128]{1,0:T(8,128)S(1)} collective-permute-done((f32[512,128]{1,0:T(8,128)S(1)}, f32[512,128]{1,0:T(8,128)S(1)}, u32[]{:S(2)}, u32[]{:S(2)}) %collective-permute-start.2) | collective-permute-done | bytes 262176 | tf_op jit(solution)/shard_map/ppermute | solution.py:273
  91.1 12.3 %all_to_all.28 = f32[16,32,128]{2,1,0:T(8,128)S(1)} all-to-all(f32[16,32,128]{2,1,0:T(8,128)S(1)} %bitcast.19), channel_id=1, replica_groups={{0,16,32,48,64,80,96,112,128,144,160,176,192,208,224,240},{8,24,40,56,7..., dimensions={0} | all-to-all | bytes 524288 | tf_op jit(solution)/shard_map/all_to_all | solution.py:277
  103.4 0.7 broadcast_in_dim.10
  104.2 3.5 %all-to-all-start.4 = ((f32[16,32,128]{2,1,0:T(8,128)}), f32[16,32,128]{2,1,0:T(8,128)S(1)}, u32[]{:S(2)}, u32[]{:S(2)}) async-start(f32[16,32,128]{2,1,0:T(8,128)} %broadcast_in_dim.10), calls=%async_computation.5 | async-start | bytes 524288 | tf_op jit(solution)/shard_map/all_to_all | solution.py:286
  107.7 4.2 %inverse_factor.1.inverse = f32[128,128]{1,0:T(8,128)S(1)} custom-call(f32[128,128]{1,0:T(8,128)S(1)} %get-tuple-element.19.gram), custom_call_target="tpu_custom_call" | custom-call | flops 2000000000 | bytes 10000000 | tf_op jit(solution)/shard_map/inverse_factor/pallas_call | solution.py:335
  111.9 4.4 %all-to-all-done.4 = f32[16,32,128]{2,1,0:T(8,128)S(1)} async-done(((f32[16,32,128]{2,1,0:T(8,128)}), f32[16,32,128]{2,1,0:T(8,128)S(1)}, u32[]{:S(2)}, u32[]{:S(2)}) %all-to-all-start.4) | async-done | bytes 262176 | tf_op jit(solution)/shard_map/all_to_all | solution.py:286
  116.4 0.0 collective-permute-start.3
  116.4 1.5 %collective-permute-done.3.query_other = f32[512,128]{1,0:T(8,128)S(1)} collective-permute-done((f32[512,128]{1,0:T(8,128)S(1)}, f32[512,128]{1,0:T(8,128)S(1)}, u32[]{:S(2)}, u32[]{:S(2)}) %collective-permute-start.3) | collective-permute-done | bytes 262176 | tf_op jit(solution)/shard_map/ppermute | solution.py:273
  117.9 8.8 %residual.1 = (bf16[2560,1024]{1,0:T(8,128)(2,1)}, f32[80,1024]{1,0:T(8,128)}, f32[1024,128]{1,0:T(8,128)}) custom-call(s32[3]{0:T(128)S(1)} %copy-done.2, bf16[128,2560]{1,0:T(8,128)(2,1)S(1)} %copy-done.1, bf16[128,1024]{1,0:T(8,128)(2,1)S(1)} %copy-done, bf16[2560,1024]{1,0:T(8,128)(2,1)} %bitcast.17, f32[1280,128]{1,0:T(8,128)S(1)} %bitcast.12, ...), custom_call_target="tpu_custom_call" | custom-call | flops 2684354560 | bytes 10485760 | tf_op jit(solution)/shard_map/residual/pallas_call | solution.py:238
  126.7 0.0 reduce-scatter.2.cloned.1.call-done
  126.7 1.6 %convert_element_type.3 = bf16[128,320]{0,1:T(8,128)(2,1)} convert(f32[128,320]{0,1:T(8,128)} %reduce-scatter.2.cloned.1.call-done) | non-fusion elementwise | flops 40960 | bytes 245760 | tf_op jit(solution)/shard_map/convert_element_type | solution.py:374
  (9 shorter events, 0.2 us)
Async XLA Ops:
  7.2 77.2 %all-gather.2.cloned.1.call-start = ((), (), s32[]{:S(2)}) async-start(), calls=%async_computation.6 | async-start | bytes 5406720 | tf_op jit(solution)/shard_map/all_gather | solution.py:362
  7.9 118.8 %reduce-scatter.2.cloned.1.call-start = ((), (), s32[]{:S(2)}) async-start(), calls=%async_computation.7 | async-start | bytes 1474560 | tf_op jit(solution)/shard_map/reduce_scatter | solution.py:365
  14.4 63.8 %copy-start = (bf16[128,1024]{1,0:T(8,128)(2,1)S(1)}, bf16[128,1024]{1,0:T(8,128)(2,1)}, u32[]{:S(2)}) copy-start(bf16[128,1024]{1,0:T(8,128)(2,1)} %hidden.5) | copy-start | bytes 786436
  14.4 63.8 %copy-start.1 = (bf16[128,2560]{1,0:T(8,128)(2,1)S(1)}, bf16[128,2560]{1,0:T(8,128)(2,1)}, u32[]{:S(2)}) copy-start(bf16[128,2560]{1,0:T(8,128)(2,1)} %acts.5) | copy-start | bytes 1966084
  14.4 63.8 %copy-start.2 = (s32[3]{0:T(128)S(1)}, s32[3]{0:T(128)}, u32[]{:S(2)}) copy-start(s32[3]{0:T(128)} %pad_add_fusion.place) | copy-start | bytes 40
  14.5 2.4 %collective-permute-start = (f32[1280,128]{1,0:T(8,128)}, f32[1280,128]{1,0:T(8,128)S(1)}, u32[]{:S(2)}, u32[]{:S(2)}) collective-permute-start(f32[1280,128]{1,0:T(8,128)} %get-tuple-element.18), channel_id=1, source_target_pairs={{0,8},{8,0},{16,24},{24,16},{32,40},{40,32},{48,56},{56,48},{64,72... | collective-permute-start | bytes 1966088 | tf_op jit(solution)/shard_map/ppermute | solution.py:273
  76.1 2.1 %collective-permute-start.1 = (f32[1280,128]{1,0:T(8,128)S(1)}, f32[1280,128]{1,0:T(8,128)S(1)}, u32[]{:S(2)}, u32[]{:S(2)}) collective-permute-start(f32[1280,128]{1,0:T(8,128)S(1)} %bitcast.10), channel_id=1, source_target_pairs={{0,8},{8,0},{16,24},{24,16},{32,40},{40,32},{48,56},{56,48},{64,72... | collective-permute-start | bytes 1966088 | tf_op jit(solution)/shard_map/ppermute | solution.py:273
  89.5 1.6 %collective-permute-start.2 = (f32[512,128]{1,0:T(8,128)S(1)}, f32[512,128]{1,0:T(8,128)S(1)}, u32[]{:S(2)}, u32[]{:S(2)}) collective-permute-start(f32[512,128]{1,0:T(8,128)S(1)} %get-tuple-element.22), channel_id=1, source_target_pairs={{0,8},{8,0},{16,24},{24,16},{32,40},{40,32},{48,56},{56,48},{64,72... | collective-permute-start | bytes 786440 | tf_op jit(solution)/shard_map/ppermute | solution.py:273
  104.2 12.2 %all-to-all-start.4 = ((f32[16,32,128]{2,1,0:T(8,128)}), f32[16,32,128]{2,1,0:T(8,128)S(1)}, u32[]{:S(2)}, u32[]{:S(2)}) async-start(f32[16,32,128]{2,1,0:T(8,128)} %broadcast_in_dim.10), calls=%async_computation.5 | async-start | bytes 524288 | tf_op jit(solution)/shard_map/all_to_all | solution.py:286
  116.4 1.5 %collective-permute-start.3 = (f32[512,128]{1,0:T(8,128)S(1)}, f32[512,128]{1,0:T(8,128)S(1)}, u32[]{:S(2)}, u32[]{:S(2)}) collective-permute-start(f32[512,128]{1,0:T(8,128)S(1)} %bitcast.13), channel_id=1, source_target_pairs={{0,8},{8,0},{16,24},{24,16},{32,40},{40,32},{48,56},{56,48},{64,72... | collective-permute-start | bytes 786440 | tf_op jit(solution)/shard_map/ppermute | solution.py:273
Sparse Core Ops, SparseCore 0:
  10.5 64.2 all-gather.1
  89.6 36.5 reduce-scatter.1

commit v6 on v5

--- a/solution.py
+++ b/solution.py
@@ -11,6 +11,7 @@
 F32 = jnp.float32
 BF16 = jnp.bfloat16
 BLOCK = 640
+HALF = 1280
 CORES = 2
 VMEM_LIMIT = 48 << 20
 
@@ -31,37 +32,37 @@
     copy.start()
     return copy
 
-def row_of(step, core, rows):
+def row_of(step, core, rows, block):
     half = rows // CORES
-    steps = half // BLOCK
+    steps = half // block
     own = jnp.where(step < steps, core, 1 - core)
-    return pl.multiple_of(own * half + lax.rem(step, steps) * BLOCK, BLOCK)
+    return pl.multiple_of(own * half + lax.rem(step, steps) * block, block)
 
 def start_rows(core, error, error_rows, sems):
-    rows = error.shape[0]
+    rows, (steps, block, _) = error.shape[0], error_rows.shape
 
     def start(step, carry):
-        load(error.at[pl.ds(row_of(step, core, rows), BLOCK)], error_rows.at[step], sems.at[step])
+        load(error.at[pl.ds(row_of(step, core, rows, block), block)], error_rows.at[step], sems.at[step])
         return carry
 
-    lax.fori_loop(0, rows // BLOCK, start, 0)
+    lax.fori_loop(0, steps, start, 0)
 
 def wait_rows(step, error, error_rows, sems):
-    pltpu.make_async_copy(error.at[pl.ds(0, BLOCK)], error_rows.at[step], sems.at[step]).wait()
-
-def halves(core, rows, body, first, second):
-    steps = rows // CORES // BLOCK
+    pltpu.make_async_copy(error.at[pl.ds(0, error_rows.shape[1])], error_rows.at[step], sems.at[step]).wait()
+
+def halves(core, rows, block, body, first, second):
+    steps = rows // CORES // block
     for base, ref in ((0, first), (steps, second)):
 
         def step_of(i, carry, base=base, ref=ref):
-            body(base + i, row_of(base + i, core, rows), pl.multiple_of(i * BLOCK, BLOCK), ref)
+            body(base + i, row_of(base + i, core, rows, block), pl.multiple_of(i * block, block), ref)
             return carry
 
         lax.fori_loop(0, steps, step_of, 0)
 
-def project_kernel(place, acts, hidden, error, query, mine, theirs,
+def project_kernel(acts, hidden, error, query, mine, theirs,
                    acts_in, hidden_in, query_in, error_rows, query_pair, token_pair, small, sems):
-    core = place[0]
+    core = lax.rem(lax.axis_index("dp"), CORES)
     copies = [
         load(query, query_in, small.at[0]),
         load(hidden, hidden_in, small.at[1]),
@@ -81,22 +82,21 @@
         total += dot(acts_in[:, pl.ds(row, BLOCK)], token_pair[...], ((0,), (0,)))
         ref[pl.ds(at, BLOCK), :] = folded(total)
 
-    halves(core, error.shape[0], body, mine, theirs)
+    halves(core, error.shape[0], BLOCK, body, mine, theirs)
 
 HBM = pl.BlockSpec(memory_space=pltpu.HBM)
-SCALARS = pl.BlockSpec(memory_space=pltpu.SMEM)
 
 def whole(shape):
     return pl.BlockSpec(shape, lambda i: (0,) * len(shape))
 
-def project_part(place, acts, hidden, error, query):
+def project_part(acts, hidden, error, query):
     tokens, rows = acts.shape
     columns, rank = query.shape
     half = (rows // CORES, rank)
     return pl.pallas_call(
         project_kernel,
         grid=(1,),
-        in_specs=[SCALARS, HBM, HBM, HBM, HBM],
+        in_specs=[HBM, HBM, HBM, HBM],
         out_specs=(whole(half), whole(half)),
         out_shape=(jax.ShapeDtypeStruct(half, F32),) * 2,
         scratch_shapes=[
@@ -114,11 +114,11 @@
             flops=4 * rows * columns * rank, bytes_accessed=2 * rows * columns, transcendentals=0
         ),
         name="project_part",
-    )(place, acts, hidden, error, query)
-
-def query_kernel(place, acts, hidden, error, own, other, mine, theirs, gram,
+    )(acts, hidden, error, query)
+
+def query_kernel(acts, hidden, error, own, other, mine, theirs, gram,
                  acts_in, hidden_in, error_rows, total, tokens_sum, gram_sum, small, sems):
-    core = place[0]
+    core = lax.rem(lax.axis_index("dp"), CORES)
     rank = gram.shape[0]
     acts_copy = load(acts, acts_in, small.at[0])
     start_rows(core, error, error_rows, sems)
@@ -129,13 +129,13 @@
     acts_copy.wait()
 
     def body(step, row, at, ref):
-        split = pair(ref[pl.ds(at, BLOCK), :])
+        split = pair(ref[pl.ds(at, HALF), :])
         gram_sum[...] += dot(split, split, ((0,), (0,)))
-        tokens_sum[...] += dot(acts_in[:, pl.ds(row, BLOCK)], split, ((1,), (0,)))
+        tokens_sum[...] += dot(acts_in[:, pl.ds(row, HALF)], split, ((1,), (0,)))
         wait_rows(step, error, error_rows, sems)
         total[...] += dot(split, error_rows[step], ((0,), (0,)))
 
-    halves(core, error.shape[0], body, own, other)
+    halves(core, error.shape[0], HALF, body, own, other)
     hidden_copy.wait()
     spread = pair(folded(tokens_sum[...]))
     turned = total[...] + dot(spread, hidden_in[...], ((0,), (0,)))
@@ -145,7 +145,7 @@
     theirs[...] = total[:rank, pl.ds(pl.multiple_of((1 - core) * half, half), half)].T
     gram[...] = folded(gram_sum[:rank, :] + gram_sum[rank:, :])
 
-def query_part(place, acts, hidden, error, own, other):
+def query_part(acts, hidden, error, own, other):
     tokens, rows = acts.shape
     columns = hidden.shape[1]
     rank = own.shape[1]
@@ -153,7 +153,7 @@
     return pl.pallas_call(
         query_kernel,
         grid=(1,),
-        in_specs=[SCALARS, HBM, HBM, HBM, whole(own.shape), whole(own.shape)],
+        in_specs=[HBM, HBM, HBM, whole(own.shape), whole(own.shape)],
         out_specs=(whole(half), whole(half), whole((rank, rank))),
         out_shape=(
             jax.ShapeDtypeStruct(half, F32),
@@ -163,19 +163,19 @@
         scratch_shapes=[
             pltpu.VMEM((tokens, rows), BF16),
             pltpu.VMEM((tokens, columns), BF16),
-            pltpu.VMEM((rows // BLOCK, BLOCK, columns), BF16),
+            pltpu.VMEM((rows // HALF, HALF, columns), BF16),
             pltpu.VMEM((2 * rank, columns), F32),
             pltpu.VMEM((tokens, 2 * rank), F32),
             pltpu.VMEM((2 * rank, 2 * rank), F32),
             pltpu.SemaphoreType.DMA((2,)),
-            pltpu.SemaphoreType.DMA((rows // BLOCK,)),
+            pltpu.SemaphoreType.DMA((rows // HALF,)),
         ],
         compiler_params=pltpu.CompilerParams(vmem_limit_bytes=VMEM_LIMIT),
         cost_estimate=pl.CostEstimate(
             flops=4 * rows * columns * rank, bytes_accessed=2 * rows * columns, transcendentals=0
         ),
         name="query_part",
-    )(place, acts, hidden, error, own, other)
+    )(acts, hidden, error, own, other)
 
 def triple(x):
     split = pair(x)
@@ -186,17 +186,18 @@
     rest = (x - high.astype(F32)).astype(BF16)
     return jnp.concatenate([high, high, rest], axis=0)
 
-def residual_kernel(place, acts, hidden, error, own, other, inverse, query_own, query_other,
+def residual_kernel(acts, hidden, error, own, other, inverse, query_own, query_other,
                     out, update, query,
                     acts_in, hidden_in, error_rows, turn, factors, small, sems, sent):
-    core, replica, replicas = place[0], place[1], place[2]
+    replica = lax.axis_index("dp")
+    core = lax.rem(replica, CORES)
     rank = inverse.shape[0]
     rows = error.shape[0]
     acts_copy = load(acts, acts_in, small.at[0])
     hidden_copy = load(hidden, hidden_in, small.at[1])
     start_rows(core, error, error_rows, sems)
     turn[...] = stacked(inverse[...])
-    scale = 1.0 / replicas.astype(F32)
+    scale = 1.0 / lax.axis_size("dp")
     half = query_own.shape[0]
     for ref, first in ((query_own, core * half), (query_other, (1 - core) * half)):
         query[pl.ds(pl.multiple_of(first, half), half), :] = (
@@ -223,7 +224,7 @@
         error_rows[step] = (error_rows[step].astype(F32) - change).astype(BF16)
         load(error_rows.at[step], out.at[pl.ds(row, BLOCK)], sent.at[step])
 
-    halves(core, rows, body, own, other)
+    halves(core, rows, BLOCK, body, own, other)
 
     def drain(step, carry):
         pltpu.make_async_copy(error_rows.at[step], out.at[pl.ds(0, BLOCK)], sent.at[step]).wait()
@@ -231,7 +232,7 @@
 
     lax.fori_loop(0, rows // BLOCK, drain, 0)
 
-def residual(place, acts, hidden, error, own, other, inverse, query_own, query_other, share):
+def residual(acts, hidden, error, own, other, inverse, query_own, query_other, share):
     tokens, rows = acts.shape
     columns = hidden.shape[1]
     rank = inverse.shape[0]
@@ -239,7 +240,7 @@
         residual_kernel,
         grid=(1,),
         in_specs=[
-            SCALARS, HBM, HBM, HBM, whole(own.shape), whole(own.shape), whole(inverse.shape),
+            HBM, HBM, HBM, whole(own.shape), whole(own.shape), whole(inverse.shape),
             whole(query_own.shape), whole(query_own.shape),
         ],
         out_specs=(HBM, whole((share, columns)), whole((columns, rank))),
@@ -263,7 +264,7 @@
             flops=8 * rows * columns * rank, bytes_accessed=4 * rows * columns, transcendentals=0
         ),
         name="residual",
-    )(place, acts, hidden, error, own, other, inverse, query_own, query_other)
+    )(acts, hidden, error, own, other, inverse, query_own, query_other)
 
 
 def chips_of(replicas):
@@ -351,13 +352,11 @@
 def local(activations, grad_hidden, up_weight, error_feedback, query_previous):
     replicas = lax.axis_size("dp")
     error = error_feedback[0]
-    replica = lax.axis_index("dp")
-    place = jnp.stack([replica % CORES, replica, jnp.int32(replicas)])
-    mine, theirs = project_part(place, activations, grad_hidden, error, query_previous)
+    mine, theirs = project_part(activations, grad_hidden, error, query_previous)
     mine = mine + swapped(theirs, replicas)
     own = gather_rows(sum_over_mp(scatter_sum(mine, replicas)), replicas)
     other = swapped(own, replicas)
-    mine, theirs, gram_matrix = query_part(place, activations, grad_hidden, error, own, other)
+    mine, theirs, gram_matrix = query_part(activations, grad_hidden, error, own, other)
     inverse = inverse_factor(gram_matrix)
     weight = lax.all_gather(up_weight, "dp", axis=0, tiled=True)
     partial_input = dot(after(grad_hidden, gram_matrix), weight, ((1,), (1,)))
@@ -367,7 +366,7 @@
     query_own, inverse = lax.optimization_barrier((query_own, inverse))
     query_other = swapped(query_own, replicas)
     error_next, update, query_next = residual(
-        place, activations, grad_hidden, error, own, other, inverse, query_own, query_other,
+        activations, grad_hidden, error, own, other, inverse, query_own, query_other,
         error.shape[0] // replicas,
     )
     grad_input, error_next = lax.optimization_barrier((grad_input, error_next))

time: 137 us -> 135 us (0.985)
  Pallas kernels: 25 us -> 22.2 us
  blocking collectives: 70.2 us -> 71.7 us
    pallas_call x3, Pallas kernels: 20.7 us -> 17.9 us  [the longest x1 8.18 us: residual(): pl.pallas_call(residual_kernel, grid=(1,), in_specs=[HBM, HBM, HBM, whole...]
    all_to_all x1, blocking collectives: 16 us -> 17.6 us  [gather_rows(): lax.all_to_all(spread, 'dp', 0, 0, axis_index_groups=chips_of(replicas))]
  transfers between devices with their start and end apart: 7 -> 7, of which waited for: 5 -> 5; matrix products, arithmetic and copies ran while one was open for 2% -> 2% of each run, Pallas kernels for 18% -> 17%
where the time goes in v6:
time: 135 us; the launch traced here: 133 us
  blocking collectives  71.7 us (53%)
  Pallas kernels  22.2 us (16%)
  between operations  14.2 us (11%)
  waiting for transfers between devices  12.5 us (9%)
  matrix products  5.11 us (4%)
  starting transfers between devices  3.94 us (3%)
  other arithmetic  2.84 us (2%)
    all_to_all x2, blocking collectives, scatter_sum(): lax.all_to_all(x.reshape(chips, x.shape[0] // chips, -1), 'dp', 0, 0, axi...  34.6 us
    all_to_all x1, blocking collectives, sum_over_mp(): return jnp.sum(lax.all_to_all(spread, 'mp', 0, 0), axis=0)  19.5 us
    all_to_all x1, blocking collectives, gather_rows(): lax.all_to_all(spread, 'dp', 0, 0, axis_index_groups=chips_of(replicas))  17.6 us
    pallas_call x1, Pallas kernels, residual(): pl.pallas_call(residual_kernel, grid=(1,), in_specs=[HBM, HBM, HBM, whole...  8.18 us
    ppermute x4, waiting for transfers between devices, swapped(): return lax.ppermute(x, 'dp', [(i, i ^ 1) for i in range(replicas)])  7.32 us
    pallas_call x1, Pallas kernels, project_part(): pl.pallas_call(project_kernel, grid=(1,), in_specs=[HBM, HBM, HBM, HBM],...  5.21 us
    dot_general x1, matrix products, dot(): return lax.dot_general(a, b, (dims, ((), ())), preferred_element_type=F32)  5.11 us
    pallas_call x1, Pallas kernels, query_part(): pl.pallas_call(query_kernel, grid=(1,), in_specs=[HBM, HBM, HBM, whole(ow...  4.56 us
  transfers between devices with their start and end apart: 7, of which 5 were waited for; matrix products, arithmetic and copies ran while one was open for 2% of the time, Pallas kernels for 17%

profile of v6, /device:TPU:32, one launch (start us, length us, event | category | flops | bytes accessed | tf_op | source)
XLA Modules:
  0.0 133.2 jit_solution(16343521173745563994)
XLA Ops:
  7.2 0.0 all-gather.2.cloned.1.call-start
  7.2 0.7 all-gather.2.cloned.1.call-update
  7.9 0.0 reduce-scatter.2.cloned.1.call-start
  7.9 5.2 %project_part.1 = (f32[1280,128]{1,0:T(8,128)}, f32[1280,128]{1,0:T(8,128)}) custom-call(bf16[128,2560]{1,0:T(8,128)(2,1)} %acts.5, bf16[128,1024]{1,0:T(8,128)(2,1)} %hidden.5, bf16[2560,1024]{1,0:T(8,128)(2,1)} %bitcast.13, f32[1024,128]{1,0:T(8,128)} %query.1), custom_call_target="tpu_custom_call" | custom-call | flops 1342177280 | bytes 5242880 | tf_op jit(solution)/shard_map/project_part/pallas_call | solution.py:96
  13.2 0.0 copy-start
  13.2 0.0 copy-start.1
  13.2 0.1 collective-permute-start
  13.3 2.3 %collective-permute-done = f32[1280,128]{1,0:T(8,128)S(1)} collective-permute-done((f32[1280,128]{1,0:T(8,128)}, f32[1280,128]{1,0:T(8,128)S(1)}, u32[]{:S(2)}, u32[]{:S(2)}) %collective-permute-start) | collective-permute-done | bytes 655392 | tf_op jit(solution)/shard_map/ppermute | solution.py:274
  15.6 1.2 add.8
  16.7 21.6 %all_to_all.25 = f32[16,80,128]{2,1,0:T(8,128)S(1)} all-to-all(f32[16,80,128]{2,1,0:T(8,128)S(1)} %bitcast.16), channel_id=1, replica_groups={{0,16,32,48,64,80,96,112,128,144,160,176,192,208,224,240},{8,24,40,56,7..., dimensions={0} | all-to-all | bytes 1310720 | tf_op jit(solution)/shard_map/all_to_all | solution.py:278
  38.4 19.5 %all_to_all.26 = f32[8,80,128]{2,1,0:T(8,128)S(1)} all-to-all(f32[8,80,128]{2,1,0:T(8,128)S(1)} %broadcast_in_dim.8), channel_id=1, replica_groups=mesh['dp'=32,'mp'=8] {'mp'}, dimensions={0} | all-to-all | bytes 655360 | tf_op jit(solution)/shard_map/all_to_all | solution.py:293
  58.0 17.6 %all_to_all.27 = f32[16,80,128]{2,1,0:T(8,128)S(1)} all-to-all(f32[16,80,128]{2,1,0:T(8,128)S(1)} %broadcast_in_dim.9), channel_id=1, replica_groups={{0,16,32,48,64,80,96,112,128,144,160,176,192,208,224,240},{8,24,40,56,7..., dimensions={0} | all-to-all | bytes 1310720 | tf_op jit(solution)/shard_map/all_to_all | solution.py:287
  75.6 0.0 collective-permute-start.1
  75.6 2.1 %collective-permute-done.1.other = f32[1280,128]{1,0:T(8,128)S(1)} collective-permute-done((f32[1280,128]{1,0:T(8,128)S(1)}, f32[1280,128]{1,0:T(8,128)S(1)}, u32[]{:S(2)}, u32[]{:S(2)}) %collective-permute-start.1) | collective-permute-done | bytes 655392 | tf_op jit(solution)/shard_map/ppermute | solution.py:274
  77.7 0.0 copy-done
  77.7 0.0 copy-done.1
  77.7 4.6 %query_part.1 = (f32[512,128]{1,0:T(8,128)S(1)}, f32[512,128]{1,0:T(8,128)S(1)}, f32[128,128]{1,0:T(8,128)S(1)}) custom-call(bf16[128,2560]{1,0:T(8,128)(2,1)S(1)} %copy-done.1, bf16[128,1024]{1,0:T(8,128)(2,1)S(1)} %copy-done, bf16[2560,1024]{1,0:T(8,128)(2,1)} %bitcast.14, f32[1280,128]{1,0:T(8,128)S(1)} %bitcast.9, ...), custom_call_target="tpu_custom_call" | custom-call | flops 1342177280 | bytes 5242880 | tf_op jit(solution)/shard_map/query_part/pallas_call | solution.py:153
  82.2 0.0 all-gather.2.cloned.1.call-done
  82.3 5.1 %fusion = f32[128,2560]{0,1:T(8,128)} fusion(bf16[128,1024]{1,0:T(8,128)(2,1)S(1)} %copy-done, bf16[2560,1024]{1,0:T(8,128)(2,1)} %all-gather.2.cloned.1.call-done), kind=kOutput, calls=%fused_computation | convolution fusion | flops 671088640 | bytes 6815744 | tf_op jit(solution)/shard_map/dot_general | solution.py:19
  87.4 0.0 reduce-scatter.2.cloned.1.call-update
  87.4 0.2 collective-permute-start.2
  87.6 1.4 %collective-permute-done.2 = f32[512,128]{1,0:T(8,128)S(1)} collective-permute-done((f32[512,128]{1,0:T(8,128)S(1)}, f32[512,128]{1,0:T(8,128)S(1)}, u32[]{:S(2)}, u32[]{:S(2)}) %collective-permute-start.2) | collective-permute-done | bytes 262176 | tf_op jit(solution)/shard_map/ppermute | solution.py:274
  89.1 13.0 %all_to_all.28 = f32[16,32,128]{2,1,0:T(8,128)S(1)} all-to-all(f32[16,32,128]{2,1,0:T(8,128)S(1)} %bitcast.17), channel_id=1, replica_groups={{0,16,32,48,64,80,96,112,128,144,160,176,192,208,224,240},{8,24,40,56,7..., dimensions={0} | all-to-all | bytes 524288 | tf_op jit(solution)/shard_map/all_to_all | solution.py:278
  102.1 0.7 broadcast_in_dim.10
  102.8 3.5 %all-to-all-start.4 = ((f32[16,32,128]{2,1,0:T(8,128)}), f32[16,32,128]{2,1,0:T(8,128)S(1)}, u32[]{:S(2)}, u32[]{:S(2)}) async-start(f32[16,32,128]{2,1,0:T(8,128)} %broadcast_in_dim.10), calls=%async_computation.5 | async-start | bytes 524288 | tf_op jit(solution)/shard_map/all_to_all | solution.py:287
  106.4 4.2 %inverse_factor.1.inverse = f32[128,128]{1,0:T(8,128)S(1)} custom-call(f32[128,128]{1,0:T(8,128)S(1)} %get-tuple-element.19.gram), custom_call_target="tpu_custom_call" | custom-call | flops 2000000000 | bytes 10000000 | tf_op jit(solution)/shard_map/inverse_factor/pallas_call | solution.py:336
  110.6 4.4 %all-to-all-done.4 = f32[16,32,128]{2,1,0:T(8,128)S(1)} async-done(((f32[16,32,128]{2,1,0:T(8,128)}), f32[16,32,128]{2,1,0:T(8,128)S(1)}, u32[]{:S(2)}, u32[]{:S(2)}) %all-to-all-start.4) | async-done | bytes 262176 | tf_op jit(solution)/shard_map/all_to_all | solution.py:287
  115.0 0.0 collective-permute-start.3
  115.0 1.5 %collective-permute-done.3.query_other = f32[512,128]{1,0:T(8,128)S(1)} collective-permute-done((f32[512,128]{1,0:T(8,128)S(1)}, f32[512,128]{1,0:T(8,128)S(1)}, u32[]{:S(2)}, u32[]{:S(2)}) %collective-permute-start.3) | collective-permute-done | bytes 262176 | tf_op jit(solution)/shard_map/ppermute | solution.py:274
  116.6 8.2 %residual.1 = (bf16[2560,1024]{1,0:T(8,128)(2,1)}, f32[80,1024]{1,0:T(8,128)}, f32[1024,128]{1,0:T(8,128)}) custom-call(bf16[128,2560]{1,0:T(8,128)(2,1)S(1)} %copy-done.1, bf16[128,1024]{1,0:T(8,128)(2,1)S(1)} %copy-done, bf16[2560,1024]{1,0:T(8,128)(2,1)} %bitcast.15, f32[1280,128]{1,0:T(8,128)S(1)} %bitcast.10, ...), custom_call_target="tpu_custom_call" | custom-call | flops 2684354560 | bytes 10485760 | tf_op jit(solution)/shard_map/residual/pallas_call | solution.py:239
  124.8 0.0 reduce-scatter.2.cloned.1.call-done
  124.8 1.6 %convert_element_type.3 = bf16[128,320]{0,1:T(8,128)(2,1)} convert(f32[128,320]{0,1:T(8,128)} %reduce-scatter.2.cloned.1.call-done) | non-fusion elementwise | flops 40960 | bytes 245760 | tf_op jit(solution)/shard_map/convert_element_type | solution.py:373
  (6 shorter events, 0.2 us)
Async XLA Ops:
  7.2 75.1 %all-gather.2.cloned.1.call-start = ((), (), s32[]{:S(2)}) async-start(), calls=%async_computation.6 | async-start | bytes 5406720 | tf_op jit(solution)/shard_map/all_gather | solution.py:361
  7.9 116.9 %reduce-scatter.2.cloned.1.call-start = ((), (), s32[]{:S(2)}) async-start(), calls=%async_computation.7 | async-start | bytes 1474560 | tf_op jit(solution)/shard_map/reduce_scatter | solution.py:364
  13.2 64.5 %copy-start = (bf16[128,1024]{1,0:T(8,128)(2,1)S(1)}, bf16[128,1024]{1,0:T(8,128)(2,1)}, u32[]{:S(2)}) copy-start(bf16[128,1024]{1,0:T(8,128)(2,1)} %hidden.5) | copy-start | bytes 786436
  13.2 64.5 %copy-start.1 = (bf16[128,2560]{1,0:T(8,128)(2,1)S(1)}, bf16[128,2560]{1,0:T(8,128)(2,1)}, u32[]{:S(2)}) copy-start(bf16[128,2560]{1,0:T(8,128)(2,1)} %acts.5) | copy-start | bytes 1966084
  13.2 2.4 %collective-permute-start = (f32[1280,128]{1,0:T(8,128)}, f32[1280,128]{1,0:T(8,128)S(1)}, u32[]{:S(2)}, u32[]{:S(2)}) collective-permute-start(f32[1280,128]{1,0:T(8,128)} %get-tuple-element.18), channel_id=1, source_target_pairs={{0,8},{8,0},{16,24},{24,16},{32,40},{40,32},{48,56},{56,48},{64,72... | collective-permute-start | bytes 1966088 | tf_op jit(solution)/shard_map/ppermute | solution.py:274
  75.6 2.1 %collective-permute-start.1 = (f32[1280,128]{1,0:T(8,128)S(1)}, f32[1280,128]{1,0:T(8,128)S(1)}, u32[]{:S(2)}, u32[]{:S(2)}) collective-permute-start(f32[1280,128]{1,0:T(8,128)S(1)} %bitcast.8), channel_id=1, source_target_pairs={{0,8},{8,0},{16,24},{24,16},{32,40},{40,32},{48,56},{56,48},{64,72... | collective-permute-start | bytes 1966088 | tf_op jit(solution)/shard_map/ppermute | solution.py:274
  87.4 1.6 %collective-permute-start.2 = (f32[512,128]{1,0:T(8,128)S(1)}, f32[512,128]{1,0:T(8,128)S(1)}, u32[]{:S(2)}, u32[]{:S(2)}) collective-permute-start(f32[512,128]{1,0:T(8,128)S(1)} %get-tuple-element.22), channel_id=1, source_target_pairs={{0,8},{8,0},{16,24},{24,16},{32,40},{40,32},{48,56},{56,48},{64,72... | collective-permute-start | bytes 786440 | tf_op jit(solution)/shard_map/ppermute | solution.py:274
  102.8 12.2 %all-to-all-start.4 = ((f32[16,32,128]{2,1,0:T(8,128)}), f32[16,32,128]{2,1,0:T(8,128)S(1)}, u32[]{:S(2)}, u32[]{:S(2)}) async-start(f32[16,32,128]{2,1,0:T(8,128)} %broadcast_in_dim.10), calls=%async_computation.5 | async-start | bytes 524288 | tf_op jit(solution)/shard_map/all_to_all | solution.py:287
  115.0 1.5 %collective-permute-start.3 = (f32[512,128]{1,0:T(8,128)S(1)}, f32[512,128]{1,0:T(8,128)S(1)}, u32[]{:S(2)}, u32[]{:S(2)}) collective-permute-start(f32[512,128]{1,0:T(8,128)S(1)} %bitcast.11), channel_id=1, source_target_pairs={{0,8},{8,0},{16,24},{24,16},{32,40},{40,32},{48,56},{56,48},{64,72... | collective-permute-start | bytes 786440 | tf_op jit(solution)/shard_map/ppermute | solution.py:274
Sparse Core Ops, SparseCore 0:
  10.5 65.7 all-gather.1
  87.5 36.3 reduce-scatter.1

commit v7 on v6

--- a/solution.py
+++ b/solution.py
@@ -345,6 +345,30 @@
         name="inverse_factor",
     )(gram_matrix)
 
+def product_kernel(weight, hidden, out):
+    out[...] = dot(weight[...], hidden[...], ((1,), (1,)))
+
+
+def product(weight, hidden):
+    rows, columns = weight.shape
+    tokens = hidden.shape[0]
+    return pl.pallas_call(
+        product_kernel,
+        grid=(rows // BLOCK,),
+        in_specs=[
+            pl.BlockSpec((BLOCK, columns), lambda i: (i, 0)),
+            pl.BlockSpec((tokens, columns), lambda i: (0, 0)),
+        ],
+        out_specs=pl.BlockSpec((BLOCK, tokens), lambda i: (i, 0)),
+        out_shape=jax.ShapeDtypeStruct((rows, tokens), F32),
+        compiler_params=pltpu.CompilerParams(vmem_limit_bytes=VMEM_LIMIT),
+        cost_estimate=pl.CostEstimate(
+            flops=2 * rows * columns * tokens, bytes_accessed=2 * rows * columns, transcendentals=0
+        ),
+        name="product",
+    )(weight, hidden)
+
+
 def after(x, earlier):
     return lax.optimization_barrier((x, earlier))[0]
 
@@ -359,9 +383,9 @@
     mine, theirs, gram_matrix = query_part(activations, grad_hidden, error, own, other)
     inverse = inverse_factor(gram_matrix)
     weight = lax.all_gather(up_weight, "dp", axis=0, tiled=True)
-    partial_input = dot(after(grad_hidden, gram_matrix), weight, ((1,), (1,)))
+    partial_input = product(weight, after(grad_hidden, gram_matrix))
     mine = after(mine + swapped(theirs, replicas), partial_input[0, 0])
-    grad_input = lax.psum_scatter(partial_input, "mp", scatter_dimension=1, tiled=True)
+    grad_input = lax.psum_scatter(partial_input, "mp", scatter_dimension=0, tiled=True)
     query_own = gather_rows(scatter_sum(mine, replicas), replicas)
     query_own, inverse = lax.optimization_barrier((query_own, inverse))
     query_other = swapped(query_own, replicas)
@@ -370,7 +394,7 @@
         error.shape[0] // replicas,
     )
     grad_input, error_next = lax.optimization_barrier((grad_input, error_next))
-    return (grad_input.astype(BF16), error_next[None], update, query_next)
+    return (grad_input.astype(BF16).T, error_next[None], update, query_next)
 
 def solution(mesh):
     in_specs = (P("dp", None), P("dp", "mp"), P("dp", "mp"), P("dp", None, "mp"), P("mp", None))

time: 135 us -> 135 us (level)
  Pallas kernels: 22.2 us -> 27.4 us
  matrix products: 5.11 us -> 0 us
    pallas_call x0 -> x1, Pallas kernels: none -> 5.24 us  [product(): pl.pallas_call(product_kernel, grid=(rows // BLOCK,), in_specs=[pl.BlockS...]
    dot_general x1 -> x0, matrix products: 5.11 us -> none  [dot(): return lax.dot_general(a, b, (dims, ((), ())), preferred_element_type=F32)]
    convert_element_type x1 -> x0, other arithmetic: 1.56 us -> none  [local(): return (grad_input.astype(BF16), error_next[None], update, query_next)]
    transpose x0 -> x1, other arithmetic: none -> 1.56 us  [local(): return (grad_input.astype(BF16).T, error_next[None], update, query_next)]
where the time goes in v7:
time: 135 us; the launch traced here: 133 us
  blocking collectives  71.7 us (53%)
  Pallas kernels  27.4 us (20%)
  between operations  14.2 us (11%)
  waiting for transfers between devices  12.5 us (9%)
  starting transfers between devices  3.93 us (3%)
  other arithmetic  2.84 us (2%)
    all_to_all x2, blocking collectives, scatter_sum(): lax.all_to_all(x.reshape(chips, x.shape[0] // chips, -1), 'dp', 0, 0, axi...  34.6 us
    all_to_all x1, blocking collectives, sum_over_mp(): return jnp.sum(lax.all_to_all(spread, 'mp', 0, 0), axis=0)  19.5 us
    all_to_all x1, blocking collectives, gather_rows(): lax.all_to_all(spread, 'dp', 0, 0, axis_index_groups=chips_of(replicas))  17.6 us
    pallas_call x1, Pallas kernels, residual(): pl.pallas_call(residual_kernel, grid=(1,), in_specs=[HBM, HBM, HBM, whole...  8.19 us
    ppermute x4, waiting for transfers between devices, swapped(): return lax.ppermute(x, 'dp', [(i, i ^ 1) for i in range(replicas)])  7.32 us
    pallas_call x1, Pallas kernels, product(): pl.pallas_call(product_kernel, grid=(rows // BLOCK,), in_specs=[pl.BlockS...  5.24 us
    pallas_call x1, Pallas kernels, project_part(): pl.pallas_call(project_kernel, grid=(1,), in_specs=[HBM, HBM, HBM, HBM],...  5.21 us
    pallas_call x1, Pallas kernels, query_part(): pl.pallas_call(query_kernel, grid=(1,), in_specs=[HBM, HBM, HBM, whole(ow...  4.56 us
  transfers between devices with their start and end apart: 7, of which 5 were waited for; matrix products, arithmetic and copies ran while one was open for 2% of the time, Pallas kernels for 17%

profile of v7, /device:TPU:32, one launch (start us, length us, event | category | flops | bytes accessed | tf_op | source)
XLA Modules:
  0.0 133.3 jit_solution(12876767814982416036)
XLA Ops:
  7.2 0.0 all-gather.2.cloned.1.call-start
  7.2 0.7 all-gather.2.cloned.1.call-update
  7.9 0.0 reduce-scatter.2.cloned.1.call-start
  7.9 5.2 %project_part.1 = (f32[1280,128]{1,0:T(8,128)}, f32[1280,128]{1,0:T(8,128)}) custom-call(bf16[128,2560]{1,0:T(8,128)(2,1)} %acts.5, bf16[128,1024]{1,0:T(8,128)(2,1)} %hidden.6, bf16[2560,1024]{1,0:T(8,128)(2,1)} %bitcast.13, f32[1024,128]{1,0:T(8,128)} %query.1), custom_call_target="tpu_custom_call" | custom-call | flops 1342177280 | bytes 5242880 | tf_op jit(solution)/shard_map/project_part/pallas_call | solution.py:96
  13.2 0.0 copy-start
  13.2 0.0 copy-start.1
  13.2 0.1 collective-permute-start
  13.3 2.3 %collective-permute-done = f32[1280,128]{1,0:T(8,128)S(1)} collective-permute-done((f32[1280,128]{1,0:T(8,128)}, f32[1280,128]{1,0:T(8,128)S(1)}, u32[]{:S(2)}, u32[]{:S(2)}) %collective-permute-start) | collective-permute-done | bytes 655392 | tf_op jit(solution)/shard_map/ppermute | solution.py:274
  15.6 1.2 add.8
  16.7 21.6 %all_to_all.25 = f32[16,80,128]{2,1,0:T(8,128)S(1)} all-to-all(f32[16,80,128]{2,1,0:T(8,128)S(1)} %bitcast.16), channel_id=1, replica_groups={{0,16,32,48,64,80,96,112,128,144,160,176,192,208,224,240},{8,24,40,56,7..., dimensions={0} | all-to-all | bytes 1310720 | tf_op jit(solution)/shard_map/all_to_all | solution.py:278
  38.4 19.5 %all_to_all.26 = f32[8,80,128]{2,1,0:T(8,128)S(1)} all-to-all(f32[8,80,128]{2,1,0:T(8,128)S(1)} %broadcast_in_dim.8), channel_id=1, replica_groups=mesh['dp'=32,'mp'=8] {'mp'}, dimensions={0} | all-to-all | bytes 655360 | tf_op jit(solution)/shard_map/all_to_all | solution.py:293
  58.0 17.6 %all_to_all.27 = f32[16,80,128]{2,1,0:T(8,128)S(1)} all-to-all(f32[16,80,128]{2,1,0:T(8,128)S(1)} %broadcast_in_dim.9), channel_id=1, replica_groups={{0,16,32,48,64,80,96,112,128,144,160,176,192,208,224,240},{8,24,40,56,7..., dimensions={0} | all-to-all | bytes 1310720 | tf_op jit(solution)/shard_map/all_to_all | solution.py:287
  75.6 0.0 collective-permute-start.1
  75.6 2.1 %collective-permute-done.1.other = f32[1280,128]{1,0:T(8,128)S(1)} collective-permute-done((f32[1280,128]{1,0:T(8,128)S(1)}, f32[1280,128]{1,0:T(8,128)S(1)}, u32[]{:S(2)}, u32[]{:S(2)}) %collective-permute-start.1) | collective-permute-done | bytes 655392 | tf_op jit(solution)/shard_map/ppermute | solution.py:274
  77.7 0.0 copy-done
  77.7 0.0 copy-done.1
  77.7 4.6 %query_part.1 = (f32[512,128]{1,0:T(8,128)S(1)}, f32[512,128]{1,0:T(8,128)S(1)}, f32[128,128]{1,0:T(8,128)S(1)}) custom-call(bf16[128,2560]{1,0:T(8,128)(2,1)S(1)} %copy-done, bf16[128,1024]{1,0:T(8,128)(2,1)S(1)} %copy-done.1, bf16[2560,1024]{1,0:T(8,128)(2,1)} %bitcast.14, f32[1280,128]{1,0:T(8,128)S(1)} %bitcast.9, ...), custom_call_target="tpu_custom_call" | custom-call | flops 1342177280 | bytes 5242880 | tf_op jit(solution)/shard_map/query_part/pallas_call | solution.py:153
  82.2 0.0 all-gather.2.cloned.1.call-done.weight
  82.3 5.2 %product.1 = f32[2560,128]{1,0:T(8,128)} custom-call(bf16[2560,1024]{1,0:T(8,128)(2,1)} %all-gather.2.cloned.1.call-done.weight, bf16[128,1024]{1,0:T(8,128)(2,1)S(1)} %copy-done.1), custom_call_target="tpu_custom_call" | custom-call | flops 671088640 | bytes 5242880 | tf_op jit(solution)/shard_map/product/pallas_call | solution.py:355
  87.5 0.0 reduce-scatter.2.cloned.1.call-update
  87.5 0.2 collective-permute-start.2
  87.7 1.4 %collective-permute-done.2 = f32[512,128]{1,0:T(8,128)S(1)} collective-permute-done((f32[512,128]{1,0:T(8,128)S(1)}, f32[512,128]{1,0:T(8,128)S(1)}, u32[]{:S(2)}, u32[]{:S(2)}) %collective-permute-start.2) | collective-permute-done | bytes 262176 | tf_op jit(solution)/shard_map/ppermute | solution.py:274
  89.2 13.0 %all_to_all.28 = f32[16,32,128]{2,1,0:T(8,128)S(1)} all-to-all(f32[16,32,128]{2,1,0:T(8,128)S(1)} %bitcast.17), channel_id=1, replica_groups={{0,16,32,48,64,80,96,112,128,144,160,176,192,208,224,240},{8,24,40,56,7..., dimensions={0} | all-to-all | bytes 524288 | tf_op jit(solution)/shard_map/all_to_all | solution.py:278
  102.2 0.7 broadcast_in_dim.10
  103.0 3.5 %all-to-all-start.4 = ((f32[16,32,128]{2,1,0:T(8,128)}), f32[16,32,128]{2,1,0:T(8,128)S(1)}, u32[]{:S(2)}, u32[]{:S(2)}) async-start(f32[16,32,128]{2,1,0:T(8,128)} %broadcast_in_dim.10), calls=%async_computation.5 | async-start | bytes 524288 | tf_op jit(solution)/shard_map/all_to_all | solution.py:287
  106.5 4.2 %inverse_factor.1.inverse = f32[128,128]{1,0:T(8,128)S(1)} custom-call(f32[128,128]{1,0:T(8,128)S(1)} %get-tuple-element.19.gram), custom_call_target="tpu_custom_call" | custom-call | flops 2000000000 | bytes 10000000 | tf_op jit(solution)/shard_map/inverse_factor/pallas_call | solution.py:336
  110.7 4.4 %all-to-all-done.4 = f32[16,32,128]{2,1,0:T(8,128)S(1)} async-done(((f32[16,32,128]{2,1,0:T(8,128)}), f32[16,32,128]{2,1,0:T(8,128)S(1)}, u32[]{:S(2)}, u32[]{:S(2)}) %all-to-all-start.4) | async-done | bytes 262176 | tf_op jit(solution)/shard_map/all_to_all | solution.py:287
  115.2 0.0 collective-permute-start.3
  115.2 1.5 %collective-permute-done.3.query_other = f32[512,128]{1,0:T(8,128)S(1)} collective-permute-done((f32[512,128]{1,0:T(8,128)S(1)}, f32[512,128]{1,0:T(8,128)S(1)}, u32[]{:S(2)}, u32[]{:S(2)}) %collective-permute-start.3) | collective-permute-done | bytes 262176 | tf_op jit(solution)/shard_map/ppermute | solution.py:274
  116.7 8.2 %residual.1 = (bf16[2560,1024]{1,0:T(8,128)(2,1)}, f32[80,1024]{1,0:T(8,128)}, f32[1024,128]{1,0:T(8,128)}) custom-call(bf16[128,2560]{1,0:T(8,128)(2,1)S(1)} %copy-done, bf16[128,1024]{1,0:T(8,128)(2,1)S(1)} %copy-done.1, bf16[2560,1024]{1,0:T(8,128)(2,1)} %bitcast.15, f32[1280,128]{1,0:T(8,128)S(1)} %bitcast.10, ...), custom_call_target="tpu_custom_call" | custom-call | flops 2684354560 | bytes 10485760 | tf_op jit(solution)/shard_map/residual/pallas_call | solution.py:239
  124.9 0.0 reduce-scatter.2.cloned.1.call-done
  124.9 1.6 %convert_bitcast_fusion = bf16[128,320]{0,1:T(8,128)(2,1)} fusion(f32[320,128]{1,0:T(8,128)} %reduce-scatter.2.cloned.1.call-done), kind=kLoop, calls=%fused_computation | loop fusion | flops 40960 | bytes 245760 | tf_op jit(solution)/shard_map/transpose | solution.py:397
  (6 shorter events, 0.2 us)
Async XLA Ops:
  7.2 75.1 %all-gather.2.cloned.1.call-start = ((), (), s32[]{:S(2)}) async-start(), calls=%async_computation.6 | async-start | bytes 5406720 | tf_op jit(solution)/shard_map/all_gather | solution.py:385
  7.9 117.0 %reduce-scatter.2.cloned.1.call-start = ((), (), s32[]{:S(2)}) async-start(), calls=%async_computation.7 | async-start | bytes 1474560 | tf_op jit(solution)/shard_map/reduce_scatter | solution.py:388
  13.2 64.5 %copy-start = (bf16[128,2560]{1,0:T(8,128)(2,1)S(1)}, bf16[128,2560]{1,0:T(8,128)(2,1)}, u32[]{:S(2)}) copy-start(bf16[128,2560]{1,0:T(8,128)(2,1)} %acts.5) | copy-start | bytes 1966084
  13.2 64.5 %copy-start.1 = (bf16[128,1024]{1,0:T(8,128)(2,1)S(1)}, bf16[128,1024]{1,0:T(8,128)(2,1)}, u32[]{:S(2)}) copy-start(bf16[128,1024]{1,0:T(8,128)(2,1)} %hidden.6) | copy-start | bytes 786436
  13.2 2.4 %collective-permute-start = (f32[1280,128]{1,0:T(8,128)}, f32[1280,128]{1,0:T(8,128)S(1)}, u32[]{:S(2)}, u32[]{:S(2)}) collective-permute-start(f32[1280,128]{1,0:T(8,128)} %get-tuple-element.18), channel_id=1, source_target_pairs={{0,8},{8,0},{16,24},{24,16},{32,40},{40,32},{48,56},{56,48},{64,72... | collective-permute-start | bytes 1966088 | tf_op jit(solution)/shard_map/ppermute | solution.py:274
  75.6 2.1 %collective-permute-start.1 = (f32[1280,128]{1,0:T(8,128)S(1)}, f32[1280,128]{1,0:T(8,128)S(1)}, u32[]{:S(2)}, u32[]{:S(2)}) collective-permute-start(f32[1280,128]{1,0:T(8,128)S(1)} %bitcast.8), channel_id=1, source_target_pairs={{0,8},{8,0},{16,24},{24,16},{32,40},{40,32},{48,56},{56,48},{64,72... | collective-permute-start | bytes 1966088 | tf_op jit(solution)/shard_map/ppermute | solution.py:274
  87.5 1.6 %collective-permute-start.2 = (f32[512,128]{1,0:T(8,128)S(1)}, f32[512,128]{1,0:T(8,128)S(1)}, u32[]{:S(2)}, u32[]{:S(2)}) collective-permute-start(f32[512,128]{1,0:T(8,128)S(1)} %get-tuple-element.22), channel_id=1, source_target_pairs={{0,8},{8,0},{16,24},{24,16},{32,40},{40,32},{48,56},{56,48},{64,72... | collective-permute-start | bytes 786440 | tf_op jit(solution)/shard_map/ppermute | solution.py:274
  103.0 12.2 %all-to-all-start.4 = ((f32[16,32,128]{2,1,0:T(8,128)}), f32[16,32,128]{2,1,0:T(8,128)S(1)}, u32[]{:S(2)}, u32[]{:S(2)}) async-start(f32[16,32,128]{2,1,0:T(8,128)} %broadcast_in_dim.10), calls=%async_computation.5 | async-start | bytes 524288 | tf_op jit(solution)/shard_map/all_to_all | solution.py:287
  115.2 1.5 %collective-permute-start.3 = (f32[512,128]{1,0:T(8,128)S(1)}, f32[512,128]{1,0:T(8,128)S(1)}, u32[]{:S(2)}, u32[]{:S(2)}) collective-permute-start(f32[512,128]{1,0:T(8,128)S(1)} %bitcast.11), channel_id=1, source_target_pairs={{0,8},{8,0},{16,24},{24,16},{32,40},{40,32},{48,56},{56,48},{64,72... | collective-permute-start | bytes 786440 | tf_op jit(solution)/shard_map/ppermute | solution.py:274
Sparse Core Ops, SparseCore 0:
  10.5 65.7 all-gather.1
  87.6 36.4 reduce-scatter.1

commit v8 on v6

--- a/solution.py
+++ b/solution.py
@@ -356,12 +356,12 @@
     mine = mine + swapped(theirs, replicas)
     own = gather_rows(sum_over_mp(scatter_sum(mine, replicas)), replicas)
     other = swapped(own, replicas)
+    weight = lax.all_gather(up_weight, "dp", axis=0, tiled=True)
+    partial_input = dot(grad_hidden, weight, ((1,), (1,)))
+    grad_input = lax.psum_scatter(partial_input, "mp", scatter_dimension=1, tiled=True)
     mine, theirs, gram_matrix = query_part(activations, grad_hidden, error, own, other)
     inverse = inverse_factor(gram_matrix)
-    weight = lax.all_gather(up_weight, "dp", axis=0, tiled=True)
-    partial_input = dot(after(grad_hidden, gram_matrix), weight, ((1,), (1,)))
-    mine = after(mine + swapped(theirs, replicas), partial_input[0, 0])
-    grad_input = lax.psum_scatter(partial_input, "mp", scatter_dimension=1, tiled=True)
+    mine = mine + swapped(theirs, replicas)
     query_own = gather_rows(scatter_sum(mine, replicas), replicas)
     query_own, inverse = lax.optimization_barrier((query_own, inverse))
     query_other = swapped(query_own, replicas)

time: 135 us -> 135 us (level)
  blocking collectives: 71.7 us -> 54.9 us
  waiting for transfers between devices: 12.5 us -> 25.3 us
  starting transfers between devices: 3.94 us -> 8.14 us
    all_to_all x1 -> x0, blocking collectives: 17.6 us -> none  [gather_rows(): lax.all_to_all(spread, 'dp', 0, 0, axis_index_groups=chips_of(replicas))]
    all_gather x1, waiting for transfers between devices: 0.02 us -> 13.2 us  [local(): weight = lax.all_gather(up_weight, 'dp', axis=0, tiled=True)]
    all_to_all x1 -> x2, starting transfers between devices: 3.53 us -> 7.3 us  [gather_rows(): lax.all_to_all(spread, 'dp', 0, 0, axis_index_groups=chips_of(replicas))]
    all_to_all x1 -> x2, waiting for transfers between devices: 4.42 us -> 4.41 us  [gather_rows(): lax.all_to_all(spread, 'dp', 0, 0, axis_index_groups=chips_of(replicas))]
  transfers between devices with their start and end apart: 7 -> 8, of which waited for: 5 -> 6; matrix products, arithmetic and copies ran while one was open for 2% -> 6% of each run, Pallas kernels for 17% -> 17%
where the time goes in v8:
time: 135 us; the launch traced here: 134 us
  blocking collectives  54.9 us (41%)
  waiting for transfers between devices  25.3 us (19%)
  Pallas kernels  22.2 us (16%)
  between operations  14.2 us (11%)
  starting transfers between devices  8.14 us (6%)
  matrix products  5.12 us (4%)
  other arithmetic  2.83 us (2%)
  local copies, waits for them, and re-layouts  1.64 us (1%)
    all_to_all x2, blocking collectives, scatter_sum(): lax.all_to_all(x.reshape(chips, x.shape[0] // chips, -1), 'dp', 0, 0, axi...  35.4 us
    all_to_all x1, blocking collectives, sum_over_mp(): return jnp.sum(lax.all_to_all(spread, 'mp', 0, 0), axis=0)  19.4 us
    all_gather x1, waiting for transfers between devices, local(): weight = lax.all_gather(up_weight, 'dp', axis=0, tiled=True)  13.2 us
    pallas_call x1, Pallas kernels, residual(): pl.pallas_call(residual_kernel, grid=(1,), in_specs=[HBM, HBM, HBM, whole...  8.18 us
    all_to_all x2, starting transfers between devices, gather_rows(): lax.all_to_all(spread, 'dp', 0, 0, axis_index_groups=chips_of(replicas))  7.3 us
    ppermute x4, waiting for transfers between devices, swapped(): return lax.ppermute(x, 'dp', [(i, i ^ 1) for i in range(replicas)])  6.97 us
    pallas_call x1, Pallas kernels, project_part(): pl.pallas_call(project_kernel, grid=(1,), in_specs=[HBM, HBM, HBM, HBM],...  5.21 us
    dot_general x1, matrix products, dot(): return lax.dot_general(a, b, (dims, ((), ())), preferred_element_type=F32)  5.12 us
  transfers between devices with their start and end apart: 8, of which 6 were waited for; matrix products, arithmetic and copies ran while one was open for 6% of the time, Pallas kernels for 17%

profile of v8, /device:TPU:32, one launch (start us, length us, event | category | flops | bytes accessed | tf_op | source)
XLA Modules:
  0.0 134.2 jit_solution(5051522707031162383)
XLA Ops:
  7.2 0.0 all-gather.2.cloned.1.call-start
  7.2 0.7 all-gather.2.cloned.1.call-update
  7.9 5.2 %project_part.1 = (f32[1280,128]{1,0:T(8,128)}, f32[1280,128]{1,0:T(8,128)}) custom-call(bf16[128,2560]{1,0:T(8,128)(2,1)} %acts.5, bf16[128,1024]{1,0:T(8,128)(2,1)} %hidden.5, bf16[2560,1024]{1,0:T(8,128)(2,1)} %bitcast.13, f32[1024,128]{1,0:T(8,128)} %query.1), custom_call_target="tpu_custom_call" | custom-call | flops 1342177280 | bytes 5242880 | tf_op jit(solution)/shard_map/project_part/pallas_call | solution.py:96
  13.1 0.0 copy-start
  13.1 0.1 collective-permute-start
  13.2 2.3 %collective-permute-done = f32[1280,128]{1,0:T(8,128)S(1)} collective-permute-done((f32[1280,128]{1,0:T(8,128)}, f32[1280,128]{1,0:T(8,128)S(1)}, u32[]{:S(2)}, u32[]{:S(2)}) %collective-permute-start) | collective-permute-done | bytes 655392 | tf_op jit(solution)/shard_map/ppermute | solution.py:274
  15.5 1.2 add.8
  16.7 21.6 %all_to_all.25 = f32[16,80,128]{2,1,0:T(8,128)S(1)} all-to-all(f32[16,80,128]{2,1,0:T(8,128)S(1)} %bitcast.16), channel_id=1, replica_groups={{0,16,32,48,64,80,96,112,128,144,160,176,192,208,224,240},{8,24,40,56,7..., dimensions={0} | all-to-all | bytes 1310720 | tf_op jit(solution)/shard_map/all_to_all | solution.py:278
  38.4 19.4 %all_to_all.26 = f32[8,80,128]{2,1,0:T(8,128)S(1)} all-to-all(f32[8,80,128]{2,1,0:T(8,128)S(1)} %broadcast_in_dim.8), channel_id=1, replica_groups=mesh['dp'=32,'mp'=8] {'mp'}, dimensions={0} | all-to-all | bytes 655360 | tf_op jit(solution)/shard_map/all_to_all | solution.py:293
  57.8 0.9 broadcast_in_dim.9
  58.7 3.8 %all-to-all-start.2 = ((f32[16,80,128]{2,1,0:T(8,128)}), f32[16,80,128]{2,1,0:T(8,128)S(1)}, u32[]{:S(2)}, u32[]{:S(2)}) async-start(f32[16,80,128]{2,1,0:T(8,128)} %broadcast_in_dim.9), calls=%async_computation.3 | async-start | bytes 1310720 | tf_op jit(solution)/shard_map/all_to_all | solution.py:287
  62.5 0.0 copy-start.1
  62.5 0.0 reduce-scatter.2.cloned.1.call-start
  62.5 13.2 %all-gather.2.cloned.1.call-done = bf16[2560,1024]{1,0:T(8,128)(2,1)} async-done(((bf16[80,1024]{1,0:T(8,128)(2,1)}), bf16[2560,1024]{1,0:T(8,128)(2,1)}) %all-gather.2.cloned.1.call-update) | async-done | bytes 5242896 | tf_op jit(solution)/shard_map/all_gather | solution.py:359
  75.7 5.1 %fusion = f32[128,2560]{0,1:T(8,128)} fusion(bf16[128,1024]{1,0:T(8,128)(2,1)S(1)} %copy-done, bf16[2560,1024]{1,0:T(8,128)(2,1)} %all-gather.2.cloned.1.call-done), kind=kOutput, calls=%fused_computation | convolution fusion | flops 671088640 | bytes 6815744 | tf_op jit(solution)/shard_map/dot_general | solution.py:19
  80.8 0.0 reduce-scatter.2.cloned.1.call-update
  80.9 0.0 all-to-all-done.2
  80.9 0.3 collective-permute-start.1
  81.2 1.8 %collective-permute-done.1.other = f32[1280,128]{1,0:T(8,128)S(1)} collective-permute-done((f32[1280,128]{1,0:T(8,128)S(1)}, f32[1280,128]{1,0:T(8,128)S(1)}, u32[]{:S(2)}, u32[]{:S(2)}) %collective-permute-start.1) | collective-permute-done | bytes 655392 | tf_op jit(solution)/shard_map/ppermute | solution.py:274
  83.1 4.6 %query_part.1 = (f32[512,128]{1,0:T(8,128)S(1)}, f32[512,128]{1,0:T(8,128)S(1)}, f32[128,128]{1,0:T(8,128)S(1)}) custom-call(bf16[128,2560]{1,0:T(8,128)(2,1)S(1)} %copy-done.1, bf16[128,1024]{1,0:T(8,128)(2,1)S(1)} %copy-done, bf16[2560,1024]{1,0:T(8,128)(2,1)} %bitcast.14, f32[1280,128]{1,0:T(8,128)S(1)} %bitcast.9, ...), custom_call_target="tpu_custom_call" | custom-call | flops 1342177280 | bytes 5242880 | tf_op jit(solution)/shard_map/query_part/pallas_call | solution.py:153
  87.6 0.3 collective-permute-start.2
  88.0 1.3 collective-permute-done.2
  89.3 13.8 %all_to_all.27 = f32[16,32,128]{2,1,0:T(8,128)S(1)} all-to-all(f32[16,32,128]{2,1,0:T(8,128)S(1)} %bitcast.17), channel_id=1, replica_groups={{0,16,32,48,64,80,96,112,128,144,160,176,192,208,224,240},{8,24,40,56,7..., dimensions={0} | all-to-all | bytes 524288 | tf_op jit(solution)/shard_map/all_to_all | solution.py:278
  103.1 0.7 broadcast_in_dim.10
  103.9 3.5 %all-to-all-start.4 = ((f32[16,32,128]{2,1,0:T(8,128)}), f32[16,32,128]{2,1,0:T(8,128)S(1)}, u32[]{:S(2)}, u32[]{:S(2)}) async-start(f32[16,32,128]{2,1,0:T(8,128)} %broadcast_in_dim.10), calls=%async_computation.5 | async-start | bytes 524288 | tf_op jit(solution)/shard_map/all_to_all | solution.py:287
  107.4 4.2 %inverse_factor.1.inverse = f32[128,128]{1,0:T(8,128)S(1)} custom-call(f32[128,128]{1,0:T(8,128)S(1)} %get-tuple-element.20.gram), custom_call_target="tpu_custom_call" | custom-call | flops 2000000000 | bytes 10000000 | tf_op jit(solution)/shard_map/inverse_factor/pallas_call | solution.py:336
  111.7 4.4 %all-to-all-done.4 = f32[16,32,128]{2,1,0:T(8,128)S(1)} async-done(((f32[16,32,128]{2,1,0:T(8,128)}), f32[16,32,128]{2,1,0:T(8,128)S(1)}, u32[]{:S(2)}, u32[]{:S(2)}) %all-to-all-start.4) | async-done | bytes 262176 | tf_op jit(solution)/shard_map/all_to_all | solution.py:287
  116.1 0.0 collective-permute-start.3
  116.1 1.5 %collective-permute-done.3.query_other = f32[512,128]{1,0:T(8,128)S(1)} collective-permute-done((f32[512,128]{1,0:T(8,128)S(1)}, f32[512,128]{1,0:T(8,128)S(1)}, u32[]{:S(2)}, u32[]{:S(2)}) %collective-permute-start.3) | collective-permute-done | bytes 262176 | tf_op jit(solution)/shard_map/ppermute | solution.py:274
  117.6 8.2 %residual.1 = (bf16[2560,1024]{1,0:T(8,128)(2,1)}, f32[80,1024]{1,0:T(8,128)}, f32[1024,128]{1,0:T(8,128)}) custom-call(bf16[128,2560]{1,0:T(8,128)(2,1)S(1)} %copy-done.1, bf16[128,1024]{1,0:T(8,128)(2,1)S(1)} %copy-done, bf16[2560,1024]{1,0:T(8,128)(2,1)} %bitcast.15, f32[1280,128]{1,0:T(8,128)S(1)} %bitcast.10, ...), custom_call_target="tpu_custom_call" | custom-call | flops 2684354560 | bytes 10485760 | tf_op jit(solution)/shard_map/residual/pallas_call | solution.py:239
  125.8 0.0 reduce-scatter.2.cloned.1.call-done
  125.8 1.6 %convert_element_type.3 = bf16[128,320]{0,1:T(8,128)(2,1)} convert(f32[128,320]{0,1:T(8,128)} %reduce-scatter.2.cloned.1.call-done) | non-fusion elementwise | flops 40960 | bytes 245760 | tf_op jit(solution)/shard_map/convert_element_type | solution.py:373
  (7 shorter events, 0.1 us)
Async XLA Ops:
  7.2 68.5 %all-gather.2.cloned.1.call-start = ((), (), s32[]{:S(2)}) async-start(), calls=%async_computation.6 | async-start | bytes 5406720 | tf_op jit(solution)/shard_map/all_gather | solution.py:359
  13.1 62.6 %copy-start = (bf16[128,1024]{1,0:T(8,128)(2,1)S(1)}, bf16[128,1024]{1,0:T(8,128)(2,1)}, u32[]{:S(2)}) copy-start(bf16[128,1024]{1,0:T(8,128)(2,1)} %hidden.5) | copy-start | bytes 786436
  13.1 2.4 %collective-permute-start = (f32[1280,128]{1,0:T(8,128)}, f32[1280,128]{1,0:T(8,128)S(1)}, u32[]{:S(2)}, u32[]{:S(2)}) collective-permute-start(f32[1280,128]{1,0:T(8,128)} %get-tuple-element.17), channel_id=1, source_target_pairs={{0,8},{8,0},{16,24},{24,16},{32,40},{40,32},{48,56},{56,48},{64,72... | collective-permute-start | bytes 1966088 | tf_op jit(solution)/shard_map/ppermute | solution.py:274
  58.7 22.2 %all-to-all-start.2 = ((f32[16,80,128]{2,1,0:T(8,128)}), f32[16,80,128]{2,1,0:T(8,128)S(1)}, u32[]{:S(2)}, u32[]{:S(2)}) async-start(f32[16,80,128]{2,1,0:T(8,128)} %broadcast_in_dim.9), calls=%async_computation.3 | async-start | bytes 1310720 | tf_op jit(solution)/shard_map/all_to_all | solution.py:287
  62.5 20.6 %copy-start.1 = (bf16[128,2560]{1,0:T(8,128)(2,1)S(1)}, bf16[128,2560]{1,0:T(8,128)(2,1)}, u32[]{:S(2)}) copy-start(bf16[128,2560]{1,0:T(8,128)(2,1)} %acts.5) | copy-start | bytes 1966084
  62.5 63.4 %reduce-scatter.2.cloned.1.call-start = ((), (), s32[]{:S(2)}) async-start(), calls=%async_computation.7 | async-start | bytes 1474560 | tf_op jit(solution)/shard_map/reduce_scatter | solution.py:361
  80.9 2.2 %collective-permute-start.1 = (f32[1280,128]{1,0:T(8,128)S(1)}, f32[1280,128]{1,0:T(8,128)S(1)}, u32[]{:S(2)}, u32[]{:S(2)}) collective-permute-start(f32[1280,128]{1,0:T(8,128)S(1)} %bitcast.8), channel_id=1, source_target_pairs={{0,8},{8,0},{16,24},{24,16},{32,40},{40,32},{48,56},{56,48},{64,72... | collective-permute-start | bytes 1966088 | tf_op jit(solution)/shard_map/ppermute | solution.py:274
  87.6 1.6 %collective-permute-start.2 = (f32[512,128]{1,0:T(8,128)S(1)}, f32[512,128]{1,0:T(8,128)S(1)}, u32[]{:S(2)}, u32[]{:S(2)}) collective-permute-start(f32[512,128]{1,0:T(8,128)S(1)} %get-tuple-element.19), channel_id=1, source_target_pairs={{0,8},{8,0},{16,24},{24,16},{32,40},{40,32},{48,56},{56,48},{64,72... | collective-permute-start | bytes 786440 | tf_op jit(solution)/shard_map/ppermute | solution.py:274
  103.9 12.2 %all-to-all-start.4 = ((f32[16,32,128]{2,1,0:T(8,128)}), f32[16,32,128]{2,1,0:T(8,128)S(1)}, u32[]{:S(2)}, u32[]{:S(2)}) async-start(f32[16,32,128]{2,1,0:T(8,128)} %broadcast_in_dim.10), calls=%async_computation.5 | async-start | bytes 524288 | tf_op jit(solution)/shard_map/all_to_all | solution.py:287
  116.1 1.5 %collective-permute-start.3 = (f32[512,128]{1,0:T(8,128)S(1)}, f32[512,128]{1,0:T(8,128)S(1)}, u32[]{:S(2)}, u32[]{:S(2)}) collective-permute-start(f32[512,128]{1,0:T(8,128)S(1)} %bitcast.11), channel_id=1, source_target_pairs={{0,8},{8,0},{16,24},{24,16},{32,40},{40,32},{48,56},{56,48},{64,72... | collective-permute-start | bytes 786440 | tf_op jit(solution)/shard_map/ppermute | solution.py:274
Sparse Core Ops, SparseCore 0:
  10.5 65.1 all-gather.1
  81.0 37.7 reduce-scatter.1
